TPU v7x, 256 devices: a whole 4x4x8 slice. The times are simulated.
256 devices in a mesh: obj: 32 (over x, z_hi, core), ep: 8 (over z_lo, y).
Axes of the slice: x: 4, y: 4, z: 8 (z_hi: 4, z_lo: 2; z = z_hi * 2 + z_lo), core: 2. Of those that a mesh axis runs over, the one named last changes fastest.
Arguments:
- light_curves: float32 [4096, 1024], P('obj', 'ep'), may hold values from -40 to 40
- valid: int32 [4096, 1024], P('obj', 'ep'), may hold values 0 or 1
- pixel: int32 [4096], P('obj'), may hold values from 0 to 127, never falling along the last dimension, each value on 1 to 64 neighbouring positions
- inv_sigma: float32 [4096], P('obj'), may hold values from 0.5 to 4
- modes_init: float32 [1024, 16], P('ep'), may hold values from -6 to 6
- epoch_jitter: float32 [1024], replicated, may hold values from 0 to 0.9
- freq_index: int32 [2048], replicated, may hold values from 4 to 2047
Outputs:
- residual: float32 [4096, 1024], P('obj', 'ep')
- power: float32 [4096, 2048], P(('obj', 'ep'))
Inputs may be any that keep to these rules, and one draw needn't show every extreme that they name: Pixels never decrease along the objects; each pixel holds 1 to 64 objects, and some pixel exactly 64.
All inputs are finite; a program needn't handle non-finite values. No bound on the sum of `valid` on one device may be relied on, other than what follows from the above.
Results may differ from a plain program's by a relative error of at most 0.0052.
Values may be sent and summed in bfloat16 or wider, within the bound.
No kernel may reach another device: no remote copies, remote signals or barrier semaphores. Data moves between devices by JAX's collectives and lax.ppermute only.
A program may use at most 64 MiB of HBM per device.

v0:
```python
import math

import jax
import jax.numpy as jnp
from jax import lax
from jax.sharding import PartitionSpec as P

ITERS = 2


HUBER = 1.345
DAMP = 2.0
RIDGE = 0.05
HIGHEST = lax.Precision.HIGHEST
CONTRACT_FIRST = (((0,), (0,)), ((), ()))
CONTRACT_LAST = (((1,), (1,)), ((), ()))


def copy_for_each(shard, axis):
    copies = jnp.broadcast_to(shard, (lax.axis_size(axis), *shard.shape))
    return lax.all_to_all(copies, axis, split_axis=0, concat_axis=0, tiled=True)


def of_everyone(shard, axis):
    return copy_for_each(shard, axis).sum(axis=0)


def with_halo(cells, sides, width):
    for axis, dim in sides:
        count = lax.axis_size(axis)
        ends = count - 1
        head = lax.slice_in_dim(cells, 0, width, axis=dim)
        tail = lax.slice_in_dim(cells, cells.shape[dim] - width, cells.shape[dim], axis=dim)
        cells = jnp.concatenate(
            [
                lax.ppermute(tail, axis, [(i, (i + 1) % count) for i in range(ends)]),
                cells,
                lax.ppermute(head, axis, [((i + 1) % count, i) for i in range(ends)]),
            ],
            axis=dim,
        )
    return cells


def together(arrays, axis):
    ends = [0]
    for a in arrays:
        ends.append(ends[-1] + a.size)
    subtotal = of_everyone(jnp.concatenate([a.ravel() for a in arrays]), axis)
    return tuple((subtotal[b:e].reshape(a.shape) for a, b, e in zip(arrays, ends, ends[1:])))


def cut_along(shard, dim, length):
    shape = shard.shape
    pieces = shard.reshape(*shape[:dim], length, shape[dim] // length, *shape[dim + 1 :])
    return jnp.moveaxis(pieces, dim, 0)


def sum_at_owner(shard, axis, dim):
    pieces = cut_along(shard, dim, lax.axis_size(axis))
    arrived = lax.all_to_all(pieces, axis, split_axis=0, concat_axis=0, tiled=True)
    return arrived.sum(axis=0)


def rows_for(lines, length):
    spare = -len(lines) % length
    return jnp.pad(lines, [(0, spare)] + [(0, 0)] * (lines.ndim - 1))


def laid_out(pieces, dim):
    shape = list(pieces.shape[1:])
    shape[dim] *= pieces.shape[0]
    return jnp.moveaxis(pieces, 0, dim).reshape(shape)


def collect(shard, axis, dim):
    return laid_out(copy_for_each(shard, axis), dim)


def nested_sum(shard, axes):
    own = sum_at_owner(rows_for(shard, lax.axis_size(axes)), axes, 0)
    whole = collect(own, axes, 0)
    return whole[: len(shard)].reshape(shard.shape)


def together_2(arrays, axis):
    vector, at, done = (jnp.concatenate([a.reshape(-1) for a in arrays]), 0, [])
    subtotal = nested_sum(vector, axis)
    for a in arrays:
        done.append(subtotal[at : at + a.size].reshape(a.shape))
        at += a.size
    return tuple(done)


def in_one_piece(arrays, axis, dim, along):
    widths = [a.shape[along] for a in arrays]
    both = jnp.concatenate(arrays, axis=along)
    whole = lax.all_gather(both, axis, axis=dim, tiled=True)
    return tuple(jnp.split(whole, [sum(widths[:k]) for k in range(1, len(widths))], axis=along))


def damped_solve(gram, target):
    order = target.shape[0]
    square = gram.reshape(order, order, gram.shape[1])
    level = jnp.arange(order)[:, None]
    lower = []
    for column_at in range(order):
        column = square[:, column_at, :] + DAMP * (level == column_at).astype(jnp.float32)
        if column_at > 0:
            earlier = jnp.stack(lower, axis=1)
            column = column - jnp.sum(earlier * earlier[column_at][None], axis=1)
        pivot = jnp.sqrt(column[column_at])
        column = jnp.where(level >= column_at, column / pivot[None, :], 0.0)
        lower.append(column)
    remain = target
    forward = []
    for column_at in range(order):
        value = remain[column_at] / lower[column_at][column_at]
        remain = remain - lower[column_at] * value[None, :]
        forward.append(value)
    solved = [None] * order
    for column_at in reversed(range(order)):
        value = forward[column_at]
        if column_at + 1 < order:
            later = jnp.stack(solved[column_at + 1 :])
            value = value - jnp.sum(lower[column_at][column_at + 1 :] * later, axis=0)
        solved[column_at] = value / lower[column_at][column_at]
    return jnp.stack(solved)


def spectrum_sums(weighted, weight, times, freqs):
    cycles = times[:, None] * freqs[None, :]
    angle = 2.0 * math.pi * (cycles - jnp.floor(cycles))
    basis = jnp.concatenate(
        [jnp.cos(angle), jnp.sin(angle), jnp.cos(2.0 * angle), jnp.sin(2.0 * angle)], axis=1
    ).astype(jnp.bfloat16)
    width = freqs.shape[0]
    by_weight = jnp.dot(weight, basis, preferred_element_type=jnp.float32)
    by_value = jnp.dot(weighted, basis[:, : 2 * width], preferred_element_type=jnp.float32)
    return (by_weight, by_value)


def powers(by_weight, by_value, total, level):
    width = by_value.shape[1] // 2
    cosine = by_weight[:, :width]
    sine = by_weight[:, width : 2 * width]
    cosine_two = by_weight[:, 2 * width : 3 * width]
    sine_two = by_weight[:, 3 * width :]
    mean_level = level / total
    ycos = by_value[:, :width] - mean_level * cosine
    ysin = by_value[:, width:] - mean_level * sine
    cc_term = 0.5 * (total + cosine_two) - cosine * cosine / total + RIDGE * total
    ss_term = 0.5 * (total - cosine_two) - sine * sine / total + RIDGE * total
    cs_term = 0.5 * sine_two - cosine * sine / total
    determinant = cc_term * ss_term - cs_term * cs_term
    return (
        ss_term * ycos * ycos + cc_term * ysin * ysin - 2.0 * cs_term * ycos * ysin
    ) / determinant


def robust_on(resid, mask_now, sigma_now, member_now, counts_now, combine):
    scaled = resid * sigma_now[:, None]
    squares = jnp.sum(mask_now * scaled * scaled, axis=1)
    partial_value = jnp.stack([jnp.dot(member_now, squares, precision=HIGHEST), counts_now])
    totals = combine(partial_value)
    spread = jnp.sqrt(totals[0] / jnp.maximum(totals[1], 1.0) + 1e-06)
    object_spread = jnp.dot(spread, member_now, precision=HIGHEST)
    zscore = scaled / object_spread[:, None]
    huber = HUBER / jnp.maximum(jnp.abs(zscore), HUBER)
    return mask_now * huber * (sigma_now * sigma_now)[:, None]


def per_device(light_curves, valid, pixel, inv_sigma, modes_init, epoch_jitter, freq_index):
    obj_count = lax.axis_size("obj")
    ep_count = lax.axis_size("ep")
    order = modes_init.shape[1]
    obj_rows, ep_cols = light_curves.shape
    npix = 4 * obj_count
    mask_f = valid.astype(jnp.float32)
    epochs_all = epoch_jitter.shape[0]
    freqs = (freq_index + 1).astype(jnp.float32) / (4.0 * epochs_all)
    pixel_ids = jnp.arange(npix, dtype=jnp.int32)[:, None]

    def pixel_combine(partial_value):
        across = of_everyone(partial_value, "ep")
        border = with_halo(across[None], (("obj", 0),), 1)
        return jnp.sum(border, axis=0)

    member = (pixel[None, :] == pixel_ids).astype(jnp.float32)
    count_part = jnp.dot(member, jnp.sum(mask_f, axis=1), precision=HIGHEST)

    def robust(resid):
        return robust_on(resid, mask_f, inv_sigma, member, count_part, pixel_combine)

    def residual_of(coef_t, modes_t):
        return light_curves - lax.dot_general(coef_t, modes_t, CONTRACT_FIRST, precision=HIGHEST)

    modes_t = modes_init.T
    coef_t = jnp.zeros((order, obj_rows), jnp.float32)
    for iteration in range(ITERS):
        object_weight = robust(residual_of(coef_t, modes_t))
        object_outer = (modes_t[:, None, :] * modes_t[None, :, :]).reshape(order * order, ep_cols)
        object_gram = lax.dot_general(object_outer, object_weight, CONTRACT_LAST, precision=HIGHEST)
        object_target = lax.dot_general(
            modes_t, object_weight * light_curves, CONTRACT_LAST, precision=HIGHEST
        )
        object_gram, object_target = together((object_gram, object_target), "ep")
        coef_t = damped_solve(object_gram, object_target)
        weight = robust(residual_of(coef_t, modes_t))
        outer = (coef_t[:, None, :] * coef_t[None, :, :]).reshape(order * order, obj_rows)
        gram = jnp.dot(outer, weight, precision=HIGHEST)
        target = jnp.dot(coef_t, weight * light_curves, precision=HIGHEST)
        gram, target = together_2((gram, target), "obj")
        modes_t = damped_solve(gram, target)
    residual = residual_of(coef_t, modes_t)
    final_weight = robust(residual)
    weighted = (final_weight * residual).astype(jnp.bfloat16)
    weight_b = final_weight.astype(jnp.bfloat16)
    local_count = freqs.shape[0] // ep_count
    my_freqs = lax.dynamic_slice_in_dim(freqs, lax.axis_index("ep") * local_count, local_count)
    values, weights = in_one_piece((weighted, weight_b), "ep", 1, 0)
    span = values.shape[1]
    times = jnp.arange(span, dtype=jnp.int32).astype(jnp.float32) + epoch_jitter
    by_weight, by_value = spectrum_sums(values, weights, times, my_freqs)
    weight_adds = [by_weight]
    value_adds = [by_value]
    weight_sums = jnp.stack(weight_adds)
    value_sums = jnp.stack(value_adds)
    total = jnp.sum(weights, axis=1, keepdims=True, dtype=jnp.float32)
    level = jnp.sum(values, axis=1, keepdims=True, dtype=jnp.float32)
    local_power = powers(weight_sums[0], value_sums[0], total, level)
    power = lax.all_to_all(
        local_power.astype(jnp.bfloat16), "ep", split_axis=0, concat_axis=1, tiled=True
    ).astype(local_power.dtype)
    return (residual, power)


def solution(mesh):
    in_specs = (P("obj", "ep"), P("obj", "ep"), P("obj"), P("obj"), P("ep", None), P(), P())
    out_specs = (P("obj", "ep"), P(("obj", "ep"), None))
    return jax.shard_map(
        per_device, mesh=mesh, in_specs=in_specs, out_specs=out_specs, check_vma=False
    )
```

profile of v0, /device:TPU:1, one launch (start us, length us, event | category | flops | bytes accessed | tf_op | source)
XLA Modules:
  0.0 285.4 jit_solution(2781019328319105566)
XLA Ops:
  0.6 0.9 copy.253
  6.3 6.4 %all-to-all-start = ((f32[8,2,128]{2,1,0:T(2,128)}), f32[8,2,128]{2,1,0:T(2,128)S(1)}, u32[]{:S(2)}, u32[]{:S(2)}) async-start(f32[8,2,128]{2,1,0:T(2,128)} %broadcast_in_dim.696), calls=%async_computation | async-start | bytes 16384 | tf_op jit(solution)/shard_map/all_to_all | solution.py:21
  13.6 4.1 %all-to-all-done = f32[8,2,128]{2,1,0:T(2,128)S(1)} async-done(((f32[8,2,128]{2,1,0:T(2,128)}), f32[8,2,128]{2,1,0:T(2,128)S(1)}, u32[]{:S(2)}, u32[]{:S(2)}) %all-to-all-start) | async-done | bytes 8224 | tf_op jit(solution)/shard_map/all_to_all | solution.py:21
  17.7 4.0 %collective-permute-start.1 = (f32[1,2,128]{2,1,0:T(2,128)S(1)}, f32[1,2,128]{2,1,0:T(2,128)S(1)}, u32[]{:S(2)}, u32[]{:S(2)}) collective-permute-start(f32[1,2,128]{2,1,0:T(2,128)S(1)} %bitcast.1509), channel_id=1, source_target_pairs={{8,0},{16,8},{24,16},{32,24},{40,32},{48,40},{56,48},{64,56},{72,6... | collective-permute-start | bytes 3080 | tf_op jit(solution)/shard_map/ppermute | solution.py:38
  21.8 4.8 %collective-permute-start = (f32[1,2,128]{2,1,0:T(2,128)S(1)}, f32[1,2,128]{2,1,0:T(2,128)S(1)}, u32[]{:S(2)}, u32[]{:S(2)}) collective-permute-start(f32[1,2,128]{2,1,0:T(2,128)S(1)} %bitcast.1510), channel_id=1, source_target_pairs={{0,8},{8,16},{16,24},{24,32},{32,40},{40,48},{48,56},{56,64},{64,7... | collective-permute-start | bytes 3080 | tf_op jit(solution)/shard_map/ppermute | solution.py:36
  28.1 1.0 convolution_bitcast_fusion.7
  29.5 1.6 broadcast_in_dim.698
  31.1 3.6 %all-to-all-start.1 = ((f32[8,1,34816]{2,1,0:T(1,128)}), f32[8,1,34816]{2,1,0:T(1,128)S(1)}, u32[]{:S(2)}, u32[]{:S(2)}) async-start(f32[8,1,34816]{2,1,0:T(1,128)} %broadcast_in_dim.698), calls=%async_computation.1 | async-start | bytes 2228224 | tf_op jit(solution)/shard_map/all_to_all | solution.py:21
  35.4 13.0 %all-to-all-done.1 = f32[8,1,34816]{2,1,0:T(1,128)S(1)} async-done(((f32[8,1,34816]{2,1,0:T(1,128)}), f32[8,1,34816]{2,1,0:T(1,128)S(1)}, u32[]{:S(2)}, u32[]{:S(2)}) %all-to-all-start.1) | async-done | bytes 1114144 | tf_op jit(solution)/shard_map/all_to_all | solution.py:21
  57.1 8.4 %all_to_all.80 = f32[8,2,128]{2,1,0:T(2,128)S(1)} all-to-all(f32[8,2,128]{2,1,0:T(2,128)S(1)} %broadcast_in_dim.730), channel_id=1, replica_groups=mesh['obj'=32,'ep'=8] {'ep'}, dimensions={0} | all-to-all | bytes 16384 | tf_op jit(solution)/shard_map/all_to_all | solution.py:21
  65.5 3.7 %collective-permute-start.3 = (f32[1,2,128]{2,1,0:T(2,128)S(1)}, f32[1,2,128]{2,1,0:T(2,128)S(1)}, u32[]{:S(2)}, u32[]{:S(2)}) collective-permute-start(f32[1,2,128]{2,1,0:T(2,128)S(1)} %bitcast.1511), channel_id=1, source_target_pairs={{8,0},{16,8},{24,16},{32,24},{40,32},{48,40},{56,48},{64,56},{72,6... | collective-permute-start | bytes 3080 | tf_op jit(solution)/shard_map/ppermute | solution.py:38
  69.3 7.1 %collective-permute-start.2 = (f32[1,2,128]{2,1,0:T(2,128)S(1)}, f32[1,2,128]{2,1,0:T(2,128)S(1)}, u32[]{:S(2)}, u32[]{:S(2)}) collective-permute-start(f32[1,2,128]{2,1,0:T(2,128)S(1)} %bitcast.1512), channel_id=1, source_target_pairs={{0,8},{8,16},{16,24},{24,32},{32,40},{40,48},{48,56},{56,64},{64,7... | collective-permute-start | bytes 3080 | tf_op jit(solution)/shard_map/ppermute | solution.py:36
  78.0 21.2 %all_to_all.81 = f32[32,1,1088]{2,1,0:T(1,128)S(1)} all-to-all(f32[32,1,1088]{2,1,0:T(1,128)S(1)} %all_to_all.56), channel_id=1, replica_groups=mesh['obj'=32,'ep'=8] {'obj'}, dimensions={0} | all-to-all | bytes 278528 | tf_op jit(solution)/shard_map/all_to_all | solution.py:61
  99.3 14.7 %all_to_all.82 = f32[32,1,1088]{2,1,0:T(1,128)S(1)} all-to-all(f32[32,1,1088]{2,1,0:T(1,128)S(1)} %broadcast_in_dim.732), channel_id=1, replica_groups=mesh['obj'=32,'ep'=8] {'obj'}, dimensions={0} | all-to-all | bytes 278528 | tf_op jit(solution)/shard_map/all_to_all | solution.py:21
  122.8 7.6 %all_to_all.83 = f32[8,2,128]{2,1,0:T(2,128)S(1)} all-to-all(f32[8,2,128]{2,1,0:T(2,128)S(1)} %broadcast_in_dim.733), channel_id=1, replica_groups=mesh['obj'=32,'ep'=8] {'ep'}, dimensions={0} | all-to-all | bytes 16384 | tf_op jit(solution)/shard_map/all_to_all | solution.py:21
  130.4 3.4 %collective-permute-start.5 = (f32[1,2,128]{2,1,0:T(2,128)S(1)}, f32[1,2,128]{2,1,0:T(2,128)S(1)}, u32[]{:S(2)}, u32[]{:S(2)}) collective-permute-start(f32[1,2,128]{2,1,0:T(2,128)S(1)} %bitcast.1513), channel_id=1, source_target_pairs={{8,0},{16,8},{24,16},{32,24},{40,32},{48,40},{56,48},{64,56},{72,6... | collective-permute-start | bytes 3080 | tf_op jit(solution)/shard_map/ppermute | solution.py:38
  133.8 3.3 %collective-permute-start.4 = (f32[1,2,128]{2,1,0:T(2,128)S(1)}, f32[1,2,128]{2,1,0:T(2,128)S(1)}, u32[]{:S(2)}, u32[]{:S(2)}) collective-permute-start(f32[1,2,128]{2,1,0:T(2,128)S(1)} %bitcast.1514), channel_id=1, source_target_pairs={{0,8},{8,16},{16,24},{24,32},{32,40},{40,48},{48,56},{56,64},{64,7... | collective-permute-start | bytes 3080 | tf_op jit(solution)/shard_map/ppermute | solution.py:36
  138.8 19.2 %all_to_all.84 = f32[8,1,34816]{2,1,0:T(1,128)S(1)} all-to-all(f32[8,1,34816]{2,1,0:T(1,128)S(1)} %broadcast_in_dim.735), channel_id=1, replica_groups=mesh['obj'=32,'ep'=8] {'ep'}, dimensions={0} | all-to-all | bytes 2228224 | tf_op jit(solution)/shard_map/all_to_all | solution.py:21
  166.9 7.4 %all_to_all.85 = f32[8,2,128]{2,1,0:T(2,128)S(1)} all-to-all(f32[8,2,128]{2,1,0:T(2,128)S(1)} %broadcast_in_dim.736), channel_id=1, replica_groups=mesh['obj'=32,'ep'=8] {'ep'}, dimensions={0} | all-to-all | bytes 16384 | tf_op jit(solution)/shard_map/all_to_all | solution.py:21
  174.3 3.6 %collective-permute-start.7 = (f32[1,2,128]{2,1,0:T(2,128)S(1)}, f32[1,2,128]{2,1,0:T(2,128)S(1)}, u32[]{:S(2)}, u32[]{:S(2)}) collective-permute-start(f32[1,2,128]{2,1,0:T(2,128)S(1)} %bitcast.1515), channel_id=1, source_target_pairs={{8,0},{16,8},{24,16},{32,24},{40,32},{48,40},{56,48},{64,56},{72,6... | collective-permute-start | bytes 3080 | tf_op jit(solution)/shard_map/ppermute | solution.py:38
  178.0 3.6 %collective-permute-start.6 = (f32[1,2,128]{2,1,0:T(2,128)S(1)}, f32[1,2,128]{2,1,0:T(2,128)S(1)}, u32[]{:S(2)}, u32[]{:S(2)}) collective-permute-start(f32[1,2,128]{2,1,0:T(2,128)S(1)} %bitcast.1516), channel_id=1, source_target_pairs={{0,8},{8,16},{16,24},{24,32},{32,40},{40,48},{48,56},{56,64},{64,7... | collective-permute-start | bytes 3080 | tf_op jit(solution)/shard_map/ppermute | solution.py:36
  183.2 19.0 %all_to_all.86 = f32[32,1,1088]{2,1,0:T(1,128)S(1)} all-to-all(f32[32,1,1088]{2,1,0:T(1,128)S(1)} %all_to_all.62), channel_id=1, replica_groups=mesh['obj'=32,'ep'=8] {'obj'}, dimensions={0} | all-to-all | bytes 278528 | tf_op jit(solution)/shard_map/all_to_all | solution.py:61
  203.0 4.0 %all-to-all-start.9 = ((f32[32,1,1088]{2,1,0:T(1,128)}), f32[32,1,1088]{2,1,0:T(1,128)S(1)}, u32[]{:S(2)}, u32[]{:S(2)}) async-start(f32[32,1,1088]{2,1,0:T(1,128)} %broadcast_in_dim.738), calls=%async_computation.9 | async-start | bytes 294912 | tf_op jit(solution)/shard_map/all_to_all | solution.py:21
  207.0 11.0 %all-to-all-done.9 = f32[32,1,1088]{2,1,0:T(1,128)S(1)} async-done(((f32[32,1,1088]{2,1,0:T(1,128)}), f32[32,1,1088]{2,1,0:T(1,128)S(1)}, u32[]{:S(2)}, u32[]{:S(2)}) %all-to-all-start.9) | async-done | bytes 139296 | tf_op jit(solution)/shard_map/all_to_all | solution.py:21
  227.3 3.3 %all-to-all-start.10 = ((f32[8,2,128]{2,1,0:T(2,128)}), f32[8,2,128]{2,1,0:T(2,128)S(1)}, u32[]{:S(2)}, u32[]{:S(2)}) async-start(f32[8,2,128]{2,1,0:T(2,128)} %broadcast_in_dim.739), calls=%async_computation.10 | async-start | bytes 16384 | tf_op jit(solution)/shard_map/all_to_all | solution.py:21
  231.4 4.2 %all-to-all-done.10 = f32[8,2,128]{2,1,0:T(2,128)S(1)} async-done(((f32[8,2,128]{2,1,0:T(2,128)}), f32[8,2,128]{2,1,0:T(2,128)S(1)}, u32[]{:S(2)}, u32[]{:S(2)}) %all-to-all-start.10) | async-done | bytes 8224 | tf_op jit(solution)/shard_map/all_to_all | solution.py:21
  235.6 3.3 %collective-permute-start.9 = (f32[1,2,128]{2,1,0:T(2,128)S(1)}, f32[1,2,128]{2,1,0:T(2,128)S(1)}, u32[]{:S(2)}, u32[]{:S(2)}) collective-permute-start(f32[1,2,128]{2,1,0:T(2,128)S(1)} %bitcast.1507), channel_id=1, source_target_pairs={{8,0},{16,8},{24,16},{32,24},{40,32},{48,40},{56,48},{64,56},{72,6... | collective-permute-start | bytes 3080 | tf_op jit(solution)/shard_map/ppermute | solution.py:38
  238.9 3.4 %collective-permute-start.8 = (f32[1,2,128]{2,1,0:T(2,128)S(1)}, f32[1,2,128]{2,1,0:T(2,128)S(1)}, u32[]{:S(2)}, u32[]{:S(2)}) collective-permute-start(f32[1,2,128]{2,1,0:T(2,128)S(1)} %bitcast.1508), channel_id=1, source_target_pairs={{0,8},{8,16},{16,24},{24,32},{32,40},{40,48},{48,56},{56,64},{64,7... | collective-permute-start | bytes 3080 | tf_op jit(solution)/shard_map/ppermute | solution.py:36
  242.3 8.5 %cosine_convert_fusion.1 = (bf16[1024,256]{1,0:T(8,128)(2,1)S(1)}, bf16[1024,256]{1,0:T(8,128)(2,1)S(1)}, bf16[1024,256]{1,0:T(8,128)(2,1)S(1)}, bf16[1024,256]{1,0:T(8,128)(2,1)S(1)}) fusion(f32[256]{0:T(256)S(1)} %fusion.221, f32[1024]{0:T(1024)S(1)} %convert_add_fusion), kind=kLoop, calls=%fused_computation.36 | loop fusion | flops 2359296 | bytes 2102272 | tf_op jit(solution)/shard_map/convert.2
  251.0 23.3 %all_gather.3 = bf16[256,1024]{0,1:T(8,128)(2,1)S(1)} all-gather(bf16[256,128]{0,1:T(8,128)(2,1)S(1)} %pad_maximum_fusion.4), channel_id=1, replica_groups=mesh['obj'=32,'ep'=8] {'ep'}, dimensions={1}, use_global_device_ids=true | all-gather | bytes 589824 | tf_op jit(solution)/shard_map/all_gather | solution.py:98
  276.2 3.4 %all-to-all-start.11 = ((bf16[8,16,256]{2,1,0:T(8,128)(2,1)}), bf16[8,16,256]{2,1,0:T(8,128)(2,1)S(1)}, u32[]{:S(2)}, u32[]{:S(2)}) async-start(bf16[8,16,256]{2,1,0:T(8,128)(2,1)} %bitcast.380), calls=%async_computation.11 | async-start | bytes 131072 | tf_op jit(solution)/shard_map/all_to_all | solution.py:232
  280.3 4.4 %all-to-all-done.11 = bf16[8,16,256]{2,1,0:T(8,128)(2,1)S(1)} async-done(((bf16[8,16,256]{2,1,0:T(8,128)(2,1)}), bf16[8,16,256]{2,1,0:T(8,128)(2,1)S(1)}, u32[]{:S(2)}, u32[]{:S(2)}) %all-to-all-start.11) | async-done | bytes 65568 | tf_op jit(solution)/shard_map/all_to_all | solution.py:232
  (877 shorter events, 51.5 us)
Async XLA Ops:
  0.6 28.5 %copy-start.1 = (f32[128]{0:T(128)S(1)}, f32[128]{0:T(128)}, u32[]{:S(2)}) copy-start(f32[128]{0:T(128)} %param.10) | copy-start | bytes 1540
  6.3 11.4 %all-to-all-start = ((f32[8,2,128]{2,1,0:T(2,128)}), f32[8,2,128]{2,1,0:T(2,128)S(1)}, u32[]{:S(2)}, u32[]{:S(2)}) async-start(f32[8,2,128]{2,1,0:T(2,128)} %broadcast_in_dim.696), calls=%async_computation | async-start | bytes 16384 | tf_op jit(solution)/shard_map/all_to_all | solution.py:21
  17.7 9.6 %collective-permute-start.1 = (f32[1,2,128]{2,1,0:T(2,128)S(1)}, f32[1,2,128]{2,1,0:T(2,128)S(1)}, u32[]{:S(2)}, u32[]{:S(2)}) collective-permute-start(f32[1,2,128]{2,1,0:T(2,128)S(1)} %bitcast.1509), channel_id=1, source_target_pairs={{8,0},{16,8},{24,16},{32,24},{40,32},{48,40},{56,48},{64,56},{72,6... | collective-permute-start | bytes 3080 | tf_op jit(solution)/shard_map/ppermute | solution.py:38
  21.8 5.6 %collective-permute-start = (f32[1,2,128]{2,1,0:T(2,128)S(1)}, f32[1,2,128]{2,1,0:T(2,128)S(1)}, u32[]{:S(2)}, u32[]{:S(2)}) collective-permute-start(f32[1,2,128]{2,1,0:T(2,128)S(1)} %bitcast.1510), channel_id=1, source_target_pairs={{0,8},{8,16},{16,24},{24,32},{32,40},{40,48},{48,56},{56,64},{64,7... | collective-permute-start | bytes 3080 | tf_op jit(solution)/shard_map/ppermute | solution.py:36
  31.1 17.4 %all-to-all-start.1 = ((f32[8,1,34816]{2,1,0:T(1,128)}), f32[8,1,34816]{2,1,0:T(1,128)S(1)}, u32[]{:S(2)}, u32[]{:S(2)}) async-start(f32[8,1,34816]{2,1,0:T(1,128)} %broadcast_in_dim.698), calls=%async_computation.1 | async-start | bytes 2228224 | tf_op jit(solution)/shard_map/all_to_all | solution.py:21
  52.5 4.1 %copy-start = (f32[128,16]{0,1:T(8,128)S(1)}, f32[128,16]{0,1:T(8,128)}, u32[]{:S(2)}) copy-start(f32[128,16]{0,1:T(8,128)} %param.11) | copy-start | bytes 24580
  52.9 4.0 %copy-start.3 = (s32[128]{0:T(128)S(1)}, s32[128]{0:T(128)}, u32[]{:S(2)}) copy-start(s32[128]{0:T(128)} %param.9) | copy-start | bytes 1540
  65.5 10.9 %collective-permute-start.3 = (f32[1,2,128]{2,1,0:T(2,128)S(1)}, f32[1,2,128]{2,1,0:T(2,128)S(1)}, u32[]{:S(2)}, u32[]{:S(2)}) collective-permute-start(f32[1,2,128]{2,1,0:T(2,128)S(1)} %bitcast.1511), channel_id=1, source_target_pairs={{8,0},{16,8},{24,16},{32,24},{40,32},{48,40},{56,48},{64,56},{72,6... | collective-permute-start | bytes 3080 | tf_op jit(solution)/shard_map/ppermute | solution.py:38
  69.3 7.8 %collective-permute-start.2 = (f32[1,2,128]{2,1,0:T(2,128)S(1)}, f32[1,2,128]{2,1,0:T(2,128)S(1)}, u32[]{:S(2)}, u32[]{:S(2)}) collective-permute-start(f32[1,2,128]{2,1,0:T(2,128)S(1)} %bitcast.1512), channel_id=1, source_target_pairs={{0,8},{8,16},{16,24},{24,32},{32,40},{40,48},{48,56},{56,64},{64,7... | collective-permute-start | bytes 3080 | tf_op jit(solution)/shard_map/ppermute | solution.py:36
  130.4 6.7 %collective-permute-start.5 = (f32[1,2,128]{2,1,0:T(2,128)S(1)}, f32[1,2,128]{2,1,0:T(2,128)S(1)}, u32[]{:S(2)}, u32[]{:S(2)}) collective-permute-start(f32[1,2,128]{2,1,0:T(2,128)S(1)} %bitcast.1513), channel_id=1, source_target_pairs={{8,0},{16,8},{24,16},{32,24},{40,32},{48,40},{56,48},{64,56},{72,6... | collective-permute-start | bytes 3080 | tf_op jit(solution)/shard_map/ppermute | solution.py:38
  133.8 3.8 %collective-permute-start.4 = (f32[1,2,128]{2,1,0:T(2,128)S(1)}, f32[1,2,128]{2,1,0:T(2,128)S(1)}, u32[]{:S(2)}, u32[]{:S(2)}) collective-permute-start(f32[1,2,128]{2,1,0:T(2,128)S(1)} %bitcast.1514), channel_id=1, source_target_pairs={{0,8},{8,16},{16,24},{24,32},{32,40},{40,48},{48,56},{56,64},{64,7... | collective-permute-start | bytes 3080 | tf_op jit(solution)/shard_map/ppermute | solution.py:36
  174.3 7.2 %collective-permute-start.7 = (f32[1,2,128]{2,1,0:T(2,128)S(1)}, f32[1,2,128]{2,1,0:T(2,128)S(1)}, u32[]{:S(2)}, u32[]{:S(2)}) collective-permute-start(f32[1,2,128]{2,1,0:T(2,128)S(1)} %bitcast.1515), channel_id=1, source_target_pairs={{8,0},{16,8},{24,16},{32,24},{40,32},{48,40},{56,48},{64,56},{72,6... | collective-permute-start | bytes 3080 | tf_op jit(solution)/shard_map/ppermute | solution.py:38
  178.0 4.3 %collective-permute-start.6 = (f32[1,2,128]{2,1,0:T(2,128)S(1)}, f32[1,2,128]{2,1,0:T(2,128)S(1)}, u32[]{:S(2)}, u32[]{:S(2)}) collective-permute-start(f32[1,2,128]{2,1,0:T(2,128)S(1)} %bitcast.1516), channel_id=1, source_target_pairs={{0,8},{8,16},{16,24},{24,32},{32,40},{40,48},{48,56},{56,64},{64,7... | collective-permute-start | bytes 3080 | tf_op jit(solution)/shard_map/ppermute | solution.py:36
  182.6 24.3 %copy-start.2 = (f32[1024]{0:T(1024)S(1)}, f32[1024]{0:T(1024)}, u32[]{:S(2)}) copy-start(f32[1024]{0:T(1024)} %param.12) | copy-start | bytes 12292
  203.0 15.0 %all-to-all-start.9 = ((f32[32,1,1088]{2,1,0:T(1,128)}), f32[32,1,1088]{2,1,0:T(1,128)S(1)}, u32[]{:S(2)}, u32[]{:S(2)}) async-start(f32[32,1,1088]{2,1,0:T(1,128)} %broadcast_in_dim.738), calls=%async_computation.9 | async-start | bytes 294912 | tf_op jit(solution)/shard_map/all_to_all | solution.py:21
  227.3 8.3 %all-to-all-start.10 = ((f32[8,2,128]{2,1,0:T(2,128)}), f32[8,2,128]{2,1,0:T(2,128)S(1)}, u32[]{:S(2)}, u32[]{:S(2)}) async-start(f32[8,2,128]{2,1,0:T(2,128)} %broadcast_in_dim.739), calls=%async_computation.10 | async-start | bytes 16384 | tf_op jit(solution)/shard_map/all_to_all | solution.py:21
  235.6 15.2 %collective-permute-start.9 = (f32[1,2,128]{2,1,0:T(2,128)S(1)}, f32[1,2,128]{2,1,0:T(2,128)S(1)}, u32[]{:S(2)}, u32[]{:S(2)}) collective-permute-start(f32[1,2,128]{2,1,0:T(2,128)S(1)} %bitcast.1507), channel_id=1, source_target_pairs={{8,0},{16,8},{24,16},{32,24},{40,32},{48,40},{56,48},{64,56},{72,6... | collective-permute-start | bytes 3080 | tf_op jit(solution)/shard_map/ppermute | solution.py:38
  238.9 11.9 %collective-permute-start.8 = (f32[1,2,128]{2,1,0:T(2,128)S(1)}, f32[1,2,128]{2,1,0:T(2,128)S(1)}, u32[]{:S(2)}, u32[]{:S(2)}) collective-permute-start(f32[1,2,128]{2,1,0:T(2,128)S(1)} %bitcast.1508), channel_id=1, source_target_pairs={{0,8},{8,16},{16,24},{24,32},{32,40},{40,48},{48,56},{56,64},{64,7... | collective-permute-start | bytes 3080 | tf_op jit(solution)/shard_map/ppermute | solution.py:36
  276.2 8.5 %all-to-all-start.11 = ((bf16[8,16,256]{2,1,0:T(8,128)(2,1)}), bf16[8,16,256]{2,1,0:T(8,128)(2,1)S(1)}, u32[]{:S(2)}, u32[]{:S(2)}) async-start(bf16[8,16,256]{2,1,0:T(8,128)(2,1)} %bitcast.380), calls=%async_computation.11 | async-start | bytes 131072 | tf_op jit(solution)/shard_map/all_to_all | solution.py:232
where the time goes:
time: 290 us; the launch traced here: 285 us
  blocking collectives  121 us (42%)
  starting transfers between devices  60.7 us (21%)
  other arithmetic  40 us (14%)
  waiting for transfers between devices  38.6 us (13%)
  local copies, waits for them, and re-layouts  13.1 us (5%)
  matrix products  8.51 us (3%)
  between operations  3.72 us (1%)
    all_to_all x5, blocking collectives, copy_for_each(): return lax.all_to_all(copies, axis, split_axis=0, concat_axis=0, tiled=True)  57.3 us
    all_to_all x2, blocking collectives, sum_at_owner(): lax.all_to_all(pieces, axis, split_axis=0, concat_axis=0, tiled=True)  40.1 us
    all_to_all x4, waiting for transfers between devices, copy_for_each(): return lax.all_to_all(copies, axis, split_axis=0, concat_axis=0, tiled=True)  32.3 us
    all_gather x1, blocking collectives, in_one_piece(): whole = lax.all_gather(both, axis, axis=dim, tiled=True)  23.3 us
    ppermute x5, starting transfers between devices, with_halo(): lax.ppermute(tail, axis, [(i, (i + 1) % count) for i in range(ends)])  22.1 us
    ppermute x5, starting transfers between devices, with_halo(): lax.ppermute(head, axis, [((i + 1) % count, i) for i in range(ends)])  18 us
    all_to_all x4, starting transfers between devices, copy_for_each(): return lax.all_to_all(copies, axis, split_axis=0, concat_axis=0, tiled=True)  17.2 us
    another operation x2, other arithmetic  9.18 us
  transfers between devices with their start and end apart: 15, of which 8 were waited for; matrix products, arithmetic and copies ran while one was open for 4% of the time, Pallas kernels for 0%

commit v1 on v0

v1 whole, which is shorter than its diff:
```python
import jax
import jax.numpy as jnp
import numpy as np
from jax import lax
from jax.experimental import pallas as pl
from jax.experimental.pallas import tpu as pltpu
from jax.sharding import PartitionSpec as P

ITERS = 2
HUBER = 1.345
DAMP = 2.0
RIDGE = 0.05
INVALID = 1e9
F32 = jnp.float32
BF16 = jnp.bfloat16
LANES = 128
VMEM = 48 << 20
NT = (((1,), (1,)), ((), ()))
NN = (((1,), (0,)), ((), ()))


def dot(a, b, dims):
    return lax.dot_general(a, b, dims, preferred_element_type=F32)


def split2(x):
    hi = x.astype(BF16)
    lo = (x - hi.astype(F32)).astype(BF16)
    return hi, lo


def split3(x):
    hi = x.astype(BF16).astype(F32)
    rest = x - hi
    mid = rest.astype(BF16).astype(F32)
    low = (rest - mid).astype(BF16).astype(F32)
    return hi, mid, low


def solve_columns(rows, target):
    order = len(rows)
    half = order // 2
    rows = list(rows)
    scaled = [None] * order
    forward = [None] * order
    for k in range(order):
        at = k if k < half else k - half
        row = rows[k]
        inverse = 1.0 / (row[at : at + 1] + DAMP)
        unit = row * inverse
        scaled[k] = unit
        value = target[k : k + 1] * inverse
        forward[k] = value
        for i in range(k + 1, order):
            here = i if k < half else i - half
            factor = row[here : here + 1]
            if i >= half and k < half:
                rows[i] = rows[i] - factor * unit[half:]
            else:
                rows[i] = rows[i] - factor * unit
        if k < half:
            target = target - row * value
        else:
            target = jnp.concatenate([target[:half], target[half:] - row * value], axis=0)
    width = target.shape[1]
    level = lax.broadcasted_iota(jnp.int32, (half, width), 0)
    upper = jnp.zeros((half, width), F32)
    lower = jnp.zeros((half, width), F32)
    for k in reversed(range(order)):
        unit = scaled[k]
        if k >= half:
            value = forward[k] - jnp.sum(unit * lower, axis=0, keepdims=True)
            lower = jnp.where(level == k - half, value, lower)
        else:
            both = unit[:half] * upper + unit[half:] * lower
            value = forward[k] - jnp.sum(both, axis=0, keepdims=True)
            upper = jnp.where(level == k, value, upper)
    return jnp.concatenate([upper, lower], axis=0)


def outer_rows(x):
    half = x.shape[0] // 2
    upper = [x[i : i + 1] * x for i in range(half)]
    lower = [x[i : i + 1] * x[half:] for i in range(half, 2 * half)]
    return jnp.concatenate(upper + lower, axis=0)


def rows_of(gram, order):
    half = order // 2
    top = [gram[order * i : order * (i + 1)] for i in range(half)]
    start = order * half
    return top + [gram[start + half * i : start + half * (i + 1)] for i in range(half)]


def coef_factors(coef_t):
    order = coef_t.shape[0]
    hi, mid, low = split3(coef_t)
    none = jnp.zeros((LANES - 6 * order, coef_t.shape[1]), F32)
    stack = jnp.concatenate([hi, mid, low, hi, mid, hi, none], axis=0)
    return stack.T.astype(BF16)


def mode_factors(modes_b):
    order = modes_b.shape[0]
    hi, mid, low = split3(modes_b)
    none = jnp.zeros((LANES - 6 * order, modes_b.shape[1]), F32)
    return jnp.concatenate([hi, hi, hi, mid, mid, low, none], axis=0).astype(BF16)


def window(meta):
    rows = meta.shape[1]
    filled = jnp.concatenate([meta, jnp.zeros((LANES - meta.shape[0], rows), F32)], axis=0)
    turned = filled.T
    same = (turned[:, 0:1] == meta[0:1]).astype(F32).astype(BF16)
    return same, turned[:, 1:2]


def block_of(win_ref, b, own_rows, order):
    coded = jnp.concatenate([win_ref[b, :own_rows], win_ref[b, own_rows + order :]], axis=0)
    ok = coded < 0.5 * INVALID
    return ok, jnp.where(ok, coded, 0.0)


def pixel_total(same, part):
    hi, mid, low = split3(part)
    wide = jnp.concatenate([hi, mid, low], axis=1).astype(BF16)
    total = dot(same, wide, NN)
    total = total[:, :LANES] + total[:, LANES : 2 * LANES] + total[:, 2 * LANES :]
    return jnp.sum(total, axis=1, keepdims=True)


def spread_of(same, part, count):
    return jnp.sqrt(pixel_total(same, part) / jnp.maximum(count, 1.0) + 1e-06)


def robust_weight(ok, scaled, edge, sigma):
    return jnp.where(ok, (sigma * sigma) * (edge / jnp.maximum(jnp.abs(scaled), edge)), 0.0)


def natural_modes(arrived, blocks, group, order):
    turns = LANES // group
    lane = lax.broadcasted_iota(jnp.int32, (order, LANES), 1)
    turned = arrived.T
    out = []
    for b in range(blocks):
        tile, inner = divmod(b * group, LANES)
        total = jnp.zeros((order, LANES), F32)
        for r in range(turns):
            piece = turned[order * r : order * (r + 1), LANES * tile : LANES * (tile + 1)]
            shift = (group * r - inner) % LANES
            if shift:
                piece = pltpu.roll(piece, shift, 1)
            inside = (lane >= group * r) & (lane < group * (r + 1))
            total = jnp.where(inside, piece, total)
        out.append(total)
    return out


def prep_kernel(lc_ref, valid_ref, pix_ref, sig_ref, init_ref, own_ref, tail_ref, head_ref):
    rows = lc_ref.shape[0]
    half = rows // 2
    coded = jnp.where(valid_ref[...] != 0, lc_ref[...], INVALID)
    own_ref[:rows] = coded
    own_ref[rows:] = init_ref[...]
    meta = jnp.concatenate(
        [pix_ref[...].astype(F32), sig_ref[...], jnp.zeros((6, rows), F32)], axis=0
    )
    tail_ref[:half] = coded[half:]
    tail_ref[half:] = meta
    head_ref[:half] = coded[:half]
    head_ref[half:] = meta


def widen_kernel(own_ref, left_ref, right_ref, pix_ref, sig_ref, out_ref, meta_ref):
    rows = pix_ref.shape[1]
    half = rows // 2
    own = own_ref[...]
    top = own.shape[0]
    left = left_ref[...]
    right = right_ref[...]
    for b in range(out_ref.shape[0]):
        out_ref[b, :top] = own
        out_ref[b, top : top + half] = left[:half]
        out_ref[b, top + half :] = right[:half]
    lane = lax.broadcasted_iota(jnp.int32, (8, rows), 1)
    beyond = pltpu.roll(jnp.where(lane >= half, left[half:], right[half:]), half, 1)
    meta_ref[:, :rows] = jnp.concatenate(
        [pix_ref[...].astype(F32), sig_ref[...], jnp.zeros((6, rows), F32)], axis=0
    )
    meta_ref[:, rows:] = beyond


def make_step_kernel(first):
    def kernel(*refs):
        if first:
            place_ref, meta_ref, win_ref = refs[:3]
            rest = refs[3:]
        else:
            place_ref, meta_ref, win_ref, arrived_ref, before_ref = refs[:5]
            rest = refs[5:]
        coef_ref, send_ref, scal_ref, wh_ref, wl_ref, ph_ref, pl_ref, oh_ref, ol_ref, mh_ref, ml_ref, ms_ref = rest
        blocks = win_ref.shape[0]
        order = coef_ref.shape[0]
        rows = meta_ref.shape[1]
        own_rows = rows // 2
        group = send_ref.shape[0] // 8
        same, sigma = window(meta_ref[...])
        if first:
            modes = [win_ref[b, own_rows : own_rows + order] for b in range(blocks)]
        else:
            modes = natural_modes(arrived_ref[...], blocks, group, order)
            factors = coef_factors(before_ref[...])
        part = jnp.zeros((rows, LANES), F32)
        seen = jnp.zeros((rows, LANES), F32)
        for b in range(blocks):
            ok, lc = block_of(win_ref, b, own_rows, order)
            ms_ref[b] = mode_factors(modes[b])
            if not first:
                lc = lc - dot(factors, ms_ref[b], NN)
            scaled = lc * sigma
            scal_ref[b] = scaled
            part = part + jnp.where(ok, scaled * scaled, 0.0)
            seen = seen + jnp.where(ok, 1.0, 0.0)
        count = jnp.sum(dot(same, seen.astype(BF16), NN), axis=1, keepdims=True)
        edge = HUBER * spread_of(same, part, count)
        for b in range(blocks):
            ok, lc = block_of(win_ref, b, own_rows, order)
            weight = robust_weight(ok, scal_ref[b], edge, sigma)
            at = slice(LANES * b, LANES * (b + 1))
            wh_ref[:, at], wl_ref[:, at] = split2(weight)
            ph_ref[:, at], pl_ref[:, at] = split2(weight * lc)
            oh_ref[:, at], ol_ref[:, at] = split2(outer_rows(modes[b]))
            mh_ref[:, at], ml_ref[:, at] = split2(modes[b])
        gram = (
            dot(oh_ref[...], wh_ref[...], NT)
            + dot(oh_ref[...], wl_ref[...], NT)
            + dot(ol_ref[...], wh_ref[...], NT)
        )
        target = (
            dot(mh_ref[...], ph_ref[...], NT)
            + dot(mh_ref[...], pl_ref[...], NT)
            + dot(ml_ref[...], ph_ref[...], NT)
        )
        coef_t = solve_columns(rows_of(gram, order), target)
        coef_ref[...] = coef_t
        factors = coef_factors(coef_t)
        part = jnp.zeros((rows, LANES), F32)
        for b in range(blocks):
            ok, lc = block_of(win_ref, b, own_rows, order)
            scaled = (lc - dot(factors, ms_ref[b], NN)) * sigma
            scal_ref[b] = scaled
            part = part + jnp.where(ok, scaled * scaled, 0.0)
        edge = HUBER * spread_of(same, part, count)
        place = place_ref[0]
        coded = win_ref[place, :own_rows]
        ok = coded < 0.5 * INVALID
        lc = jnp.where(ok, coded, 0.0)
        weight = robust_weight(ok, scal_ref[place, :own_rows], edge[:own_rows], sigma[:own_rows])
        weight_hi, weight_lo = split2(weight)
        value_hi, value_lo = split2(weight * lc)
        own_coef = coef_t[:, :own_rows]
        outer_hi, outer_lo = split2(outer_rows(own_coef))
        coef_hi, coef_lo = split2(own_coef)
        gram = dot(outer_hi, weight_hi, NN) + dot(outer_hi, weight_lo, NN) + dot(outer_lo, weight_hi, NN)
        target = dot(coef_hi, value_hi, NN) + dot(coef_hi, value_lo, NN) + dot(coef_lo, value_hi, NN)
        spare = jnp.zeros((2 * LANES - gram.shape[0] - order, LANES), F32)
        tall = jnp.concatenate([gram, target, spare], axis=0)
        turns = LANES // group
        for side in range(2):
            turned = tall[LANES * side : LANES * (side + 1)].T
            for r in range(turns):
                send_ref[pl.ds(turns * side + r, group, stride=8), :] = turned[group * r : group * (r + 1)]

    return kernel


def mode_kernel(arrived_ref, out_ref, *, order):
    total = arrived_ref[0]
    for j in range(1, arrived_ref.shape[0]):
        total = total + arrived_ref[j]
    turns = total.shape[0] // 2
    tall = jnp.concatenate([total, jnp.zeros((LANES - 2 * turns, LANES), F32)], axis=0).T
    after = pltpu.roll(tall, LANES - turns, 1)
    half = order // 2
    gram = jnp.concatenate([tall, after[: half * half]], axis=0)
    target = after[half * half : half * half + order]
    solved = solve_columns(rows_of(gram, order), target)
    lane = lax.broadcasted_iota(jnp.int32, solved.shape, 1)
    solved = jnp.where(lane < turns, solved, 0.0)
    wide = jnp.concatenate([solved, jnp.zeros((LANES - order, LANES), F32)], axis=0).T
    line = wide[0:1]
    for r in range(1, turns):
        line = line + pltpu.roll(wide[0:8], order * r, 1)[r : r + 1]
    out_ref[...] = jnp.broadcast_to(line.reshape(1, 1, LANES), out_ref.shape)


def sine_series(terms):
    x = (np.cos(np.pi * (np.arange(400) + 0.5) / 400) + 1) / 2 * 0.0625
    v = np.sqrt(x)
    scale = 0.0625
    grid = x / scale
    sine = np.polynomial.polynomial.polyfit(grid, np.sin(2 * np.pi * v) / v, terms)
    cosine = np.polynomial.polynomial.polyfit(grid, np.cos(2 * np.pi * v), terms)
    power = scale ** np.arange(terms + 1)
    return [float(c) for c in sine / power], [float(c) for c in cosine / power]


SINE, COSINE = sine_series(6)


def horner(series, x):
    total = jnp.full(x.shape, series[-1], F32)
    for c in series[-2::-1]:
        total = total * x + c
    return total


def basis_kernel(jitter_ref, freq_ref, out_ref):
    blocks, width = jitter_ref.shape[0], freq_ref.shape[1]
    jitter = jnp.concatenate([jitter_ref[...], jnp.zeros((LANES - blocks, LANES), F32)], axis=0).T
    freqs = freq_ref[...]
    for b in range(blocks):
        index = lax.broadcasted_iota(jnp.int32, (LANES, 1), 0) + LANES * b
        times = index.astype(F32) + jitter[:, b : b + 1]
        cycles = times * freqs
        turn = cycles - jnp.floor(cycles)
        turn = jnp.where(turn >= 0.5, turn - 1.0, turn)
        far = jnp.abs(turn) > 0.25
        near = jnp.where(far, jnp.where(turn > 0.0, 0.5, -0.5) - turn, turn)
        square = near * near
        sine = near * horner(SINE, square)
        cosine = horner(COSINE, square)
        cosine = jnp.where(far, -cosine, cosine)
        at = slice(LANES * b, LANES * (b + 1))
        out_ref[at, :width] = cosine.astype(BF16)
        out_ref[at, width : 2 * width] = sine.astype(BF16)
        out_ref[at, 2 * width : 3 * width] = (1.0 - 2.0 * sine * sine).astype(BF16)
        out_ref[at, 3 * width :] = (2.0 * sine * cosine).astype(BF16)


def final_kernel(place_ref, meta_ref, win_ref, arrived_ref, coef_ref, basis_ref, lc_ref,
                 resid_ref, power_ref, res_ref, w_ref, q_ref, *, group):
    blocks = win_ref.shape[0]
    order = coef_ref.shape[0]
    rows = meta_ref.shape[1]
    own_rows = rows // 2
    same, sigma = window(meta_ref[...])
    modes = natural_modes(arrived_ref[...], blocks, group, order)
    factors = coef_factors(coef_ref[...])
    part = jnp.zeros((rows, LANES), F32)
    seen = jnp.zeros((rows, LANES), F32)
    for b in range(blocks):
        ok, lc = block_of(win_ref, b, own_rows, order)
        trend = dot(factors, mode_factors(modes[b]), NN)
        resid = lc - trend
        res_ref[b] = resid[:own_rows]
        scaled = resid * sigma
        part = part + jnp.where(ok, scaled * scaled, 0.0)
        seen = seen + jnp.where(ok, 1.0, 0.0)
    count = jnp.sum(dot(same, seen.astype(BF16), NN), axis=1, keepdims=True)
    edge = (HUBER * spread_of(same, part, count))[:own_rows]
    sigma = sigma[:own_rows]
    total = jnp.zeros((own_rows, LANES), F32)
    level = jnp.zeros((own_rows, LANES), F32)
    for b in range(blocks):
        ok = win_ref[b, :own_rows] < 0.5 * INVALID
        resid = res_ref[b]
        weight = robust_weight(ok, resid * sigma, edge, sigma)
        at = slice(LANES * b, LANES * (b + 1))
        weight_b = weight.astype(BF16)
        value_b = (weight * resid).astype(BF16)
        w_ref[:, at] = weight_b
        q_ref[:, at] = value_b
        total = total + weight_b.astype(F32)
        level = level + value_b.astype(F32)
    place = place_ref[0]
    resid = res_ref[place]
    ok = win_ref[place, :own_rows] < 0.5 * INVALID
    resid_ref[...] = jnp.where(ok, resid, lc_ref[...] + resid)
    total = jnp.sum(total, axis=1, keepdims=True)
    level = jnp.sum(level, axis=1, keepdims=True)
    by_weight = dot(w_ref[...], basis_ref[...], NN)
    width = by_weight.shape[1] // 4
    by_value = dot(q_ref[...], basis_ref[:, : 2 * width], NN)
    cosine = by_weight[:, :width]
    sine = by_weight[:, width : 2 * width]
    cosine_two = by_weight[:, 2 * width : 3 * width]
    sine_two = by_weight[:, 3 * width :]
    inverse = 1.0 / total
    mean_level = level * inverse
    ycos = by_value[:, :width] - mean_level * cosine
    ysin = by_value[:, width:] - mean_level * sine
    cc_term = 0.5 * (total + cosine_two) - cosine * cosine * inverse + RIDGE * total
    ss_term = 0.5 * (total - cosine_two) - sine * sine * inverse + RIDGE * total
    cs_term = 0.5 * sine_two - cosine * sine * inverse
    determinant = cc_term * ss_term - cs_term * cs_term
    power = (ss_term * ycos * ycos + cc_term * ysin * ysin - 2.0 * cs_term * ycos * ysin) / determinant
    power_ref[...] = power.astype(BF16)


def place_kernel(in_ref, out_ref):
    width = in_ref.shape[2]
    for b in range(in_ref.shape[0]):
        out_ref[:, width * b : width * (b + 1)] = in_ref[b].astype(F32)


def shaped(shape, dtype=F32):
    return jax.ShapeDtypeStruct(shape, dtype)


def call(kernel, out_shape, args, scratch=(), scalar=False, staged=(), name=None):
    specs = [
        pl.BlockSpec(a.shape, lambda i, n=a.ndim: (0,) * n)
        if at in staged
        else pl.BlockSpec(memory_space=pltpu.VMEM)
        for at, a in enumerate(args)
    ]
    if scalar:
        specs[0] = pl.BlockSpec(memory_space=pltpu.SMEM)
    many = isinstance(out_shape, (tuple, list))
    out_specs = [pl.BlockSpec(memory_space=pltpu.VMEM) for _ in (out_shape if many else [0])]
    return pl.pallas_call(
        kernel,
        grid=(1,),
        out_shape=out_shape,
        in_specs=specs,
        out_specs=out_specs if many else out_specs[0],
        scratch_shapes=list(scratch),
        compiler_params=pltpu.CompilerParams(vmem_limit_bytes=VMEM),
        name=name,
    )(*args)


def per_device(light_curves, valid, pixel, inv_sigma, modes_init, epoch_jitter, freq_index):
    obj_count = lax.axis_size("obj")
    ep_count = lax.axis_size("ep")
    rows, cols = light_curves.shape
    order = modes_init.shape[1]
    half = rows // 2
    span = ep_count * cols
    group = obj_count
    place = lax.axis_index("ep").astype(jnp.int32)
    places = place.reshape(1)

    pixels = pixel.reshape(1, rows)
    sigmas = inv_sigma.reshape(1, rows)
    own, tail, head = call(
        prep_kernel,
        (shaped((rows + order, cols)), shaped((half + 8, cols)), shaped((half + 8, cols))),
        (light_curves, valid, pixels, sigmas, modes_init.T),
        staged=range(5),
        name="prep",
    )
    ring = [(i, (i + 1) % obj_count) for i in range(obj_count)]
    back = [(i, (i - 1) % obj_count) for i in range(obj_count)]
    left = lax.ppermute(tail, "obj", ring)
    right = lax.ppermute(head, "obj", back)
    wide, meta = call(
        widen_kernel,
        (shaped((ep_count, 2 * rows + order, cols)), shaped((8, 2 * rows))),
        (own, left, right, pixels, sigmas),
        staged=(3, 4),
        name="widen",
    )
    win = lax.all_to_all(wide, "ep", split_axis=0, concat_axis=0, tiled=True)

    width = freq_index.shape[0] // ep_count
    freqs = (lax.dynamic_slice_in_dim(freq_index, place * width, width) + 1).astype(F32) / (4.0 * span)
    basis = call(
        basis_kernel,
        shaped((span, 4 * width), BF16),
        (epoch_jitter.reshape(ep_count, cols), freqs.reshape(1, width)),
        name="basis",
    )

    window_rows = 2 * rows
    products = order * order * 3 // 4
    scratch = [
        pltpu.VMEM((ep_count, window_rows, LANES), F32),
        pltpu.VMEM((window_rows, span), BF16),
        pltpu.VMEM((window_rows, span), BF16),
        pltpu.VMEM((window_rows, span), BF16),
        pltpu.VMEM((window_rows, span), BF16),
        pltpu.VMEM((products, span), BF16),
        pltpu.VMEM((products, span), BF16),
        pltpu.VMEM((order, span), BF16),
        pltpu.VMEM((order, span), BF16),
        pltpu.VMEM((ep_count, LANES, LANES), BF16),
    ]
    args = (places, meta, win)
    everyone = ep_count * obj_count
    for iteration in range(ITERS):
        coef_t, send = call(
            make_step_kernel(iteration == 0),
            (shaped((order, window_rows)), shaped((8 * group, LANES))),
            args,
            scratch=scratch,
            scalar=True,
            name=f"objects_{iteration}",
        )
        arrived = lax.all_to_all(
            send.reshape(group, 8, LANES), "obj", split_axis=0, concat_axis=0, tiled=True
        )
        lines = call(
            lambda a, o: mode_kernel(a, o, order=order),
            shaped((everyone, 1, LANES)),
            (arrived,),
            name=f"modes_{iteration}",
        )
        lines = lax.all_to_all(lines, ("ep", "obj"), split_axis=0, concat_axis=0, tiled=True)
        args = (places, meta, win, lines.reshape(everyone, LANES), coef_t)
    residual, power = call(
        lambda *refs: final_kernel(*refs, group=group),
        (shaped((rows, cols)), shaped((rows, width), BF16)),
        (*args, basis, light_curves),
        staged=(6,),
        scratch=[
            pltpu.VMEM((ep_count, rows, LANES), F32),
            pltpu.VMEM((rows, span), BF16),
            pltpu.VMEM((rows, span), BF16),
        ],
        scalar=True,
        name="spectrum",
    )
    share = rows // ep_count
    power = lax.all_to_all(
        power.reshape(ep_count, share, width), "ep", split_axis=0, concat_axis=0, tiled=True
    )
    power = call(place_kernel, shaped((share, ep_count * width)), (power,), name="place")
    return residual, power


def solution(mesh):
    in_specs = (P("obj", "ep"), P("obj", "ep"), P("obj"), P("obj"), P("ep", None), P(), P())
    out_specs = (P("obj", "ep"), P(("obj", "ep"), None))
    return jax.shard_map(
        per_device, mesh=mesh, in_specs=in_specs, out_specs=out_specs, check_vma=False
    )
```

time: 290 us -> 129 us (0.44); the launches traced: 285 us -> 128 us
  blocking collectives: 121 us -> 62 us
  starting transfers between devices: 60.7 us -> 15.6 us
  other arithmetic: 40 us -> 0.8 us
  Pallas kernels: 0 us -> 15.8 us
  local copies, waits for them, and re-layouts: 13.1 us -> 3.69 us
  waiting for transfers between devices: 38.6 us -> 29.4 us
  matrix products: 8.51 us -> 0 us
  between operations: 3.72 us -> 0.71 us
    ppermute x10 -> x2, starting transfers between devices: 40.1 us -> 4.46 us  [the longest x1 4.46 us: per_device(): left = lax.ppermute(tail, 'obj', ring)]
    all_to_all x7 -> x4, blocking collectives: 97.4 us -> 62 us  [the longest x2 36.1 us: per_device(): lax.all_to_all(send.reshape(group, 8, LANES), 'obj', split_axis=0, concat...]
    all_gather x1 -> x0, blocking collectives: 23.3 us -> none  [in_one_piece(): whole = lax.all_gather(both, axis, axis=dim, tiled=True)]
    pallas_call x0 -> x9, Pallas kernels: none -> 15.8 us  [call(): pl.pallas_call(kernel, grid=(1,), out_shape=out_shape, in_specs=specs, ou...]
    all_to_all x5 -> x2, waiting for transfers between devices: 36.7 us -> 25.2 us  [the longest x1 14.8 us: per_device(): win = lax.all_to_all(wide, 'ep', split_axis=0, concat_axis=0, tiled=True)]
    another operation x23 -> x0, other arithmetic: 9.74 us -> none
    all_to_all x5 -> x2, starting transfers between devices: 20.6 us -> 11.2 us  [the longest x1 5.84 us: per_device(): win = lax.all_to_all(wide, 'ep', split_axis=0, concat_axis=0, tiled=True)]
    sub x116 -> x0, other arithmetic: 8.66 us -> none  [the longest x60 4.46 us: damped_solve(): column = column - jnp.sum(earlier * earlier[column_at][None], axis=1)]
  transfers between devices with their start and end apart: 15 -> 4, of which waited for: 8 -> 4; matrix products, arithmetic and copies ran while one was open for 4% -> 1% of each run, Pallas kernels for 0% -> 1%
where the time goes in v1:
time: 129 us; the launch traced here: 128 us
  blocking collectives  62 us (48%)
  waiting for transfers between devices  29.4 us (23%)
  Pallas kernels  15.8 us (12%)
  starting transfers between devices  15.6 us (12%)
  local copies, waits for them, and re-layouts  3.69 us (3%)
    all_to_all x2, blocking collectives, per_device(): lax.all_to_all(send.reshape(group, 8, LANES), 'obj', split_axis=0, concat...  36.1 us
    all_to_all x1, blocking collectives, per_device(): lax.all_to_all(lines, ('ep', 'obj'), split_axis=0, concat_axis=0, tiled=T...  17.9 us
    pallas_call x9, Pallas kernels, call(): pl.pallas_call(kernel, grid=(1,), out_shape=out_shape, in_specs=specs, ou...  15.8 us
    all_to_all x1, waiting for transfers between devices, per_device(): win = lax.all_to_all(wide, 'ep', split_axis=0, concat_axis=0, tiled=True)  14.8 us
    all_to_all x1, waiting for transfers between devices, per_device(): lax.all_to_all(lines, ('ep', 'obj'), split_axis=0, concat_axis=0, tiled=T...  10.4 us
    all_to_all x1, blocking collectives, per_device(): lax.all_to_all(power.reshape(ep_count, share, width), 'ep', split_axis=0,...  8.05 us
    all_to_all x1, starting transfers between devices, per_device(): win = lax.all_to_all(wide, 'ep', split_axis=0, concat_axis=0, tiled=True)  5.84 us
    all_to_all x1, starting transfers between devices, per_device(): lax.all_to_all(lines, ('ep', 'obj'), split_axis=0, concat_axis=0, tiled=T...  5.34 us
  transfers between devices with their start and end apart: 4, of which 4 were waited for; matrix products, arithmetic and copies ran while one was open for 1% of the time, Pallas kernels for 1%

profile of v1, /device:TPU:1, one launch (start us, length us, event | category | flops | bytes accessed | tf_op | source)
XLA Modules:
  0.0 128.1 jit_solution(13800504475609250038)
XLA Ops:
  0.6 0.0 copy-start
  0.6 0.8 copy-done
  1.5 0.0 copy-start.2
  1.5 0.8 copy-done.2
  2.3 0.7 copy-done.3
  3.0 0.7 copy-done.5
  3.7 0.7 copy-done.6
  4.3 4.5 %collective-permute-start = (f32[72,128]{1,0:T(8,128)S(1)}, f32[72,128]{1,0:T(8,128)S(1)}, u32[]{:S(2)}, u32[]{:S(2)}) collective-permute-start(f32[72,128]{1,0:T(8,128)S(1)} %get-tuple-element.14), channel_id=1, source_target_pairs={{0,8},{8,16},{16,24},{24,32},{32,40},{40,48},{48,56},{56,64},{64,7... | collective-permute-start | bytes 110600 | tf_op jit(solution)/shard_map/ppermute | solution.py:456
  8.8 0.0 collective-permute-start.1
  8.8 1.1 collective-permute-done.left_ref
  9.9 3.2 %collective-permute-done.1.right_ref = f32[72,128]{1,0:T(8,128)S(1)} collective-permute-done((f32[72,128]{1,0:T(8,128)S(1)}, f32[72,128]{1,0:T(8,128)S(1)}, u32[]{:S(2)}, u32[]{:S(2)}) %collective-permute-start.1) | collective-permute-done | bytes 36896 | tf_op jit(solution)/shard_map/ppermute | solution.py:457
  13.1 1.1 widen.1
  14.2 5.8 %all-to-all-start = ((f32[8,272,128]{2,1,0:T(8,128)}), f32[8,272,128]{2,1,0:T(8,128)S(1)}, u32[]{:S(2)}, u32[]{:S(2)}) async-start(f32[8,272,128]{2,1,0:T(8,128)} %get-tuple-element.17), calls=%async_computation | async-start | bytes 2228224 | tf_op jit(solution)/shard_map/all_to_all | solution.py:465
  20.0 14.8 %all-to-all-done.refs_2_ = f32[8,272,128]{2,1,0:T(8,128)S(1)} async-done(((f32[8,272,128]{2,1,0:T(8,128)}), f32[8,272,128]{2,1,0:T(8,128)S(1)}, u32[]{:S(2)}, u32[]{:S(2)}) %all-to-all-start) | async-done | bytes 1114144 | tf_op jit(solution)/shard_map/all_to_all | solution.py:465
  34.8 3.8 %objects_0.1 = (f32[16,256]{1,0:T(8,128)S(1)}, f32[256,128]{1,0:T(8,128)S(1)}) custom-call(s32[1]{0:T(128)} %bitcast.refs_0_, f32[8,256]{1,0:T(8,128)S(1)} %get-tuple-element.16.refs_1_, f32[8,272,128]{2,1,0:T(8,128)S(1)} %all-to-all-done.refs_2_), custom_call_target="tpu_custom_call" | custom-call | tf_op jit(solution)/shard_map/objects_0/pallas_call | solution.py:422
  38.6 21.3 %all_to_all.30.a = f32[32,8,128]{2,1,0:T(8,128)S(1)} all-to-all(f32[32,8,128]{2,1,0:T(8,128)S(1)} %bitcast.14), channel_id=1, replica_groups=mesh['obj'=32,'ep'=8] {'obj'}, dimensions={0} | all-to-all | bytes 262144 | tf_op jit(solution)/shard_map/all_to_all | solution.py:501
  59.9 0.6 modes_0.1
  60.5 0.0 copy-start.4
  60.5 17.9 %all_to_all.31 = f32[256,1,128]{2,1,0:T(1,128)S(1)} all-to-all(f32[256,1,128]{2,1,0:T(1,128)S(1)} %modes_0.1), channel_id=1, replica_groups=mesh['obj'=32,'ep'=8] {'ep','obj'}, dimensions={0} | all-to-all | bytes 262144 | tf_op jit(solution)/shard_map/all_to_all | solution.py:510
  78.4 4.2 %objects_1.1 = (f32[16,256]{1,0:T(8,128)S(1)}, f32[256,128]{1,0:T(8,128)S(1)}) custom-call(s32[1]{0:T(128)} %bitcast.refs_0_, f32[8,256]{1,0:T(8,128)S(1)} %get-tuple-element.16.refs_1_, f32[8,272,128]{2,1,0:T(8,128)S(1)} %all-to-all-done.refs_2_, f32[256,128]{1,0:T(8,128)S(1)} %bitcast.12, f32[16,256]{1,0:T(8,128)S(1)} %get-tuple-element.19.refs_4_), custom_call_target="tpu_custom_call" | custom-call | tf_op jit(solution)/shard_map/objects_1/pallas_call | solution.py:422
  82.6 14.8 %all_to_all.32.a = f32[32,8,128]{2,1,0:T(8,128)S(1)} all-to-all(f32[32,8,128]{2,1,0:T(8,128)S(1)} %bitcast.13), channel_id=1, replica_groups=mesh['obj'=32,'ep'=8] {'obj'}, dimensions={0} | all-to-all | bytes 262144 | tf_op jit(solution)/shard_map/all_to_all | solution.py:501
  97.5 1.3 %modes_1.1 = f32[256,1,128]{2,1,0:T(1,128)} custom-call(f32[32,8,128]{2,1,0:T(8,128)S(1)} %all_to_all.32.a), custom_call_target="tpu_custom_call" | custom-call | tf_op jit(solution)/shard_map/modes_1/pallas_call | solution.py:422
  98.8 5.3 %all-to-all-start.4 = ((f32[256,1,128]{2,1,0:T(1,128)}), f32[256,1,128]{2,1,0:T(1,128)S(1)}, u32[]{:S(2)}, u32[]{:S(2)}) async-start(f32[256,1,128]{2,1,0:T(1,128)} %modes_1.1), calls=%async_computation.4 | async-start | bytes 262144 | tf_op jit(solution)/shard_map/all_to_all | solution.py:510
  104.1 0.0 copy-start.1
  104.1 0.8 convert_multiply_fusion
  104.9 0.0 copy-done.4
  104.9 1.7 %basis.1.refs_5_ = bf16[1024,1024]{1,0:T(8,128)(2,1)S(1)} custom-call(f32[8,128]{1,0:T(8,128)S(1)} %bitcast.17, f32[1,256]{1,0:T(1,128)S(1)} %bitcast.18), custom_call_target="tpu_custom_call" | custom-call | tf_op jit(solution)/shard_map/basis/pallas_call | solution.py:422
  106.7 10.4 %all-to-all-done.4 = f32[256,1,128]{2,1,0:T(1,128)S(1)} async-done(((f32[256,1,128]{2,1,0:T(1,128)}), f32[256,1,128]{2,1,0:T(1,128)S(1)}, u32[]{:S(2)}, u32[]{:S(2)}) %all-to-all-start.4) | async-done | bytes 131104 | tf_op jit(solution)/shard_map/all_to_all | solution.py:510
  117.0 0.0 copy-done.1
  117.0 2.3 %spectrum.1 = (f32[128,128]{1,0:T(8,128)}, bf16[128,256]{1,0:T(8,128)(2,1)S(1)}) custom-call(s32[1]{0:T(128)} %bitcast.refs_0_, f32[8,256]{1,0:T(8,128)S(1)} %get-tuple-element.16.refs_1_, f32[8,272,128]{2,1,0:T(8,128)S(1)} %all-to-all-done.refs_2_, f32[256,128]{1,0:T(8,128)S(1)} %bitcast.11, f32[16,256]{1,0:T(8,128)S(1)} %get-tuple-element.21.refs_4_, ...), custom_call_target="tpu_custom_call" | custom-call | tf_op jit(solution)/shard_map/spectrum/pallas_call | solution.py:422
  119.4 8.0 %all_to_all.33.in_ref = bf16[8,16,256]{2,1,0:T(8,128)(2,1)S(1)} all-to-all(bf16[8,16,256]{2,1,0:T(8,128)(2,1)S(1)} %bitcast.15), channel_id=1, replica_groups=mesh['obj'=32,'ep'=8] {'ep'}, dimensions={0} | all-to-all | bytes 131072 | tf_op jit(solution)/shard_map/all_to_all | solution.py:526
  127.4 0.7 place.1
  (4 shorter events, 0.0 us)
Async XLA Ops:
  0.6 0.8 copy-start
  1.5 0.8 copy-start.2
  2.3 0.7 copy-start.3
  3.0 0.7 copy-start.5
  3.7 0.7 copy-start.6
  4.3 5.5 %collective-permute-start = (f32[72,128]{1,0:T(8,128)S(1)}, f32[72,128]{1,0:T(8,128)S(1)}, u32[]{:S(2)}, u32[]{:S(2)}) collective-permute-start(f32[72,128]{1,0:T(8,128)S(1)} %get-tuple-element.14), channel_id=1, source_target_pairs={{0,8},{8,16},{16,24},{24,32},{32,40},{40,48},{48,56},{56,64},{64,7... | collective-permute-start | bytes 110600 | tf_op jit(solution)/shard_map/ppermute | solution.py:456
  8.8 4.3 %collective-permute-start.1 = (f32[72,128]{1,0:T(8,128)S(1)}, f32[72,128]{1,0:T(8,128)S(1)}, u32[]{:S(2)}, u32[]{:S(2)}) collective-permute-start(f32[72,128]{1,0:T(8,128)S(1)} %get-tuple-element.15), channel_id=1, source_target_pairs={{0,248},{8,0},{16,8},{24,16},{32,24},{40,32},{48,40},{56,48},{64,5... | collective-permute-start | bytes 110600 | tf_op jit(solution)/shard_map/ppermute | solution.py:457
  14.2 20.6 %all-to-all-start = ((f32[8,272,128]{2,1,0:T(8,128)}), f32[8,272,128]{2,1,0:T(8,128)S(1)}, u32[]{:S(2)}, u32[]{:S(2)}) async-start(f32[8,272,128]{2,1,0:T(8,128)} %get-tuple-element.17), calls=%async_computation | async-start | bytes 2228224 | tf_op jit(solution)/shard_map/all_to_all | solution.py:465
  60.5 44.4 %copy-start.4 = (f32[1024]{0:T(1024)S(1)}, f32[1024]{0:T(1024)}, u32[]{:S(2)}) copy-start(f32[1024]{0:T(1024)} %param.12) | copy-start | bytes 12292
  98.8 18.3 %all-to-all-start.4 = ((f32[256,1,128]{2,1,0:T(1,128)}), f32[256,1,128]{2,1,0:T(1,128)S(1)}, u32[]{:S(2)}, u32[]{:S(2)}) async-start(f32[256,1,128]{2,1,0:T(1,128)} %modes_1.1), calls=%async_computation.4 | async-start | bytes 262144 | tf_op jit(solution)/shard_map/all_to_all | solution.py:510
  104.1 12.9 %copy-start.1 = (f32[128,128]{1,0:T(8,128)S(1)}, f32[128,128]{1,0:T(8,128)}, u32[]{:S(2)}) copy-start(f32[128,128]{1,0:T(8,128)} %refs_6_.1) | copy-start | bytes 196612

commit v2 on v1

--- a/solution.py
+++ b/solution.py
@@ -14,7 +14,7 @@
 F32 = jnp.float32
 BF16 = jnp.bfloat16
 LANES = 128
-VMEM = 48 << 20
+VMEM = 14 << 20
 NT = (((1,), (1,)), ((), ()))
 NN = (((1,), (0,)), ((), ()))
 
@@ -156,7 +156,16 @@
     return out
 
 
-def prep_kernel(lc_ref, valid_ref, pix_ref, sig_ref, init_ref, own_ref, tail_ref, head_ref):
+def prep_kernel(lc_hbm, valid_hbm, pix_hbm, sig_hbm, init_hbm, own_ref, tail_ref, head_ref,
+                lc_ref, valid_ref, pix_ref, sig_ref, init_ref, sems):
+    pairs = (
+        (lc_hbm, lc_ref), (valid_hbm, valid_ref), (pix_hbm, pix_ref), (sig_hbm, sig_ref), (init_hbm, init_ref)
+    )
+    copies = [pltpu.make_async_copy(a, b, sems.at[i]) for i, (a, b) in enumerate(pairs)]
+    for copy in copies:
+        copy.start()
+    for copy in copies:
+        copy.wait()
     rows = lc_ref.shape[0]
     half = rows // 2
     coded = jnp.where(valid_ref[...] != 0, lc_ref[...], INVALID)
@@ -171,8 +180,8 @@
     head_ref[half:] = meta
 
 
-def widen_kernel(own_ref, left_ref, right_ref, pix_ref, sig_ref, out_ref, meta_ref):
-    rows = pix_ref.shape[1]
+def widen_kernel(own_ref, tail_ref, left_ref, right_ref, out_ref, meta_ref):
+    rows = tail_ref.shape[1]
     half = rows // 2
     own = own_ref[...]
     top = own.shape[0]
@@ -184,9 +193,7 @@
         out_ref[b, top + half :] = right[:half]
     lane = lax.broadcasted_iota(jnp.int32, (8, rows), 1)
     beyond = pltpu.roll(jnp.where(lane >= half, left[half:], right[half:]), half, 1)
-    meta_ref[:, :rows] = jnp.concatenate(
-        [pix_ref[...].astype(F32), sig_ref[...], jnp.zeros((6, rows), F32)], axis=0
-    )
+    meta_ref[:, :rows] = tail_ref[half:]
     meta_ref[:, rows:] = beyond
 
 
@@ -294,48 +301,49 @@
     out_ref[...] = jnp.broadcast_to(line.reshape(1, 1, LANES), out_ref.shape)
 
 
-def sine_series(terms):
-    x = (np.cos(np.pi * (np.arange(400) + 0.5) / 400) + 1) / 2 * 0.0625
-    v = np.sqrt(x)
-    scale = 0.0625
-    grid = x / scale
-    sine = np.polynomial.polynomial.polyfit(grid, np.sin(2 * np.pi * v) / v, terms)
-    cosine = np.polynomial.polynomial.polyfit(grid, np.cos(2 * np.pi * v), terms)
-    power = scale ** np.arange(terms + 1)
+def half_turn_series():
+    grid = (np.cos(np.pi * (np.arange(400) + 0.5) / 400) + 1) / 2
+    u = np.sqrt(grid) / 2
+    sine = np.polynomial.polynomial.polyfit(grid, np.sin(np.pi * u) / u, 5)
+    cosine = np.polynomial.polynomial.polyfit(grid, np.cos(np.pi * u), 5)
+    power = 0.25 ** np.arange(6)
     return [float(c) for c in sine / power], [float(c) for c in cosine / power]
 
 
-SINE, COSINE = sine_series(6)
+SINE, COSINE = half_turn_series()
 
 
 def horner(series, x):
-    total = jnp.full(x.shape, series[-1], F32)
-    for c in series[-2::-1]:
+    total = x * series[-1] + series[-2]
+    for c in series[-3::-1]:
         total = total * x + c
     return total
 
 
-def basis_kernel(jitter_ref, freq_ref, out_ref):
+def basis_kernel(jitter_ref, freq_ref, out_ref, time_ref):
     blocks, width = jitter_ref.shape[0], freq_ref.shape[1]
     jitter = jnp.concatenate([jitter_ref[...], jnp.zeros((LANES - blocks, LANES), F32)], axis=0).T
-    freqs = freq_ref[...]
+    index = lax.broadcasted_iota(jnp.int32, (LANES, LANES), 0)
     for b in range(blocks):
-        index = lax.broadcasted_iota(jnp.int32, (LANES, 1), 0) + LANES * b
-        times = index.astype(F32) + jitter[:, b : b + 1]
-        cycles = times * freqs
-        turn = cycles - jnp.floor(cycles)
-        turn = jnp.where(turn >= 0.5, turn - 1.0, turn)
-        far = jnp.abs(turn) > 0.25
-        near = jnp.where(far, jnp.where(turn > 0.0, 0.5, -0.5) - turn, turn)
-        square = near * near
-        sine = near * horner(SINE, square)
-        cosine = horner(COSINE, square)
-        cosine = jnp.where(far, -cosine, cosine)
-        at = slice(LANES * b, LANES * (b + 1))
-        out_ref[at, :width] = cosine.astype(BF16)
-        out_ref[at, width : 2 * width] = sine.astype(BF16)
-        out_ref[at, 2 * width : 3 * width] = (1.0 - 2.0 * sine * sine).astype(BF16)
-        out_ref[at, 3 * width :] = (2.0 * sine * cosine).astype(BF16)
+        time_ref[LANES * b : LANES * (b + 1)] = (index + LANES * b).astype(F32) + jitter[:, b : b + 1]
+    step = 32
+
+    @pl.loop(0, time_ref.shape[0] // step)
+    def _(i):
+        at = pl.ds(pl.multiple_of(step * i, step), step)
+        times = time_ref[at]
+        for c in range(width // LANES):
+            cycles = times * freq_ref[:, LANES * c : LANES * (c + 1)]
+            turn = cycles - jnp.floor(cycles + 0.5)
+            square = turn * turn
+            sine = turn * horner(SINE, square)
+            cosine = horner(COSINE, square)
+            for k in range(2):
+                twice = sine + sine
+                sine, cosine = twice * cosine, 1.0 - twice * sine
+                start = 2 * k * width + LANES * c
+                out_ref[at, start : start + LANES] = cosine.astype(BF16)
+                out_ref[at, start + width : start + width + LANES] = sine.astype(BF16)
 
 
 def final_kernel(place_ref, meta_ref, win_ref, arrived_ref, coef_ref, basis_ref, lc_ref,
@@ -408,25 +416,19 @@
     return jax.ShapeDtypeStruct(shape, dtype)
 
 
-def call(kernel, out_shape, args, scratch=(), scalar=False, staged=(), name=None):
-    specs = [
-        pl.BlockSpec(a.shape, lambda i, n=a.ndim: (0,) * n)
-        if at in staged
-        else pl.BlockSpec(memory_space=pltpu.VMEM)
-        for at, a in enumerate(args)
-    ]
+def call(kernel, out_shape, args, scratch=(), scalar=False, away=(), out_space=pltpu.VMEM, limit=VMEM, name=None):
+    specs = [pl.BlockSpec(memory_space=pltpu.HBM if at in away else pltpu.VMEM) for at in range(len(args))]
     if scalar:
         specs[0] = pl.BlockSpec(memory_space=pltpu.SMEM)
     many = isinstance(out_shape, (tuple, list))
-    out_specs = [pl.BlockSpec(memory_space=pltpu.VMEM) for _ in (out_shape if many else [0])]
+    out_specs = [pl.BlockSpec(memory_space=out_space) for _ in (out_shape if many else [0])]
     return pl.pallas_call(
         kernel,
-        grid=(1,),
         out_shape=out_shape,
         in_specs=specs,
         out_specs=out_specs if many else out_specs[0],
         scratch_shapes=list(scratch),
-        compiler_params=pltpu.CompilerParams(vmem_limit_bytes=VMEM),
+        compiler_params=pltpu.CompilerParams(vmem_limit_bytes=limit),
         name=name,
     )(*args)
 
@@ -442,13 +444,14 @@
     place = lax.axis_index("ep").astype(jnp.int32)
     places = place.reshape(1)
 
-    pixels = pixel.reshape(1, rows)
-    sigmas = inv_sigma.reshape(1, rows)
+    fetched = (light_curves, valid, pixel.reshape(1, rows), inv_sigma.reshape(1, rows), modes_init.T)
+    fetched = tuple(pltpu.with_memory_space_constraint(a, pltpu.HBM) for a in fetched)
     own, tail, head = call(
         prep_kernel,
         (shaped((rows + order, cols)), shaped((half + 8, cols)), shaped((half + 8, cols))),
-        (light_curves, valid, pixels, sigmas, modes_init.T),
-        staged=range(5),
+        fetched,
+        scratch=[pltpu.VMEM(a.shape, a.dtype) for a in fetched] + [pltpu.SemaphoreType.DMA((5,))],
+        away=range(5),
         name="prep",
     )
     ring = [(i, (i + 1) % obj_count) for i in range(obj_count)]
@@ -458,20 +461,21 @@
     wide, meta = call(
         widen_kernel,
         (shaped((ep_count, 2 * rows + order, cols)), shaped((8, 2 * rows))),
-        (own, left, right, pixels, sigmas),
-        staged=(3, 4),
+        (own, tail, left, right),
         name="widen",
     )
-    win = lax.all_to_all(wide, "ep", split_axis=0, concat_axis=0, tiled=True)
-
     width = freq_index.shape[0] // ep_count
     freqs = (lax.dynamic_slice_in_dim(freq_index, place * width, width) + 1).astype(F32) / (4.0 * span)
+    wide, freqs = lax.optimization_barrier((wide, freqs))
+    win = lax.all_to_all(wide, "ep", split_axis=0, concat_axis=0, tiled=True)
     basis = call(
         basis_kernel,
         shaped((span, 4 * width), BF16),
         (epoch_jitter.reshape(ep_count, cols), freqs.reshape(1, width)),
+        scratch=[pltpu.VMEM((span, LANES), F32)],
         name="basis",
     )
+    win, basis = lax.optimization_barrier((win, basis))
 
     window_rows = 2 * rows
     products = order * order * 3 // 4
@@ -513,7 +517,6 @@
         lambda *refs: final_kernel(*refs, group=group),
         (shaped((rows, cols)), shaped((rows, width), BF16)),
         (*args, basis, light_curves),
-        staged=(6,),
         scratch=[
             pltpu.VMEM((ep_count, rows, LANES), F32),
             pltpu.VMEM((rows, span), BF16),

time: 129 us -> 124 us (0.961)
  blocking collectives: 62 us -> 84 us
  waiting for transfers between devices: 29.4 us -> 12.9 us
  starting transfers between devices: 15.6 us -> 9.32 us
  local copies, waits for them, and re-layouts: 3.69 us -> 0.01 us
    all_to_all x1 -> x2, blocking collectives: 17.9 us -> 36.1 us  [per_device(): lax.all_to_all(lines, ('ep', 'obj'), split_axis=0, concat_axis=0, tiled=T...]
    all_to_all x1 -> x0, waiting for transfers between devices: 10.4 us -> none  [per_device(): lax.all_to_all(lines, ('ep', 'obj'), split_axis=0, concat_axis=0, tiled=T...]
    all_to_all x1, waiting for transfers between devices: 14.8 us -> 7.95 us  [per_device(): win = lax.all_to_all(wide, 'ep', split_axis=0, concat_axis=0, tiled=True)]
    all_to_all x1 -> x0, starting transfers between devices: 5.34 us -> none  [per_device(): lax.all_to_all(lines, ('ep', 'obj'), split_axis=0, concat_axis=0, tiled=T...]
    all_to_all x2, blocking collectives: 36.1 us -> 39.9 us  [per_device(): lax.all_to_all(send.reshape(group, 8, LANES), 'obj', split_axis=0, concat...]
    unnamed x14 -> x4, local copies, waits for them, and re-layouts: 3.69 us -> 0.01 us
    ppermute x1, starting transfers between devices: 0.01 us -> 3.32 us  [per_device(): right = lax.ppermute(head, 'obj', back)]
    ppermute x1, starting transfers between devices: 4.46 us -> 1.23 us  [per_device(): left = lax.ppermute(tail, 'obj', ring)]
  transfers between devices with their start and end apart: 4 -> 3, of which waited for: 4 -> 3; matrix products, arithmetic and copies ran while one was open for 1% -> 1% of each run, Pallas kernels for 1% -> 1%
where the time goes in v2:
time: 124 us
  blocking collectives  84 us (68%)
  Pallas kernels  16.1 us (13%)
  waiting for transfers between devices  12.9 us (10%)
  starting transfers between devices  9.32 us (8%)
    all_to_all x2, blocking collectives, per_device(): lax.all_to_all(send.reshape(group, 8, LANES), 'obj', split_axis=0, concat...  39.9 us
    all_to_all x2, blocking collectives, per_device(): lax.all_to_all(lines, ('ep', 'obj'), split_axis=0, concat_axis=0, tiled=T...  36.1 us
    pallas_call x9, Pallas kernels, call(): pl.pallas_call(kernel, out_shape=out_shape, in_specs=specs, out_specs=out...  16.1 us
    all_to_all x1, blocking collectives, per_device(): lax.all_to_all(power.reshape(ep_count, share, width), 'ep', split_axis=0,...  8.05 us
    all_to_all x1, waiting for transfers between devices, per_device(): win = lax.all_to_all(wide, 'ep', split_axis=0, concat_axis=0, tiled=True)  7.95 us
    all_to_all x1, starting transfers between devices, per_device(): win = lax.all_to_all(wide, 'ep', split_axis=0, concat_axis=0, tiled=True)  4.78 us
    ppermute x1, waiting for transfers between devices, per_device(): left = lax.ppermute(tail, 'obj', ring)  4.12 us
    ppermute x1, starting transfers between devices, per_device(): right = lax.ppermute(head, 'obj', back)  3.32 us
  transfers between devices with their start and end apart: 3, of which 3 were waited for; matrix products, arithmetic and copies ran while one was open for 1% of the time, Pallas kernels for 1%

profile of v2, /device:TPU:1, one launch (start us, length us, event | category | flops | bytes accessed | tf_op | source)
XLA Modules:
  0.0 123.8 jit_solution(17270741428409109641)
XLA Ops:
  0.6 0.9 prep.1
  1.6 3.3 %collective-permute-start.1 = (f32[72,128]{1,0:T(8,128)S(1)}, f32[72,128]{1,0:T(8,128)S(1)}, u32[]{:S(2)}, u32[]{:S(2)}) collective-permute-start(f32[72,128]{1,0:T(8,128)S(1)} %get-tuple-element.19), channel_id=1, source_target_pairs={{0,248},{8,0},{16,8},{24,16},{32,24},{40,32},{48,40},{56,48},{64,5... | collective-permute-start | bytes 110600 | tf_op jit(solution)/shard_map/ppermute | solution.py:460
  4.9 1.2 collective-permute-start
  6.1 0.8 convert_multiply_fusion
  6.9 0.8 collective-permute-done.1.right_ref
  7.7 4.1 %collective-permute-done.left_ref = f32[72,128]{1,0:T(8,128)S(1)} collective-permute-done((f32[72,128]{1,0:T(8,128)S(1)}, f32[72,128]{1,0:T(8,128)S(1)}, u32[]{:S(2)}, u32[]{:S(2)}) %collective-permute-start) | collective-permute-done | bytes 36896 | tf_op jit(solution)/shard_map/ppermute | solution.py:459
  11.8 1.1 widen.1
  12.9 0.0 copy-start.1
  12.9 4.8 %all-to-all-start = ((f32[8,272,128]{2,1,0:T(8,128)}), f32[8,272,128]{2,1,0:T(8,128)S(1)}, u32[]{:S(2)}, u32[]{:S(2)}) async-start(f32[8,272,128]{2,1,0:T(8,128)} %get-tuple-element.22), calls=%async_computation | async-start | bytes 2228224 | tf_op jit(solution)/shard_map/all_to_all | solution.py:470
  17.7 0.0 copy-done.1
  17.7 1.8 %basis.1.refs_5_ = bf16[1024,1024]{1,0:T(8,128)(2,1)S(1)} custom-call(f32[8,128]{1,0:T(8,128)S(1)} %bitcast.16, f32[1,256]{1,0:T(1,128)S(1)} %bitcast.17), custom_call_target="tpu_custom_call" | custom-call | tf_op jit(solution)/shard_map/basis/pallas_call | solution.py:425
  19.5 8.0 %all-to-all-done.refs_2_ = f32[8,272,128]{2,1,0:T(8,128)S(1)} async-done(((f32[8,272,128]{2,1,0:T(8,128)}), f32[8,272,128]{2,1,0:T(8,128)S(1)}, u32[]{:S(2)}, u32[]{:S(2)}) %all-to-all-start) | async-done | bytes 1114144 | tf_op jit(solution)/shard_map/all_to_all | solution.py:470
  27.5 3.8 %objects_0.1 = (f32[16,256]{1,0:T(8,128)S(1)}, f32[256,128]{1,0:T(8,128)S(1)}) custom-call(s32[1]{0:T(128)} %bitcast.refs_0_, f32[8,256]{1,0:T(8,128)S(1)} %get-tuple-element.20.refs_1_, f32[8,272,128]{2,1,0:T(8,128)S(1)} %all-to-all-done.refs_2_), custom_call_target="tpu_custom_call" | custom-call | tf_op jit(solution)/shard_map/objects_0/pallas_call | solution.py:425
  31.3 25.1 %all_to_all.30.a = f32[32,8,128]{2,1,0:T(8,128)S(1)} all-to-all(f32[32,8,128]{2,1,0:T(8,128)S(1)} %bitcast.14), channel_id=1, replica_groups=mesh['obj'=32,'ep'=8] {'obj'}, dimensions={0} | all-to-all | bytes 262144 | tf_op jit(solution)/shard_map/all_to_all | solution.py:505
  56.3 0.6 modes_0.1
  57.0 0.0 copy-start
  57.0 18.0 %all_to_all.31 = f32[256,1,128]{2,1,0:T(1,128)S(1)} all-to-all(f32[256,1,128]{2,1,0:T(1,128)S(1)} %modes_0.1), channel_id=1, replica_groups=mesh['obj'=32,'ep'=8] {'ep','obj'}, dimensions={0} | all-to-all | bytes 262144 | tf_op jit(solution)/shard_map/all_to_all | solution.py:514
  75.0 4.2 %objects_1.1 = (f32[16,256]{1,0:T(8,128)S(1)}, f32[256,128]{1,0:T(8,128)S(1)}) custom-call(s32[1]{0:T(128)} %bitcast.refs_0_, f32[8,256]{1,0:T(8,128)S(1)} %get-tuple-element.20.refs_1_, f32[8,272,128]{2,1,0:T(8,128)S(1)} %all-to-all-done.refs_2_, f32[256,128]{1,0:T(8,128)S(1)} %bitcast.12, f32[16,256]{1,0:T(8,128)S(1)} %get-tuple-element.26.refs_4_), custom_call_target="tpu_custom_call" | custom-call | tf_op jit(solution)/shard_map/objects_1/pallas_call | solution.py:425
  79.2 14.9 %all_to_all.32.a = f32[32,8,128]{2,1,0:T(8,128)S(1)} all-to-all(f32[32,8,128]{2,1,0:T(8,128)S(1)} %bitcast.13), channel_id=1, replica_groups=mesh['obj'=32,'ep'=8] {'obj'}, dimensions={0} | all-to-all | bytes 262144 | tf_op jit(solution)/shard_map/all_to_all | solution.py:505
  94.1 0.6 modes_1.1
  94.7 18.1 %all_to_all.33 = f32[256,1,128]{2,1,0:T(1,128)S(1)} all-to-all(f32[256,1,128]{2,1,0:T(1,128)S(1)} %modes_1.1), channel_id=1, replica_groups=mesh['obj'=32,'ep'=8] {'ep','obj'}, dimensions={0} | all-to-all | bytes 262144 | tf_op jit(solution)/shard_map/all_to_all | solution.py:514
  112.8 0.0 copy-done
  112.8 2.3 %spectrum.1 = (f32[128,128]{1,0:T(8,128)}, bf16[128,256]{1,0:T(8,128)(2,1)S(1)}) custom-call(s32[1]{0:T(128)} %bitcast.refs_0_, f32[8,256]{1,0:T(8,128)S(1)} %get-tuple-element.20.refs_1_, f32[8,272,128]{2,1,0:T(8,128)S(1)} %all-to-all-done.refs_2_, f32[256,128]{1,0:T(8,128)S(1)} %bitcast.11, f32[16,256]{1,0:T(8,128)S(1)} %get-tuple-element.28.refs_4_, ...), custom_call_target="tpu_custom_call" | custom-call | tf_op jit(solution)/shard_map/spectrum/pallas_call | solution.py:425
  115.1 8.1 %all_to_all.34.in_ref = bf16[8,16,256]{2,1,0:T(8,128)(2,1)S(1)} all-to-all(bf16[8,16,256]{2,1,0:T(8,128)(2,1)S(1)} %bitcast.15), channel_id=1, replica_groups=mesh['obj'=32,'ep'=8] {'ep'}, dimensions={0} | all-to-all | bytes 131072 | tf_op jit(solution)/shard_map/all_to_all | solution.py:529
  123.2 0.7 place.1
Async XLA Ops:
  1.6 6.1 %collective-permute-start.1 = (f32[72,128]{1,0:T(8,128)S(1)}, f32[72,128]{1,0:T(8,128)S(1)}, u32[]{:S(2)}, u32[]{:S(2)}) collective-permute-start(f32[72,128]{1,0:T(8,128)S(1)} %get-tuple-element.19), channel_id=1, source_target_pairs={{0,248},{8,0},{16,8},{24,16},{32,24},{40,32},{48,40},{56,48},{64,5... | collective-permute-start | bytes 110600 | tf_op jit(solution)/shard_map/ppermute | solution.py:460
  4.9 6.9 %collective-permute-start = (f32[72,128]{1,0:T(8,128)S(1)}, f32[72,128]{1,0:T(8,128)S(1)}, u32[]{:S(2)}, u32[]{:S(2)}) collective-permute-start(f32[72,128]{1,0:T(8,128)S(1)} %get-tuple-element.18.tail_ref), channel_id=1, source_target_pairs={{0,8},{8,16},{16,24},{24,32},{32,40},{40,48},{48,56},{56,64},{64,7... | collective-permute-start | bytes 110600 | tf_op jit(solution)/shard_map/ppermute | solution.py:459
  12.9 4.8 %copy-start.1 = (f32[1024]{0:T(1024)S(1)}, f32[1024]{0:T(1024)}, u32[]{:S(2)}) copy-start(f32[1024]{0:T(1024)} %param.12) | copy-start | bytes 12292
  12.9 14.6 %all-to-all-start = ((f32[8,272,128]{2,1,0:T(8,128)}), f32[8,272,128]{2,1,0:T(8,128)S(1)}, u32[]{:S(2)}, u32[]{:S(2)}) async-start(f32[8,272,128]{2,1,0:T(8,128)} %get-tuple-element.22), calls=%async_computation | async-start | bytes 2228224 | tf_op jit(solution)/shard_map/all_to_all | solution.py:470
  57.0 55.8 %copy-start = (f32[128,128]{1,0:T(8,128)S(1)}, f32[128,128]{1,0:T(8,128)}, u32[]{:S(2)}) copy-start(f32[128,128]{1,0:T(8,128)} %refs_6_.1) | copy-start | bytes 196612

commit v3 on v2

--- a/solution.py
+++ b/solution.py
@@ -15,6 +15,12 @@
 BF16 = jnp.bfloat16
 LANES = 128
 VMEM = 14 << 20
+CHUNKS = 4
+NEAR = 1
+EARLY = 1
+SLAB = 256
+PARTS = 4
+NEAREST = 1.5 * 2.0**23
 NT = (((1,), (1,)), ((), ()))
 NN = (((1,), (0,)), ((), ()))
 
@@ -304,10 +310,9 @@
 def half_turn_series():
     grid = (np.cos(np.pi * (np.arange(400) + 0.5) / 400) + 1) / 2
     u = np.sqrt(grid) / 2
-    sine = np.polynomial.polynomial.polyfit(grid, np.sin(np.pi * u) / u, 5)
+    sine = np.polynomial.polynomial.polyfit(grid, np.sin(np.pi * u) / u, 4)
     cosine = np.polynomial.polynomial.polyfit(grid, np.cos(np.pi * u), 5)
-    power = 0.25 ** np.arange(6)
-    return [float(c) for c in sine / power], [float(c) for c in cosine / power]
+    return [float(c) * 4.0**k for k, c in enumerate(sine)], [float(c) * 4.0**k for k, c in enumerate(cosine)]
 
 
 SINE, COSINE = half_turn_series()
@@ -320,7 +325,8 @@
     return total
 
 
-def basis_kernel(jitter_ref, freq_ref, out_ref, time_ref):
+def basis_kernel(jitter_ref, freq_ref, *rest):
+    (out_ref, time_ref), far = (rest, None) if len(rest) == 2 else ((rest[2], rest[1]), rest)
     blocks, width = jitter_ref.shape[0], freq_ref.shape[1]
     jitter = jnp.concatenate([jitter_ref[...], jnp.zeros((LANES - blocks, LANES), F32)], axis=0).T
     index = lax.broadcasted_iota(jnp.int32, (LANES, LANES), 0)
@@ -328,30 +334,55 @@
         time_ref[LANES * b : LANES * (b + 1)] = (index + LANES * b).astype(F32) + jitter[:, b : b + 1]
     step = 32
 
-    @pl.loop(0, time_ref.shape[0] // step)
-    def _(i):
+    def copy(b):
+        at = pl.ds(pl.multiple_of(LANES * b, LANES), LANES)
+        return pltpu.make_async_copy(out_ref.at[at], far[0].at[at], far[3].at[b])
+
+    def rows_from(i):
         at = pl.ds(pl.multiple_of(step * i, step), step)
         times = time_ref[at]
         for c in range(width // LANES):
             cycles = times * freq_ref[:, LANES * c : LANES * (c + 1)]
-            turn = cycles - jnp.floor(cycles + 0.5)
+            turn = cycles - ((cycles + NEAREST) - NEAREST)
             square = turn * turn
             sine = turn * horner(SINE, square)
             cosine = horner(COSINE, square)
-            for k in range(2):
-                twice = sine + sine
-                sine, cosine = twice * cosine, 1.0 - twice * sine
-                start = 2 * k * width + LANES * c
-                out_ref[at, start : start + LANES] = cosine.astype(BF16)
-                out_ref[at, start + width : start + width + LANES] = sine.astype(BF16)
-
-
-def final_kernel(place_ref, meta_ref, win_ref, arrived_ref, coef_ref, basis_ref, lc_ref,
-                 resid_ref, power_ref, res_ref, w_ref, q_ref, *, group):
+            twice = sine + sine
+            start = LANES * c
+            out_ref[at, start : start + LANES] = (1.0 - twice * sine).astype(BF16)
+            out_ref[at, start + width : start + width + LANES] = (twice * cosine).astype(BF16)
+
+    @pl.loop(0, blocks)
+    def _(b):
+        @pl.loop(0, LANES // step)
+        def _(i):
+            rows_from(b * (LANES // step) + i)
+
+        if far:
+            copy(b).start()
+
+    if far:
+
+        @pl.loop(0, blocks)
+        def _(b):
+            copy(b).wait()
+
+
+def final_kernel(place_ref, meta_ref, win_ref, arrived_ref, coef_ref, lc_ref, *rest, group):
+    far, (resid_ref, power_ref, res_ref, col_ref, both_ref) = rest[:CHUNKS], rest[CHUNKS : CHUNKS + 5]
+    basis_refs, sems = far[:NEAR] + rest[CHUNKS + 5 : -1], rest[-1]
+    copies = [None] * (PARTS * NEAR)
+    for c in range(NEAR, CHUNKS):
+        tall = basis_refs[c].shape[0] // PARTS
+        for k in range(PARTS):
+            at = pl.ds(tall * k, tall)
+            copies.append(pltpu.make_async_copy(far[c].at[at], basis_refs[c].at[at], sems.at[c * PARTS + k]))
+            copies[-1].start()
     blocks = win_ref.shape[0]
     order = coef_ref.shape[0]
     rows = meta_ref.shape[1]
     own_rows = rows // 2
+    share = power_ref.shape[0]
     same, sigma = window(meta_ref[...])
     modes = natural_modes(arrived_ref[...], blocks, group, order)
     factors = coef_factors(coef_ref[...])
@@ -359,57 +390,69 @@
     seen = jnp.zeros((rows, LANES), F32)
     for b in range(blocks):
         ok, lc = block_of(win_ref, b, own_rows, order)
-        trend = dot(factors, mode_factors(modes[b]), NN)
-        resid = lc - trend
+        resid = lc - dot(factors, mode_factors(modes[b]), NN)
         res_ref[b] = resid[:own_rows]
         scaled = resid * sigma
         part = part + jnp.where(ok, scaled * scaled, 0.0)
         seen = seen + jnp.where(ok, 1.0, 0.0)
     count = jnp.sum(dot(same, seen.astype(BF16), NN), axis=1, keepdims=True)
-    edge = (HUBER * spread_of(same, part, count))[:own_rows]
-    sigma = sigma[:own_rows]
-    total = jnp.zeros((own_rows, LANES), F32)
-    level = jnp.zeros((own_rows, LANES), F32)
+    edge = HUBER * spread_of(same, part, count)
+    col_ref[0] = jnp.broadcast_to(edge[:own_rows], (own_rows, LANES))
+    col_ref[1] = jnp.broadcast_to(sigma[:own_rows], (own_rows, LANES))
+    place = place_ref[0]
+    ok = win_ref[place, :own_rows] < 0.5 * INVALID
+    resid = res_ref[place]
+    resid_ref[...] = jnp.where(ok, resid, lc_ref[...] + resid)
+    mine = pl.ds(pl.multiple_of(place * share, share), share)
+    edge = col_ref[0, mine]
+    sigma = col_ref[1, mine]
+    total = jnp.zeros((share, LANES), F32)
+    level = jnp.zeros((share, LANES), F32)
     for b in range(blocks):
-        ok = win_ref[b, :own_rows] < 0.5 * INVALID
-        resid = res_ref[b]
+        ok = win_ref[b, mine] < 0.5 * INVALID
+        resid = res_ref[b, mine]
         weight = robust_weight(ok, resid * sigma, edge, sigma)
         at = slice(LANES * b, LANES * (b + 1))
         weight_b = weight.astype(BF16)
         value_b = (weight * resid).astype(BF16)
-        w_ref[:, at] = weight_b
-        q_ref[:, at] = value_b
+        both_ref[:share, at] = weight_b
+        both_ref[share:, at] = value_b
         total = total + weight_b.astype(F32)
         level = level + value_b.astype(F32)
-    place = place_ref[0]
-    resid = res_ref[place]
-    ok = win_ref[place, :own_rows] < 0.5 * INVALID
-    resid_ref[...] = jnp.where(ok, resid, lc_ref[...] + resid)
     total = jnp.sum(total, axis=1, keepdims=True)
     level = jnp.sum(level, axis=1, keepdims=True)
-    by_weight = dot(w_ref[...], basis_ref[...], NN)
-    width = by_weight.shape[1] // 4
-    by_value = dot(q_ref[...], basis_ref[:, : 2 * width], NN)
-    cosine = by_weight[:, :width]
-    sine = by_weight[:, width : 2 * width]
-    cosine_two = by_weight[:, 2 * width : 3 * width]
-    sine_two = by_weight[:, 3 * width :]
     inverse = 1.0 / total
     mean_level = level * inverse
-    ycos = by_value[:, :width] - mean_level * cosine
-    ysin = by_value[:, width:] - mean_level * sine
-    cc_term = 0.5 * (total + cosine_two) - cosine * cosine * inverse + RIDGE * total
-    ss_term = 0.5 * (total - cosine_two) - sine * sine * inverse + RIDGE * total
-    cs_term = 0.5 * sine_two - cosine * sine * inverse
-    determinant = cc_term * ss_term - cs_term * cs_term
-    power = (ss_term * ycos * ycos + cc_term * ysin * ysin - 2.0 * cs_term * ycos * ysin) / determinant
-    power_ref[...] = power.astype(BF16)
-
-
-def place_kernel(in_ref, out_ref):
-    width = in_ref.shape[2]
-    for b in range(in_ref.shape[0]):
-        out_ref[:, width * b : width * (b + 1)] = in_ref[b].astype(F32)
+    for c, basis_ref in enumerate(basis_refs):
+        width = basis_ref.shape[1] // 2
+        for copy in copies[PARTS * c : PARTS * (c + 1)] if c >= NEAR else ():
+            copy.wait()
+        single = jnp.zeros((2 * share, 2 * width), F32)
+        double_cos = [jnp.zeros((share, SLAB), F32) for _ in range(width // SLAB)]
+        double_sin = [jnp.zeros((share, SLAB), F32) for _ in range(width // SLAB)]
+        for k in range(basis_ref.shape[0] // SLAB):
+            at = slice(SLAB * k, SLAB * (k + 1))
+            single = single + dot(both_ref[:, at], basis_ref[at], NN)
+            for n in range(width // SLAB):
+                cos_b = basis_ref[at, SLAB * n : SLAB * (n + 1)].astype(F32)
+                sin_b = basis_ref[at, width + SLAB * n : width + SLAB * (n + 1)].astype(F32)
+                twice = sin_b + sin_b
+                cos_two = (1.0 - twice * sin_b).astype(BF16)
+                sin_two = (twice * cos_b).astype(BF16)
+                double_cos[n] = double_cos[n] + dot(both_ref[:share, at], cos_two, NN)
+                double_sin[n] = double_sin[n] + dot(both_ref[:share, at], sin_two, NN)
+        cosine = single[:share, :width]
+        sine = single[:share, width:]
+        cosine_two = jnp.concatenate(double_cos, axis=1)
+        sine_two = jnp.concatenate(double_sin, axis=1)
+        ycos = single[share:, :width] - mean_level * cosine
+        ysin = single[share:, width:] - mean_level * sine
+        cc_term = 0.5 * (total + cosine_two) - cosine * cosine * inverse + RIDGE * total
+        ss_term = 0.5 * (total - cosine_two) - sine * sine * inverse + RIDGE * total
+        cs_term = 0.5 * sine_two - cosine * sine * inverse
+        determinant = cc_term * ss_term - cs_term * cs_term
+        power = (ss_term * ycos * ycos + cc_term * ysin * ysin - 2.0 * cs_term * ycos * ysin) / determinant
+        power_ref[:, width * c : width * (c + 1)] = power
 
 
 def shaped(shape, dtype=F32):
@@ -454,28 +497,36 @@
         away=range(5),
         name="prep",
     )
+    jitter = epoch_jitter.reshape(ep_count, cols)
+    freqs = (freq_index + 1).astype(F32) / (4.0 * span)
+    width = freqs.shape[0] // CHUNKS
+    own, *pieces = lax.optimization_barrier(
+        (own, *[freqs[width * c : width * (c + 1)].reshape(1, width) for c in range(CHUNKS)])
+    )
+
+    def basis_of(piece, far):
+        scratch = [pltpu.VMEM((span, LANES), F32)]
+        if far:
+            scratch += [pltpu.VMEM((span, 2 * width), BF16), pltpu.SemaphoreType.DMA((ep_count,))]
+        out = pltpu.HBM((span, 2 * width), BF16) if far else shaped((span, 2 * width), BF16)
+        space = pltpu.HBM if far else pltpu.VMEM
+        return call(basis_kernel, out, (jitter, piece), scratch=scratch, out_space=space, name="basis")
+
     ring = [(i, (i + 1) % obj_count) for i in range(obj_count)]
     back = [(i, (i - 1) % obj_count) for i in range(obj_count)]
     left = lax.ppermute(tail, "obj", ring)
     right = lax.ppermute(head, "obj", back)
+    made = [basis_of(pieces.pop(0), c >= NEAR) for c in range(EARLY)]
+    left, right, *made = lax.optimization_barrier((left, right, *made))
     wide, meta = call(
         widen_kernel,
         (shaped((ep_count, 2 * rows + order, cols)), shaped((8, 2 * rows))),
         (own, tail, left, right),
         name="widen",
     )
-    width = freq_index.shape[0] // ep_count
-    freqs = (lax.dynamic_slice_in_dim(freq_index, place * width, width) + 1).astype(F32) / (4.0 * span)
-    wide, freqs = lax.optimization_barrier((wide, freqs))
+    wide, *pieces = lax.optimization_barrier((wide, *pieces))
     win = lax.all_to_all(wide, "ep", split_axis=0, concat_axis=0, tiled=True)
-    basis = call(
-        basis_kernel,
-        shaped((span, 4 * width), BF16),
-        (epoch_jitter.reshape(ep_count, cols), freqs.reshape(1, width)),
-        scratch=[pltpu.VMEM((span, LANES), F32)],
-        name="basis",
-    )
-    win, basis = lax.optimization_barrier((win, basis))
+    win, *basis = lax.optimization_barrier((win, *(made + [basis_of(p, True) for p in pieces])))
 
     window_rows = 2 * rows
     products = order * order * 3 // 4
@@ -513,23 +564,23 @@
         )
         lines = lax.all_to_all(lines, ("ep", "obj"), split_axis=0, concat_axis=0, tiled=True)
         args = (places, meta, win, lines.reshape(everyone, LANES), coef_t)
+    basis[NEAR:] = [pltpu.with_memory_space_constraint(b, pltpu.HBM) for b in basis[NEAR:]]
     residual, power = call(
         lambda *refs: final_kernel(*refs, group=group),
-        (shaped((rows, cols)), shaped((rows, width), BF16)),
-        (*args, basis, light_curves),
+        (shaped((rows, cols)), shaped((rows // ep_count, freqs.shape[0]))),
+        (*args, light_curves, *basis),
         scratch=[
             pltpu.VMEM((ep_count, rows, LANES), F32),
-            pltpu.VMEM((rows, span), BF16),
-            pltpu.VMEM((rows, span), BF16),
+            pltpu.VMEM((2, rows, LANES), F32),
+            pltpu.VMEM((2 * rows // ep_count, span), BF16),
+            *[pltpu.VMEM((span, 2 * width), BF16) for _ in range(NEAR, CHUNKS)],
+            pltpu.SemaphoreType.DMA((CHUNKS * PARTS,)),
         ],
         scalar=True,
+        away=range(len(args) + 1 + NEAR, len(args) + 1 + CHUNKS),
+        limit=32 << 20,
         name="spectrum",
     )
-    share = rows // ep_count
-    power = lax.all_to_all(
-        power.reshape(ep_count, share, width), "ep", split_axis=0, concat_axis=0, tiled=True
-    )
-    power = call(place_kernel, shaped((share, ep_count * width)), (power,), name="place")
     return residual, power
 
 

time: 124 us -> 120 us (0.968)
  Pallas kernels: 16.1 us -> 29 us
  waiting for transfers between devices: 12.9 us -> 1.57 us
  blocking collectives: 84 us -> 76.3 us
  local copies, waits for them, and re-layouts: 0.01 us -> 1.71 us
    pallas_call x9 -> x11, Pallas kernels: 16.1 us -> 29 us  [call(): pl.pallas_call(kernel, out_shape=out_shape, in_specs=specs, out_specs=out...]
    all_to_all x1 -> x0, blocking collectives: 8.05 us -> none  [per_device(): lax.all_to_all(power.reshape(ep_count, share, width), 'ep', split_axis=0,...]
    all_to_all x1, waiting for transfers between devices: 7.95 us -> 0.01 us  [per_device(): win = lax.all_to_all(wide, 'ep', split_axis=0, concat_axis=0, tiled=True)]
    ppermute x1, waiting for transfers between devices: 4.12 us -> 1.57 us  [per_device(): left = lax.ppermute(tail, 'obj', ring)]
    unnamed x4 -> x8, local copies, waits for them, and re-layouts: 0.01 us -> 1.71 us
  transfers between devices with their start and end apart: 3 -> 3, of which waited for: 3 -> 1; matrix products, arithmetic and copies ran while one was open for 1% -> 1% of each run, Pallas kernels for 1% -> 11%
where the time goes in v3:
time: 120 us; the launch traced here: 119 us
  blocking collectives  76.3 us (64%)
  Pallas kernels  29 us (24%)
  starting transfers between devices  9.19 us (8%)
  local copies, waits for them, and re-layouts  1.71 us (1%)
  waiting for transfers between devices  1.57 us (1%)
    all_to_all x2, blocking collectives, per_device(): lax.all_to_all(send.reshape(group, 8, LANES), 'obj', split_axis=0, concat...  40.5 us
    all_to_all x2, blocking collectives, per_device(): lax.all_to_all(lines, ('ep', 'obj'), split_axis=0, concat_axis=0, tiled=T...  35.7 us
    pallas_call x11, Pallas kernels, call(): pl.pallas_call(kernel, out_shape=out_shape, in_specs=specs, out_specs=out...  29 us
    all_to_all x1, starting transfers between devices, per_device(): win = lax.all_to_all(wide, 'ep', split_axis=0, concat_axis=0, tiled=True)  4.64 us
    ppermute x1, starting transfers between devices, per_device(): right = lax.ppermute(head, 'obj', back)  3.32 us
  transfers between devices with their start and end apart: 3, of which 1 were waited for; matrix products, arithmetic and copies ran while one was open for 1% of the time, Pallas kernels for 11%

profile of v3, /device:TPU:1, one launch (start us, length us, event | category | flops | bytes accessed | tf_op | source)
XLA Modules:
  0.0 119.3 jit_solution(6509038783351119407)
XLA Ops:
  0.6 0.9 prep.1
  1.6 3.3 %collective-permute-start.1 = (f32[72,128]{1,0:T(8,128)S(1)}, f32[72,128]{1,0:T(8,128)S(1)}, u32[]{:S(2)}, u32[]{:S(2)}) collective-permute-start(f32[72,128]{1,0:T(8,128)S(1)} %get-tuple-element.31), channel_id=1, source_target_pairs={{0,248},{8,0},{16,8},{24,16},{32,24},{40,32},{48,40},{56,48},{64,5... | collective-permute-start | bytes 110600 | tf_op jit(solution)/shard_map/ppermute | solution.py:518
  4.9 1.2 %collective-permute-start = (f32[72,128]{1,0:T(8,128)S(1)}, f32[72,128]{1,0:T(8,128)S(1)}, u32[]{:S(2)}, u32[]{:S(2)}) collective-permute-start(f32[72,128]{1,0:T(8,128)S(1)} %get-tuple-element.30.tail_ref), channel_id=1, source_target_pairs={{0,8},{8,16},{16,24},{24,32},{32,40},{40,48},{48,56},{56,64},{64,7... | collective-permute-start | bytes 110600 | tf_op jit(solution)/shard_map/ppermute | solution.py:517
  6.1 0.7 convert_multiply_fusion
  6.8 0.0 copy-start.2
  6.8 0.7 copy-done.2
  7.5 0.0 copy-start.3
  7.5 2.7 %basis.4.refs_6_ = bf16[1024,1024]{1,0:T(8,128)(2,1)S(1)} custom-call(f32[8,128]{1,0:T(8,128)S(1)} %bitcast.17, f32[1,512]{1,0:T(1,128)S(1)} %bitcast.24), custom_call_target="tpu_custom_call" | custom-call | tf_op jit(solution)/shard_map/basis/pallas_call | solution.py:468
  10.2 0.0 collective-permute-done.1.right_ref
  10.2 1.6 %collective-permute-done.left_ref = f32[72,128]{1,0:T(8,128)S(1)} collective-permute-done((f32[72,128]{1,0:T(8,128)S(1)}, f32[72,128]{1,0:T(8,128)S(1)}, u32[]{:S(2)}, u32[]{:S(2)}) %collective-permute-start) | collective-permute-done | bytes 36896 | tf_op jit(solution)/shard_map/ppermute | solution.py:517
  11.8 0.1 widen.1
  11.9 0.0 copy-start
  11.9 1.0 copy-done
  12.9 4.6 %all-to-all-start = ((f32[8,272,128]{2,1,0:T(8,128)}), f32[8,272,128]{2,1,0:T(8,128)S(1)}, u32[]{:S(2)}, u32[]{:S(2)}) async-start(f32[8,272,128]{2,1,0:T(8,128)} %copy-done), calls=%async_computation | async-start | bytes 2228224 | tf_op jit(solution)/shard_map/all_to_all | solution.py:528
  17.5 0.0 copy-done.3
  17.5 3.5 %basis.5.refs_7_ = bf16[1024,1024]{1,0:T(8,128)(2,1)} custom-call(f32[8,128]{1,0:T(8,128)S(1)} %bitcast.18, f32[1,512]{1,0:T(1,128)S(1)} %bitcast.23), custom_call_target="tpu_custom_call" | custom-call | tf_op jit(solution)/shard_map/basis/pallas_call | solution.py:468
  21.1 3.4 %basis.6.refs_8_ = bf16[1024,1024]{1,0:T(8,128)(2,1)} custom-call(f32[8,128]{1,0:T(8,128)S(1)} %bitcast.19, f32[1,512]{1,0:T(1,128)S(1)} %bitcast.22), custom_call_target="tpu_custom_call" | custom-call | tf_op jit(solution)/shard_map/basis/pallas_call | solution.py:468
  24.5 3.5 %basis.7.refs_9_ = bf16[1024,1024]{1,0:T(8,128)(2,1)} custom-call(f32[8,128]{1,0:T(8,128)S(1)} %bitcast.20, f32[1,512]{1,0:T(1,128)S(1)} %bitcast.21), custom_call_target="tpu_custom_call" | custom-call | tf_op jit(solution)/shard_map/basis/pallas_call | solution.py:468
  28.0 0.0 copy-start.1
  28.0 0.0 all-to-all-done.refs_2_
  28.0 3.8 %objects_0.1 = (f32[16,256]{1,0:T(8,128)S(1)}, f32[256,128]{1,0:T(8,128)S(1)}) custom-call(s32[1]{0:T(128)} %bitcast.refs_0_, f32[8,256]{1,0:T(8,128)S(1)} %get-tuple-element.35.refs_1_, f32[8,272,128]{2,1,0:T(8,128)S(1)} %all-to-all-done.refs_2_), custom_call_target="tpu_custom_call" | custom-call | tf_op jit(solution)/shard_map/objects_0/pallas_call | solution.py:468
  31.8 25.7 %all_to_all.25.a = f32[32,8,128]{2,1,0:T(8,128)S(1)} all-to-all(f32[32,8,128]{2,1,0:T(8,128)S(1)} %bitcast.16), channel_id=1, replica_groups=mesh['obj'=32,'ep'=8] {'obj'}, dimensions={0} | all-to-all | bytes 262144 | tf_op jit(solution)/shard_map/all_to_all | solution.py:556
  57.5 0.6 modes_0.1
  58.1 17.9 %all_to_all.26 = f32[256,1,128]{2,1,0:T(1,128)S(1)} all-to-all(f32[256,1,128]{2,1,0:T(1,128)S(1)} %modes_0.1), channel_id=1, replica_groups=mesh['obj'=32,'ep'=8] {'ep','obj'}, dimensions={0} | all-to-all | bytes 262144 | tf_op jit(solution)/shard_map/all_to_all | solution.py:565
  76.0 4.2 %objects_1.1 = (f32[16,256]{1,0:T(8,128)S(1)}, f32[256,128]{1,0:T(8,128)S(1)}) custom-call(s32[1]{0:T(128)} %bitcast.refs_0_, f32[8,256]{1,0:T(8,128)S(1)} %get-tuple-element.35.refs_1_, f32[8,272,128]{2,1,0:T(8,128)S(1)} %all-to-all-done.refs_2_, f32[256,128]{1,0:T(8,128)S(1)} %bitcast.14, f32[16,256]{1,0:T(8,128)S(1)} %get-tuple-element.47.refs_4_), custom_call_target="tpu_custom_call" | custom-call | tf_op jit(solution)/shard_map/objects_1/pallas_call | solution.py:468
  80.2 14.9 %all_to_all.27.a = f32[32,8,128]{2,1,0:T(8,128)S(1)} all-to-all(f32[32,8,128]{2,1,0:T(8,128)S(1)} %bitcast.15), channel_id=1, replica_groups=mesh['obj'=32,'ep'=8] {'obj'}, dimensions={0} | all-to-all | bytes 262144 | tf_op jit(solution)/shard_map/all_to_all | solution.py:556
  95.1 0.6 modes_1.1
  95.7 17.9 %all_to_all.28 = f32[256,1,128]{2,1,0:T(1,128)S(1)} all-to-all(f32[256,1,128]{2,1,0:T(1,128)S(1)} %modes_1.1), channel_id=1, replica_groups=mesh['obj'=32,'ep'=8] {'ep','obj'}, dimensions={0} | all-to-all | bytes 262144 | tf_op jit(solution)/shard_map/all_to_all | solution.py:565
  113.6 0.0 copy-done.1
  113.6 5.6 %spectrum.1 = (f32[128,128]{1,0:T(8,128)}, f32[16,2048]{1,0:T(8,128)}) custom-call(s32[1]{0:T(128)} %bitcast.refs_0_, f32[8,256]{1,0:T(8,128)S(1)} %get-tuple-element.35.refs_1_, f32[8,272,128]{2,1,0:T(8,128)S(1)} %all-to-all-done.refs_2_, f32[256,128]{1,0:T(8,128)S(1)} %bitcast.13, f32[16,256]{1,0:T(8,128)S(1)} %get-tuple-element.49.refs_4_, ...), custom_call_target="tpu_custom_call" | custom-call | tf_op jit(solution)/shard_map/spectrum/pallas_call | solution.py:468
  (1 shorter events, 0.0 us)
Async XLA Ops:
  1.6 8.6 %collective-permute-start.1 = (f32[72,128]{1,0:T(8,128)S(1)}, f32[72,128]{1,0:T(8,128)S(1)}, u32[]{:S(2)}, u32[]{:S(2)}) collective-permute-start(f32[72,128]{1,0:T(8,128)S(1)} %get-tuple-element.31), channel_id=1, source_target_pairs={{0,248},{8,0},{16,8},{24,16},{32,24},{40,32},{48,40},{56,48},{64,5... | collective-permute-start | bytes 110600 | tf_op jit(solution)/shard_map/ppermute | solution.py:518
  4.9 6.9 %collective-permute-start = (f32[72,128]{1,0:T(8,128)S(1)}, f32[72,128]{1,0:T(8,128)S(1)}, u32[]{:S(2)}, u32[]{:S(2)}) collective-permute-start(f32[72,128]{1,0:T(8,128)S(1)} %get-tuple-element.30.tail_ref), channel_id=1, source_target_pairs={{0,8},{8,16},{16,24},{24,32},{32,40},{40,48},{48,56},{56,64},{64,7... | collective-permute-start | bytes 110600 | tf_op jit(solution)/shard_map/ppermute | solution.py:517
  6.8 0.7 copy-start.2
  7.5 10.0 %copy-start.3 = (f32[1024]{0:T(1024)S(1)}, f32[1024]{0:T(1024)}, u32[]{:S(2)}) copy-start(f32[1024]{0:T(1024)} %param.12) | copy-start | bytes 12292
  11.9 1.0 copy-start
  12.9 15.1 %all-to-all-start = ((f32[8,272,128]{2,1,0:T(8,128)}), f32[8,272,128]{2,1,0:T(8,128)S(1)}, u32[]{:S(2)}, u32[]{:S(2)}) async-start(f32[8,272,128]{2,1,0:T(8,128)} %copy-done), calls=%async_computation | async-start | bytes 2228224 | tf_op jit(solution)/shard_map/all_to_all | solution.py:528
  28.0 85.6 %copy-start.1 = (f32[128,128]{1,0:T(8,128)S(1)}, f32[128,128]{1,0:T(8,128)}, u32[]{:S(2)}) copy-start(f32[128,128]{1,0:T(8,128)} %refs_5_.1) | copy-start | bytes 196612

commit v4 on v3

--- a/solution.py
+++ b/solution.py
@@ -17,7 +17,6 @@
 VMEM = 14 << 20
 CHUNKS = 4
 NEAR = 1
-EARLY = 1
 SLAB = 256
 PARTS = 4
 NEAREST = 1.5 * 2.0**23
@@ -121,10 +120,22 @@
     return same, turned[:, 1:2]
 
 
-def block_of(win_ref, b, own_rows, order):
-    coded = jnp.concatenate([win_ref[b, :own_rows], win_ref[b, own_rows + order :]], axis=0)
+def own_of(win_ref, b, rows):
+    coded = win_ref[b, :rows].astype(F32) + win_ref[b, rows : 2 * rows].astype(F32)
     ok = coded < 0.5 * INVALID
     return ok, jnp.where(ok, coded, 0.0)
+
+
+def block_of(win_ref, b, rows):
+    own = win_ref[b, :rows].astype(F32) + win_ref[b, rows : 2 * rows].astype(F32)
+    coded = jnp.concatenate([own, win_ref[b, 2 * rows : 3 * rows].astype(F32)], axis=0)
+    ok = coded < 0.5 * INVALID
+    return ok, jnp.where(ok, coded, 0.0)
+
+
+def first_modes(win_ref, b, rows, order):
+    parts = win_ref[b, 3 * rows :].astype(F32)
+    return parts[:order] + (parts[order : 2 * order] + parts[2 * order :])
 
 
 def pixel_total(same, part):
@@ -175,8 +186,8 @@
     rows = lc_ref.shape[0]
     half = rows // 2
     coded = jnp.where(valid_ref[...] != 0, lc_ref[...], INVALID)
-    own_ref[:rows] = coded
-    own_ref[rows:] = init_ref[...]
+    own_ref[:rows], own_ref[rows : 2 * rows] = split2(coded)
+    own_ref[2 * rows :] = jnp.concatenate(split3(init_ref[...]), axis=0).astype(BF16)
     meta = jnp.concatenate(
         [pix_ref[...].astype(F32), sig_ref[...], jnp.zeros((6, rows), F32)], axis=0
     )
@@ -186,21 +197,23 @@
     head_ref[half:] = meta
 
 
-def widen_kernel(own_ref, tail_ref, left_ref, right_ref, out_ref, meta_ref):
+def widen_kernel(own_ref, tail_ref, left_ref, right_ref, out_hbm, meta_ref, one_ref, sems):
     rows = tail_ref.shape[1]
     half = rows // 2
-    own = own_ref[...]
-    top = own.shape[0]
     left = left_ref[...]
     right = right_ref[...]
-    for b in range(out_ref.shape[0]):
-        out_ref[b, :top] = own
-        out_ref[b, top : top + half] = left[:half]
-        out_ref[b, top + half :] = right[:half]
+    one_ref[: 2 * rows] = own_ref[: 2 * rows]
+    one_ref[2 * rows : 3 * rows] = jnp.concatenate([left[:half], right[:half]], axis=0).astype(BF16)
+    one_ref[3 * rows :] = own_ref[2 * rows :]
+    copies = [pltpu.make_async_copy(one_ref, out_hbm.at[b], sems.at[b]) for b in range(out_hbm.shape[0])]
+    for copy in copies:
+        copy.start()
     lane = lax.broadcasted_iota(jnp.int32, (8, rows), 1)
     beyond = pltpu.roll(jnp.where(lane >= half, left[half:], right[half:]), half, 1)
     meta_ref[:, :rows] = tail_ref[half:]
     meta_ref[:, rows:] = beyond
+    for copy in copies:
+        copy.wait()
 
 
 def make_step_kernel(first):
@@ -219,14 +232,14 @@
         group = send_ref.shape[0] // 8
         same, sigma = window(meta_ref[...])
         if first:
-            modes = [win_ref[b, own_rows : own_rows + order] for b in range(blocks)]
+            modes = [first_modes(win_ref, b, own_rows, order) for b in range(blocks)]
         else:
             modes = natural_modes(arrived_ref[...], blocks, group, order)
             factors = coef_factors(before_ref[...])
         part = jnp.zeros((rows, LANES), F32)
         seen = jnp.zeros((rows, LANES), F32)
         for b in range(blocks):
-            ok, lc = block_of(win_ref, b, own_rows, order)
+            ok, lc = block_of(win_ref, b, own_rows)
             ms_ref[b] = mode_factors(modes[b])
             if not first:
                 lc = lc - dot(factors, ms_ref[b], NN)
@@ -237,7 +250,7 @@
         count = jnp.sum(dot(same, seen.astype(BF16), NN), axis=1, keepdims=True)
         edge = HUBER * spread_of(same, part, count)
         for b in range(blocks):
-            ok, lc = block_of(win_ref, b, own_rows, order)
+            ok, lc = block_of(win_ref, b, own_rows)
             weight = robust_weight(ok, scal_ref[b], edge, sigma)
             at = slice(LANES * b, LANES * (b + 1))
             wh_ref[:, at], wl_ref[:, at] = split2(weight)
@@ -259,15 +272,13 @@
         factors = coef_factors(coef_t)
         part = jnp.zeros((rows, LANES), F32)
         for b in range(blocks):
-            ok, lc = block_of(win_ref, b, own_rows, order)
+            ok, lc = block_of(win_ref, b, own_rows)
             scaled = (lc - dot(factors, ms_ref[b], NN)) * sigma
             scal_ref[b] = scaled
             part = part + jnp.where(ok, scaled * scaled, 0.0)
         edge = HUBER * spread_of(same, part, count)
         place = place_ref[0]
-        coded = win_ref[place, :own_rows]
-        ok = coded < 0.5 * INVALID
-        lc = jnp.where(ok, coded, 0.0)
+        ok, lc = own_of(win_ref, place, own_rows)
         weight = robust_weight(ok, scal_ref[place, :own_rows], edge[:own_rows], sigma[:own_rows])
         weight_hi, weight_lo = split2(weight)
         value_hi, value_lo = split2(weight * lc)
@@ -325,47 +336,50 @@
     return total
 
 
-def basis_kernel(jitter_ref, freq_ref, *rest):
-    (out_ref, time_ref), far = (rest, None) if len(rest) == 2 else ((rest[2], rest[1]), rest)
-    blocks, width = jitter_ref.shape[0], freq_ref.shape[1]
+def basis_kernel(jitter_ref, index_ref, *rest, pieces, far):
+    count = len(pieces)
+    time_ref = rest[count]
+    made = rest[count + 1 : 2 * count + 1] if far else rest[:count]
+    blocks, width = jitter_ref.shape[0], index_ref.shape[1]
+    freqs = (index_ref[...] + 1).astype(F32) / (4.0 * time_ref.shape[0])
     jitter = jnp.concatenate([jitter_ref[...], jnp.zeros((LANES - blocks, LANES), F32)], axis=0).T
     index = lax.broadcasted_iota(jnp.int32, (LANES, LANES), 0)
     for b in range(blocks):
         time_ref[LANES * b : LANES * (b + 1)] = (index + LANES * b).astype(F32) + jitter[:, b : b + 1]
     step = 32
 
-    def copy(b):
+    def copy(c, b):
         at = pl.ds(pl.multiple_of(LANES * b, LANES), LANES)
-        return pltpu.make_async_copy(out_ref.at[at], far[0].at[at], far[3].at[b])
-
-    def rows_from(i):
-        at = pl.ds(pl.multiple_of(step * i, step), step)
-        times = time_ref[at]
-        for c in range(width // LANES):
-            cycles = times * freq_ref[:, LANES * c : LANES * (c + 1)]
-            turn = cycles - ((cycles + NEAREST) - NEAREST)
-            square = turn * turn
-            sine = turn * horner(SINE, square)
-            cosine = horner(COSINE, square)
-            twice = sine + sine
-            start = LANES * c
-            out_ref[at, start : start + LANES] = (1.0 - twice * sine).astype(BF16)
-            out_ref[at, start + width : start + width + LANES] = (twice * cosine).astype(BF16)
+        return pltpu.make_async_copy(made[c].at[at], rest[c].at[at], rest[-1].at[c, b])
 
     @pl.loop(0, blocks)
     def _(b):
         @pl.loop(0, LANES // step)
         def _(i):
-            rows_from(b * (LANES // step) + i)
+            at = pl.ds(pl.multiple_of(LANES * b + step * i, step), step)
+            times = time_ref[at]
+            for c in range(count):
+                for n in range(width // LANES):
+                    cycles = times * freqs[pieces[c] : pieces[c] + 1, LANES * n : LANES * (n + 1)]
+                    turn = cycles - ((cycles + NEAREST) - NEAREST)
+                    square = turn * turn
+                    sine = turn * horner(SINE, square)
+                    cosine = horner(COSINE, square)
+                    twice = sine + sine
+                    start = LANES * n
+                    made[c][at, start : start + LANES] = (1.0 - twice * sine).astype(BF16)
+                    made[c][at, start + width : start + width + LANES] = (twice * cosine).astype(BF16)
 
         if far:
-            copy(b).start()
+            for c in range(count):
+                copy(c, b).start()
 
     if far:
 
         @pl.loop(0, blocks)
         def _(b):
-            copy(b).wait()
+            for c in range(count):
+                copy(c, b).wait()
 
 
 def final_kernel(place_ref, meta_ref, win_ref, arrived_ref, coef_ref, lc_ref, *rest, group):
@@ -389,7 +403,7 @@
     part = jnp.zeros((rows, LANES), F32)
     seen = jnp.zeros((rows, LANES), F32)
     for b in range(blocks):
-        ok, lc = block_of(win_ref, b, own_rows, order)
+        ok, lc = block_of(win_ref, b, own_rows)
         resid = lc - dot(factors, mode_factors(modes[b]), NN)
         res_ref[b] = resid[:own_rows]
         scaled = resid * sigma
@@ -400,16 +414,15 @@
     col_ref[0] = jnp.broadcast_to(edge[:own_rows], (own_rows, LANES))
     col_ref[1] = jnp.broadcast_to(sigma[:own_rows], (own_rows, LANES))
     place = place_ref[0]
-    ok = win_ref[place, :own_rows] < 0.5 * INVALID
-    resid = res_ref[place]
-    resid_ref[...] = jnp.where(ok, resid, lc_ref[...] + resid)
+    ok, lc = own_of(win_ref, place, own_rows)
+    resid_ref[...] = lc_ref[...] - (lc - res_ref[place])
     mine = pl.ds(pl.multiple_of(place * share, share), share)
     edge = col_ref[0, mine]
     sigma = col_ref[1, mine]
     total = jnp.zeros((share, LANES), F32)
     level = jnp.zeros((share, LANES), F32)
     for b in range(blocks):
-        ok = win_ref[b, mine] < 0.5 * INVALID
+        ok = win_ref[b, mine].astype(F32) < 0.5 * INVALID
         resid = res_ref[b, mine]
         weight = robust_weight(ok, resid * sigma, edge, sigma)
         at = slice(LANES * b, LANES * (b + 1))
@@ -464,7 +477,8 @@
     if scalar:
         specs[0] = pl.BlockSpec(memory_space=pltpu.SMEM)
     many = isinstance(out_shape, (tuple, list))
-    out_specs = [pl.BlockSpec(memory_space=out_space) for _ in (out_shape if many else [0])]
+    spaces = out_space if isinstance(out_space, (tuple, list)) else [out_space] * (len(out_shape) if many else 1)
+    out_specs = [pl.BlockSpec(memory_space=space) for space in spaces]
     return pl.pallas_call(
         kernel,
         out_shape=out_shape,
@@ -491,42 +505,49 @@
     fetched = tuple(pltpu.with_memory_space_constraint(a, pltpu.HBM) for a in fetched)
     own, tail, head = call(
         prep_kernel,
-        (shaped((rows + order, cols)), shaped((half + 8, cols)), shaped((half + 8, cols))),
+        (shaped((2 * rows + 3 * order, cols), BF16), shaped((half + 8, cols)), shaped((half + 8, cols))),
         fetched,
         scratch=[pltpu.VMEM(a.shape, a.dtype) for a in fetched] + [pltpu.SemaphoreType.DMA((5,))],
         away=range(5),
         name="prep",
     )
-    jitter = epoch_jitter.reshape(ep_count, cols)
-    freqs = (freq_index + 1).astype(F32) / (4.0 * span)
-    width = freqs.shape[0] // CHUNKS
-    own, *pieces = lax.optimization_barrier(
-        (own, *[freqs[width * c : width * (c + 1)].reshape(1, width) for c in range(CHUNKS)])
-    )
-
-    def basis_of(piece, far):
-        scratch = [pltpu.VMEM((span, LANES), F32)]
-        if far:
-            scratch += [pltpu.VMEM((span, 2 * width), BF16), pltpu.SemaphoreType.DMA((ep_count,))]
-        out = pltpu.HBM((span, 2 * width), BF16) if far else shaped((span, 2 * width), BF16)
-        space = pltpu.HBM if far else pltpu.VMEM
-        return call(basis_kernel, out, (jitter, piece), scratch=scratch, out_space=space, name="basis")
-
     ring = [(i, (i + 1) % obj_count) for i in range(obj_count)]
     back = [(i, (i - 1) % obj_count) for i in range(obj_count)]
     left = lax.ppermute(tail, "obj", ring)
     right = lax.ppermute(head, "obj", back)
-    made = [basis_of(pieces.pop(0), c >= NEAR) for c in range(EARLY)]
-    left, right, *made = lax.optimization_barrier((left, right, *made))
+    shape = (ep_count, 3 * (rows + order), cols)
     wide, meta = call(
         widen_kernel,
-        (shaped((ep_count, 2 * rows + order, cols)), shaped((8, 2 * rows))),
+        (pltpu.HBM(shape, BF16), shaped((8, 2 * rows))),
         (own, tail, left, right),
+        scratch=[pltpu.VMEM(shape[1:], BF16), pltpu.SemaphoreType.DMA((ep_count,))],
+        out_space=(pltpu.HBM, pltpu.VMEM),
         name="widen",
     )
-    wide, *pieces = lax.optimization_barrier((wide, *pieces))
+
+    width = freq_index.shape[0] // CHUNKS
+    jitter = epoch_jitter.reshape(ep_count, cols)
+
+    index = freq_index.reshape(CHUNKS, width)
+
+    def basis_of(index, pieces, far):
+        scratch = [pltpu.VMEM((span, LANES), F32)]
+        if far:
+            scratch += [pltpu.VMEM((span, 2 * width), BF16) for _ in pieces]
+            scratch += [pltpu.SemaphoreType.DMA((len(pieces), ep_count))]
+        place_of = pltpu.HBM if far else shaped
+        return call(
+            lambda *refs: basis_kernel(*refs, pieces=pieces, far=far),
+            [place_of((span, 2 * width), BF16) for _ in pieces],
+            (jitter, index),
+            scratch=scratch,
+            out_space=[pltpu.HBM if far else pltpu.VMEM] * len(pieces),
+            name="basis",
+        )
+
+    wide, index = lax.optimization_barrier((wide, index))
     win = lax.all_to_all(wide, "ep", split_axis=0, concat_axis=0, tiled=True)
-    win, *basis = lax.optimization_barrier((win, *(made + [basis_of(p, True) for p in pieces])))
+    win, *basis = lax.optimization_barrier((win, *basis_of(index, range(NEAR, CHUNKS), True)))
 
     window_rows = 2 * rows
     products = order * order * 3 // 4
@@ -562,12 +583,17 @@
             (arrived,),
             name=f"modes_{iteration}",
         )
+        if iteration == 0:
+            lines, index = lax.optimization_barrier((lines, index))
         lines = lax.all_to_all(lines, ("ep", "obj"), split_axis=0, concat_axis=0, tiled=True)
+        if iteration == 0:
+            lines, *close = lax.optimization_barrier((lines, *basis_of(index, range(NEAR), False)))
+            basis = close + basis
         args = (places, meta, win, lines.reshape(everyone, LANES), coef_t)
     basis[NEAR:] = [pltpu.with_memory_space_constraint(b, pltpu.HBM) for b in basis[NEAR:]]
     residual, power = call(
         lambda *refs: final_kernel(*refs, group=group),
-        (shaped((rows, cols)), shaped((rows // ep_count, freqs.shape[0]))),
+        (shaped((rows, cols)), shaped((rows // ep_count, freq_index.shape[0]))),
         (*args, light_curves, *basis),
         scratch=[
             pltpu.VMEM((ep_count, rows, LANES), F32),

time: 120 us -> 118 us (0.983)
  blocking collectives: 76.3 us -> 56.4 us
  waiting for transfers between devices: 1.57 us -> 16.1 us
  starting transfers between devices: 9.19 us -> 14.6 us
    all_to_all x2 -> x1, blocking collectives: 35.7 us -> 17.9 us  [per_device(): lax.all_to_all(lines, ('ep', 'obj'), split_axis=0, concat_axis=0, tiled=T...]
    all_to_all x0 -> x1, waiting for transfers between devices: none -> 10.2 us  [per_device(): lax.all_to_all(lines, ('ep', 'obj'), split_axis=0, concat_axis=0, tiled=T...]
    all_to_all x0 -> x1, starting transfers between devices: none -> 5.38 us  [per_device(): lax.all_to_all(lines, ('ep', 'obj'), split_axis=0, concat_axis=0, tiled=T...]
    ppermute x1, waiting for transfers between devices: 1.57 us -> 4.12 us  [per_device(): left = lax.ppermute(tail, 'obj', ring)]
    all_to_all x2, blocking collectives: 40.5 us -> 38.5 us  [per_device(): lax.all_to_all(send.reshape(group, 8, LANES), 'obj', split_axis=0, concat...]
    unnamed x8 -> x4, local copies, waits for them, and re-layouts: 1.71 us -> 0.01 us
    pallas_call x11 -> x9, Pallas kernels: 29 us -> 28.6 us  [call(): pl.pallas_call(kernel, out_shape=out_shape, in_specs=specs, out_specs=out...]
  transfers between devices with their start and end apart: 3 -> 4, of which waited for: 1 -> 4; matrix products, arithmetic and copies ran while one was open for 1% -> 1% of each run, Pallas kernels for 11% -> 9%
where the time goes in v4:
time: 118 us; the launch traced here: 117 us
  blocking collectives  56.4 us (48%)
  Pallas kernels  28.6 us (24%)
  waiting for transfers between devices  16.1 us (14%)
  starting transfers between devices  14.6 us (12%)
    all_to_all x2, blocking collectives, per_device(): lax.all_to_all(send.reshape(group, 8, LANES), 'obj', split_axis=0, concat...  38.5 us
    pallas_call x9, Pallas kernels, call(): pl.pallas_call(kernel, out_shape=out_shape, in_specs=specs, out_specs=out...  28.6 us
    all_to_all x1, blocking collectives, per_device(): lax.all_to_all(lines, ('ep', 'obj'), split_axis=0, concat_axis=0, tiled=T...  17.9 us
    all_to_all x1, waiting for transfers between devices, per_device(): lax.all_to_all(lines, ('ep', 'obj'), split_axis=0, concat_axis=0, tiled=T...  10.2 us
    all_to_all x1, starting transfers between devices, per_device(): lax.all_to_all(lines, ('ep', 'obj'), split_axis=0, concat_axis=0, tiled=T...  5.38 us
    all_to_all x1, starting transfers between devices, per_device(): win = lax.all_to_all(wide, 'ep', split_axis=0, concat_axis=0, tiled=True)  4.66 us
    ppermute x1, waiting for transfers between devices, per_device(): left = lax.ppermute(tail, 'obj', ring)  4.12 us
    ppermute x1, starting transfers between devices, per_device(): right = lax.ppermute(head, 'obj', back)  3.32 us
  transfers between devices with their start and end apart: 4, of which 4 were waited for; matrix products, arithmetic and copies ran while one was open for 1% of the time, Pallas kernels for 9%

profile of v4, /device:TPU:1, one launch (start us, length us, event | category | flops | bytes accessed | tf_op | source)
XLA Modules:
  0.0 117.2 jit_solution(2615139931636730422)
XLA Ops:
  0.6 0.0 copy-start.1
  0.6 0.9 prep.1
  1.6 3.3 %collective-permute-start.1 = (f32[72,128]{1,0:T(8,128)S(1)}, f32[72,128]{1,0:T(8,128)S(1)}, u32[]{:S(2)}, u32[]{:S(2)}) collective-permute-start(f32[72,128]{1,0:T(8,128)S(1)} %get-tuple-element.26), channel_id=1, source_target_pairs={{0,248},{8,0},{16,8},{24,16},{32,24},{40,32},{48,40},{56,48},{64,5... | collective-permute-start | bytes 110600 | tf_op jit(solution)/shard_map/ppermute | solution.py:517
  4.9 1.2 %collective-permute-start = (f32[72,128]{1,0:T(8,128)S(1)}, f32[72,128]{1,0:T(8,128)S(1)}, u32[]{:S(2)}, u32[]{:S(2)}) collective-permute-start(f32[72,128]{1,0:T(8,128)S(1)} %get-tuple-element.25.tail_ref), channel_id=1, source_target_pairs={{0,8},{8,16},{16,24},{24,32},{32,40},{40,48},{48,56},{56,64},{64,7... | collective-permute-start | bytes 110600 | tf_op jit(solution)/shard_map/ppermute | solution.py:516
  6.1 0.7 reshape.34.refs_1_
  6.8 0.8 collective-permute-done.1.right_ref
  7.7 4.1 %collective-permute-done.left_ref = f32[72,128]{1,0:T(8,128)S(1)} collective-permute-done((f32[72,128]{1,0:T(8,128)S(1)}, f32[72,128]{1,0:T(8,128)S(1)}, u32[]{:S(2)}, u32[]{:S(2)}) %collective-permute-start) | collective-permute-done | bytes 36896 | tf_op jit(solution)/shard_map/ppermute | solution.py:516
  11.8 1.0 widen.1
  12.9 4.7 %all-to-all-start = ((bf16[8,432,128]{2,1,0:T(8,128)(2,1)}), bf16[8,432,128]{2,1,0:T(8,128)(2,1)S(1)}, u32[]{:S(2)}, u32[]{:S(2)}) async-start(bf16[8,432,128]{2,1,0:T(8,128)(2,1)} %get-tuple-element.29), calls=%async_computation | async-start | bytes 1769472 | tf_op jit(solution)/shard_map/all_to_all | solution.py:549
  17.5 0.0 copy-done.1
  17.5 7.8 %basis.2 = (bf16[1024,1024]{1,0:T(8,128)(2,1)}, bf16[1024,1024]{1,0:T(8,128)(2,1)}, bf16[1024,1024]{1,0:T(8,128)(2,1)}) custom-call(f32[8,128]{1,0:T(8,128)S(1)} %bitcast.13, s32[4,512]{1,0:T(4,128)S(1)} %reshape.34.refs_1_), custom_call_target="tpu_custom_call" | custom-call | tf_op jit(solution)/shard_map/basis/pallas_call | solution.py:482
  25.3 0.9 all-to-all-done.refs_2_
  26.2 4.0 %objects_0.1 = (f32[16,256]{1,0:T(8,128)S(1)}, f32[256,128]{1,0:T(8,128)S(1)}) custom-call(s32[1]{0:T(128)} %bitcast.refs_0_, f32[8,256]{1,0:T(8,128)S(1)} %get-tuple-element.27.refs_1_, bf16[8,432,128]{2,1,0:T(8,128)(2,1)S(1)} %all-to-all-done.refs_2_), custom_call_target="tpu_custom_call" | custom-call | tf_op jit(solution)/shard_map/objects_0/pallas_call | solution.py:482
  30.2 23.7 %all_to_all.25.a = f32[32,8,128]{2,1,0:T(8,128)S(1)} all-to-all(f32[32,8,128]{2,1,0:T(8,128)S(1)} %bitcast.12), channel_id=1, replica_groups=mesh['obj'=32,'ep'=8] {'obj'}, dimensions={0} | all-to-all | bytes 262144 | tf_op jit(solution)/shard_map/all_to_all | solution.py:577
  53.9 1.3 %modes_0.1 = f32[256,1,128]{2,1,0:T(1,128)} custom-call(f32[32,8,128]{2,1,0:T(8,128)S(1)} %all_to_all.25.a), custom_call_target="tpu_custom_call" | custom-call | tf_op jit(solution)/shard_map/modes_0/pallas_call | solution.py:482
  55.2 0.0 copy-start
  55.2 5.4 %all-to-all-start.2 = ((f32[256,1,128]{2,1,0:T(1,128)}), f32[256,1,128]{2,1,0:T(1,128)S(1)}, u32[]{:S(2)}, u32[]{:S(2)}) async-start(f32[256,1,128]{2,1,0:T(1,128)} %modes_0.1), calls=%async_computation.2 | async-start | bytes 262144 | tf_op jit(solution)/shard_map/all_to_all | solution.py:588
  60.6 2.7 %basis.3.refs_6_ = bf16[1024,1024]{1,0:T(8,128)(2,1)S(1)} custom-call(f32[8,128]{1,0:T(8,128)S(1)} %bitcast.14, s32[4,512]{1,0:T(4,128)S(1)} %reshape.34.refs_1_), custom_call_target="tpu_custom_call" | custom-call | tf_op jit(solution)/shard_map/basis/pallas_call | solution.py:482
  63.3 10.2 %all-to-all-done.2 = f32[256,1,128]{2,1,0:T(1,128)S(1)} async-done(((f32[256,1,128]{2,1,0:T(1,128)}), f32[256,1,128]{2,1,0:T(1,128)S(1)}, u32[]{:S(2)}, u32[]{:S(2)}) %all-to-all-start.2) | async-done | bytes 131104 | tf_op jit(solution)/shard_map/all_to_all | solution.py:588
  73.5 4.4 %objects_1.1 = (f32[16,256]{1,0:T(8,128)S(1)}, f32[256,128]{1,0:T(8,128)S(1)}) custom-call(s32[1]{0:T(128)} %bitcast.refs_0_, f32[8,256]{1,0:T(8,128)S(1)} %get-tuple-element.27.refs_1_, bf16[8,432,128]{2,1,0:T(8,128)(2,1)S(1)} %all-to-all-done.refs_2_, f32[256,128]{1,0:T(8,128)S(1)} %bitcast.10, f32[16,256]{1,0:T(8,128)S(1)} %get-tuple-element.39.refs_4_), custom_call_target="tpu_custom_call" | custom-call | tf_op jit(solution)/shard_map/objects_1/pallas_call | solution.py:482
  77.9 14.8 %all_to_all.26.a = f32[32,8,128]{2,1,0:T(8,128)S(1)} all-to-all(f32[32,8,128]{2,1,0:T(8,128)S(1)} %bitcast.11), channel_id=1, replica_groups=mesh['obj'=32,'ep'=8] {'obj'}, dimensions={0} | all-to-all | bytes 262144 | tf_op jit(solution)/shard_map/all_to_all | solution.py:577
  92.7 0.6 modes_1.1
  93.4 17.9 %all_to_all.27 = f32[256,1,128]{2,1,0:T(1,128)S(1)} all-to-all(f32[256,1,128]{2,1,0:T(1,128)S(1)} %modes_1.1), channel_id=1, replica_groups=mesh['obj'=32,'ep'=8] {'ep','obj'}, dimensions={0} | all-to-all | bytes 262144 | tf_op jit(solution)/shard_map/all_to_all | solution.py:588
  111.2 0.0 copy-done
  111.2 5.8 %spectrum.1 = (f32[128,128]{1,0:T(8,128)}, f32[16,2048]{1,0:T(8,128)}) custom-call(s32[1]{0:T(128)} %bitcast.refs_0_, f32[8,256]{1,0:T(8,128)S(1)} %get-tuple-element.27.refs_1_, bf16[8,432,128]{2,1,0:T(8,128)(2,1)S(1)} %all-to-all-done.refs_2_, f32[256,128]{1,0:T(8,128)S(1)} %bitcast.9, f32[16,256]{1,0:T(8,128)S(1)} %get-tuple-element.41.refs_4_, ...), custom_call_target="tpu_custom_call" | custom-call | tf_op jit(solution)/shard_map/spectrum/pallas_call | solution.py:482
Async XLA Ops:
  0.6 16.9 %copy-start.1 = (f32[1024]{0:T(1024)S(1)}, f32[1024]{0:T(1024)}, u32[]{:S(2)}) copy-start(f32[1024]{0:T(1024)} %param.12) | copy-start | bytes 12292
  1.6 6.1 %collective-permute-start.1 = (f32[72,128]{1,0:T(8,128)S(1)}, f32[72,128]{1,0:T(8,128)S(1)}, u32[]{:S(2)}, u32[]{:S(2)}) collective-permute-start(f32[72,128]{1,0:T(8,128)S(1)} %get-tuple-element.26), channel_id=1, source_target_pairs={{0,248},{8,0},{16,8},{24,16},{32,24},{40,32},{48,40},{56,48},{64,5... | collective-permute-start | bytes 110600 | tf_op jit(solution)/shard_map/ppermute | solution.py:517
  4.9 6.9 %collective-permute-start = (f32[72,128]{1,0:T(8,128)S(1)}, f32[72,128]{1,0:T(8,128)S(1)}, u32[]{:S(2)}, u32[]{:S(2)}) collective-permute-start(f32[72,128]{1,0:T(8,128)S(1)} %get-tuple-element.25.tail_ref), channel_id=1, source_target_pairs={{0,8},{8,16},{16,24},{24,32},{32,40},{40,48},{48,56},{56,64},{64,7... | collective-permute-start | bytes 110600 | tf_op jit(solution)/shard_map/ppermute | solution.py:516
  12.9 13.4 %all-to-all-start = ((bf16[8,432,128]{2,1,0:T(8,128)(2,1)}), bf16[8,432,128]{2,1,0:T(8,128)(2,1)S(1)}, u32[]{:S(2)}, u32[]{:S(2)}) async-start(bf16[8,432,128]{2,1,0:T(8,128)(2,1)} %get-tuple-element.29), calls=%async_computation | async-start | bytes 1769472 | tf_op jit(solution)/shard_map/all_to_all | solution.py:549
  55.2 56.1 %copy-start = (f32[128,128]{1,0:T(8,128)S(1)}, f32[128,128]{1,0:T(8,128)}, u32[]{:S(2)}) copy-start(f32[128,128]{1,0:T(8,128)} %refs_5_.1) | copy-start | bytes 196612
  55.2 18.3 %all-to-all-start.2 = ((f32[256,1,128]{2,1,0:T(1,128)}), f32[256,1,128]{2,1,0:T(1,128)S(1)}, u32[]{:S(2)}, u32[]{:S(2)}) async-start(f32[256,1,128]{2,1,0:T(1,128)} %modes_0.1), calls=%async_computation.2 | async-start | bytes 262144 | tf_op jit(solution)/shard_map/all_to_all | solution.py:588

commit v5 on v4

--- a/solution.py
+++ b/solution.py
@@ -340,7 +340,8 @@
     count = len(pieces)
     time_ref = rest[count]
     made = rest[count + 1 : 2 * count + 1] if far else rest[:count]
-    blocks, width = jitter_ref.shape[0], index_ref.shape[1]
+    blocks, width = jitter_ref.shape[0], made[0].shape[1] // 2
+    tiles = width // LANES
     freqs = (index_ref[...] + 1).astype(F32) / (4.0 * time_ref.shape[0])
     jitter = jnp.concatenate([jitter_ref[...], jnp.zeros((LANES - blocks, LANES), F32)], axis=0).T
     index = lax.broadcasted_iota(jnp.int32, (LANES, LANES), 0)
@@ -359,8 +360,9 @@
             at = pl.ds(pl.multiple_of(LANES * b + step * i, step), step)
             times = time_ref[at]
             for c in range(count):
-                for n in range(width // LANES):
-                    cycles = times * freqs[pieces[c] : pieces[c] + 1, LANES * n : LANES * (n + 1)]
+                for n in range(tiles):
+                    line = pieces[c] * tiles + n
+                    cycles = times * freqs[line : line + 1]
                     turn = cycles - ((cycles + NEAREST) - NEAREST)
                     square = turn * turn
                     sine = turn * horner(SINE, square)
@@ -447,11 +449,11 @@
             at = slice(SLAB * k, SLAB * (k + 1))
             single = single + dot(both_ref[:, at], basis_ref[at], NN)
             for n in range(width // SLAB):
-                cos_b = basis_ref[at, SLAB * n : SLAB * (n + 1)].astype(F32)
-                sin_b = basis_ref[at, width + SLAB * n : width + SLAB * (n + 1)].astype(F32)
+                cos_b = basis_ref[at, SLAB * n : SLAB * (n + 1)]
+                sin_b = basis_ref[at, width + SLAB * n : width + SLAB * (n + 1)]
                 twice = sin_b + sin_b
-                cos_two = (1.0 - twice * sin_b).astype(BF16)
-                sin_two = (twice * cos_b).astype(BF16)
+                cos_two = 1.0 - twice * sin_b
+                sin_two = twice * cos_b
                 double_cos[n] = double_cos[n] + dot(both_ref[:share, at], cos_two, NN)
                 double_sin[n] = double_sin[n] + dot(both_ref[:share, at], sin_two, NN)
         cosine = single[:share, :width]
@@ -528,7 +530,7 @@
     width = freq_index.shape[0] // CHUNKS
     jitter = epoch_jitter.reshape(ep_count, cols)
 
-    index = freq_index.reshape(CHUNKS, width)
+    index = freq_index.reshape(-1, LANES)
 
     def basis_of(index, pieces, far):
         scratch = [pltpu.VMEM((span, LANES), F32)]

time: 118 us -> 117 us (level)
  transfers between devices with their start and end apart: 4 -> 4, of which waited for: 4 -> 4; matrix products, arithmetic and copies ran while one was open for 1% -> 0% of each run, Pallas kernels for 9% -> 9%
where the time goes in v5:
time: 117 us
  blocking collectives  56.4 us (48%)
  Pallas kernels  28.3 us (24%)
  waiting for transfers between devices  16.8 us (14%)
  starting transfers between devices  14.5 us (12%)
    all_to_all x2, blocking collectives, per_device(): lax.all_to_all(send.reshape(group, 8, LANES), 'obj', split_axis=0, concat...  38.5 us
    pallas_call x9, Pallas kernels, call(): pl.pallas_call(kernel, out_shape=out_shape, in_specs=specs, out_specs=out...  28.3 us
    all_to_all x1, blocking collectives, per_device(): lax.all_to_all(lines, ('ep', 'obj'), split_axis=0, concat_axis=0, tiled=T...  17.9 us
    all_to_all x1, waiting for transfers between devices, per_device(): lax.all_to_all(lines, ('ep', 'obj'), split_axis=0, concat_axis=0, tiled=T...  10.2 us
    all_to_all x1, starting transfers between devices, per_device(): lax.all_to_all(lines, ('ep', 'obj'), split_axis=0, concat_axis=0, tiled=T...  5.3 us
    all_to_all x1, starting transfers between devices, per_device(): win = lax.all_to_all(wide, 'ep', split_axis=0, concat_axis=0, tiled=True)  4.66 us
    ppermute x1, waiting for transfers between devices, per_device(): left = lax.ppermute(tail, 'obj', ring)  4.12 us
    ppermute x1, starting transfers between devices, per_device(): right = lax.ppermute(head, 'obj', back)  3.32 us
  transfers between devices with their start and end apart: 4, of which 4 were waited for; matrix products, arithmetic and copies ran while one was open for 0% of the time, Pallas kernels for 9%

profile of v5, /device:TPU:1, one launch (start us, length us, event | category | flops | bytes accessed | tf_op | source)
XLA Modules:
  0.0 116.8 jit_solution(2496872685989463439)
XLA Ops:
  0.6 0.0 copy-start.1
  0.6 0.0 copy-start.2
  0.7 0.9 prep.1
  1.6 3.3 %collective-permute-start.1 = (f32[72,128]{1,0:T(8,128)S(1)}, f32[72,128]{1,0:T(8,128)S(1)}, u32[]{:S(2)}, u32[]{:S(2)}) collective-permute-start(f32[72,128]{1,0:T(8,128)S(1)} %get-tuple-element.26), channel_id=1, source_target_pairs={{0,248},{8,0},{16,8},{24,16},{32,24},{40,32},{48,40},{56,48},{64,5... | collective-permute-start | bytes 110600 | tf_op jit(solution)/shard_map/ppermute | solution.py:519
  4.9 1.2 %collective-permute-start = (f32[72,128]{1,0:T(8,128)S(1)}, f32[72,128]{1,0:T(8,128)S(1)}, u32[]{:S(2)}, u32[]{:S(2)}) collective-permute-start(f32[72,128]{1,0:T(8,128)S(1)} %get-tuple-element.25.tail_ref), channel_id=1, source_target_pairs={{0,8},{8,16},{16,24},{24,32},{32,40},{40,48},{48,56},{56,64},{64,7... | collective-permute-start | bytes 110600 | tf_op jit(solution)/shard_map/ppermute | solution.py:518
  6.2 1.6 %collective-permute-done.1.right_ref = f32[72,128]{1,0:T(8,128)S(1)} collective-permute-done((f32[72,128]{1,0:T(8,128)S(1)}, f32[72,128]{1,0:T(8,128)S(1)}, u32[]{:S(2)}, u32[]{:S(2)}) %collective-permute-start.1) | collective-permute-done | bytes 36896 | tf_op jit(solution)/shard_map/ppermute | solution.py:519
  7.7 4.1 %collective-permute-done.left_ref = f32[72,128]{1,0:T(8,128)S(1)} collective-permute-done((f32[72,128]{1,0:T(8,128)S(1)}, f32[72,128]{1,0:T(8,128)S(1)}, u32[]{:S(2)}, u32[]{:S(2)}) %collective-permute-start) | collective-permute-done | bytes 36896 | tf_op jit(solution)/shard_map/ppermute | solution.py:518
  11.8 1.0 widen.1
  12.9 4.7 %all-to-all-start = ((bf16[8,432,128]{2,1,0:T(8,128)(2,1)}), bf16[8,432,128]{2,1,0:T(8,128)(2,1)S(1)}, u32[]{:S(2)}, u32[]{:S(2)}) async-start(bf16[8,432,128]{2,1,0:T(8,128)(2,1)} %get-tuple-element.29), calls=%async_computation | async-start | bytes 1769472 | tf_op jit(solution)/shard_map/all_to_all | solution.py:551
  17.5 0.0 copy-done.1
  17.5 0.0 copy-done.2
  17.5 7.8 %basis.2 = (bf16[1024,1024]{1,0:T(8,128)(2,1)}, bf16[1024,1024]{1,0:T(8,128)(2,1)}, bf16[1024,1024]{1,0:T(8,128)(2,1)}) custom-call(f32[8,128]{1,0:T(8,128)S(1)} %bitcast.16, s32[16,128]{1,0:T(8,128)S(1)} %bitcast.14), custom_call_target="tpu_custom_call" | custom-call | tf_op jit(solution)/shard_map/basis/pallas_call | solution.py:484
  25.4 0.9 all-to-all-done.refs_2_
  26.3 4.0 %objects_0.1 = (f32[16,256]{1,0:T(8,128)S(1)}, f32[256,128]{1,0:T(8,128)S(1)}) custom-call(s32[1]{0:T(128)} %bitcast.refs_0_, f32[8,256]{1,0:T(8,128)S(1)} %get-tuple-element.27.refs_1_, bf16[8,432,128]{2,1,0:T(8,128)(2,1)S(1)} %all-to-all-done.refs_2_), custom_call_target="tpu_custom_call" | custom-call | tf_op jit(solution)/shard_map/objects_0/pallas_call | solution.py:484
  30.2 23.7 %all_to_all.25.a = f32[32,8,128]{2,1,0:T(8,128)S(1)} all-to-all(f32[32,8,128]{2,1,0:T(8,128)S(1)} %bitcast.13), channel_id=1, replica_groups=mesh['obj'=32,'ep'=8] {'obj'}, dimensions={0} | all-to-all | bytes 262144 | tf_op jit(solution)/shard_map/all_to_all | solution.py:579
  53.9 1.3 %modes_0.1 = f32[256,1,128]{2,1,0:T(1,128)} custom-call(f32[32,8,128]{2,1,0:T(8,128)S(1)} %all_to_all.25.a), custom_call_target="tpu_custom_call" | custom-call | tf_op jit(solution)/shard_map/modes_0/pallas_call | solution.py:484
  55.2 0.0 copy-start
  55.2 5.3 %all-to-all-start.2 = ((f32[256,1,128]{2,1,0:T(1,128)}), f32[256,1,128]{2,1,0:T(1,128)S(1)}, u32[]{:S(2)}, u32[]{:S(2)}) async-start(f32[256,1,128]{2,1,0:T(1,128)} %modes_0.1), calls=%async_computation.2 | async-start | bytes 262144 | tf_op jit(solution)/shard_map/all_to_all | solution.py:590
  60.5 2.7 %basis.3.refs_6_ = bf16[1024,1024]{1,0:T(8,128)(2,1)S(1)} custom-call(f32[8,128]{1,0:T(8,128)S(1)} %bitcast.17, s32[16,128]{1,0:T(8,128)S(1)} %bitcast.15), custom_call_target="tpu_custom_call" | custom-call | tf_op jit(solution)/shard_map/basis/pallas_call | solution.py:484
  63.3 10.2 %all-to-all-done.2 = f32[256,1,128]{2,1,0:T(1,128)S(1)} async-done(((f32[256,1,128]{2,1,0:T(1,128)}), f32[256,1,128]{2,1,0:T(1,128)S(1)}, u32[]{:S(2)}, u32[]{:S(2)}) %all-to-all-start.2) | async-done | bytes 131104 | tf_op jit(solution)/shard_map/all_to_all | solution.py:590
  73.5 4.4 %objects_1.1 = (f32[16,256]{1,0:T(8,128)S(1)}, f32[256,128]{1,0:T(8,128)S(1)}) custom-call(s32[1]{0:T(128)} %bitcast.refs_0_, f32[8,256]{1,0:T(8,128)S(1)} %get-tuple-element.27.refs_1_, bf16[8,432,128]{2,1,0:T(8,128)(2,1)S(1)} %all-to-all-done.refs_2_, f32[256,128]{1,0:T(8,128)S(1)} %bitcast.11, f32[16,256]{1,0:T(8,128)S(1)} %get-tuple-element.39.refs_4_), custom_call_target="tpu_custom_call" | custom-call | tf_op jit(solution)/shard_map/objects_1/pallas_call | solution.py:484
  77.8 14.8 %all_to_all.26.a = f32[32,8,128]{2,1,0:T(8,128)S(1)} all-to-all(f32[32,8,128]{2,1,0:T(8,128)S(1)} %bitcast.12), channel_id=1, replica_groups=mesh['obj'=32,'ep'=8] {'obj'}, dimensions={0} | all-to-all | bytes 262144 | tf_op jit(solution)/shard_map/all_to_all | solution.py:579
  92.7 0.6 modes_1.1
  93.3 17.9 %all_to_all.27 = f32[256,1,128]{2,1,0:T(1,128)S(1)} all-to-all(f32[256,1,128]{2,1,0:T(1,128)S(1)} %modes_1.1), channel_id=1, replica_groups=mesh['obj'=32,'ep'=8] {'ep','obj'}, dimensions={0} | all-to-all | bytes 262144 | tf_op jit(solution)/shard_map/all_to_all | solution.py:590
  111.2 0.0 copy-done
  111.2 5.5 %spectrum.1 = (f32[128,128]{1,0:T(8,128)}, f32[16,2048]{1,0:T(8,128)}) custom-call(s32[1]{0:T(128)} %bitcast.refs_0_, f32[8,256]{1,0:T(8,128)S(1)} %get-tuple-element.27.refs_1_, bf16[8,432,128]{2,1,0:T(8,128)(2,1)S(1)} %all-to-all-done.refs_2_, f32[256,128]{1,0:T(8,128)S(1)} %bitcast.10, f32[16,256]{1,0:T(8,128)S(1)} %get-tuple-element.41.refs_4_, ...), custom_call_target="tpu_custom_call" | custom-call | tf_op jit(solution)/shard_map/spectrum/pallas_call | solution.py:484
Async XLA Ops:
  0.6 16.9 %copy-start.1 = (s32[2048]{0:T(1024)S(1)}, s32[2048]{0:T(1024)}, u32[]{:S(2)}) copy-start(s32[2048]{0:T(1024)} %param.13) | copy-start | bytes 24580
  0.6 16.9 %copy-start.2 = (f32[1024]{0:T(1024)S(1)}, f32[1024]{0:T(1024)}, u32[]{:S(2)}) copy-start(f32[1024]{0:T(1024)} %param.12) | copy-start | bytes 12292
  1.6 6.1 %collective-permute-start.1 = (f32[72,128]{1,0:T(8,128)S(1)}, f32[72,128]{1,0:T(8,128)S(1)}, u32[]{:S(2)}, u32[]{:S(2)}) collective-permute-start(f32[72,128]{1,0:T(8,128)S(1)} %get-tuple-element.26), channel_id=1, source_target_pairs={{0,248},{8,0},{16,8},{24,16},{32,24},{40,32},{48,40},{56,48},{64,5... | collective-permute-start | bytes 110600 | tf_op jit(solution)/shard_map/ppermute | solution.py:519
  4.9 6.9 %collective-permute-start = (f32[72,128]{1,0:T(8,128)S(1)}, f32[72,128]{1,0:T(8,128)S(1)}, u32[]{:S(2)}, u32[]{:S(2)}) collective-permute-start(f32[72,128]{1,0:T(8,128)S(1)} %get-tuple-element.25.tail_ref), channel_id=1, source_target_pairs={{0,8},{8,16},{16,24},{24,32},{32,40},{40,48},{48,56},{56,64},{64,7... | collective-permute-start | bytes 110600 | tf_op jit(solution)/shard_map/ppermute | solution.py:518
  12.9 13.4 %all-to-all-start = ((bf16[8,432,128]{2,1,0:T(8,128)(2,1)}), bf16[8,432,128]{2,1,0:T(8,128)(2,1)S(1)}, u32[]{:S(2)}, u32[]{:S(2)}) async-start(bf16[8,432,128]{2,1,0:T(8,128)(2,1)} %get-tuple-element.29), calls=%async_computation | async-start | bytes 1769472 | tf_op jit(solution)/shard_map/all_to_all | solution.py:551
  55.2 56.0 %copy-start = (f32[128,128]{1,0:T(8,128)S(1)}, f32[128,128]{1,0:T(8,128)}, u32[]{:S(2)}) copy-start(f32[128,128]{1,0:T(8,128)} %refs_5_.1) | copy-start | bytes 196612
  55.2 18.2 %all-to-all-start.2 = ((f32[256,1,128]{2,1,0:T(1,128)}), f32[256,1,128]{2,1,0:T(1,128)S(1)}, u32[]{:S(2)}, u32[]{:S(2)}) async-start(f32[256,1,128]{2,1,0:T(1,128)} %modes_0.1), calls=%async_computation.2 | async-start | bytes 262144 | tf_op jit(solution)/shard_map/all_to_all | solution.py:590

commit v6 on v5

--- a/solution.py
+++ b/solution.py
@@ -336,10 +336,10 @@
     return total
 
 
-def basis_kernel(jitter_ref, index_ref, *rest, pieces, far):
+def basis_kernel(jitter_ref, index_ref, *rest, pieces, near):
     count = len(pieces)
     time_ref = rest[count]
-    made = rest[count + 1 : 2 * count + 1] if far else rest[:count]
+    made = rest[:near] + rest[count + 1 : -1]
     blocks, width = jitter_ref.shape[0], made[0].shape[1] // 2
     tiles = width // LANES
     freqs = (index_ref[...] + 1).astype(F32) / (4.0 * time_ref.shape[0])
@@ -351,7 +351,7 @@
 
     def copy(c, b):
         at = pl.ds(pl.multiple_of(LANES * b, LANES), LANES)
-        return pltpu.make_async_copy(made[c].at[at], rest[c].at[at], rest[-1].at[c, b])
+        return pltpu.make_async_copy(made[c].at[at], rest[c].at[at], rest[-1].at[c - near, b])
 
     @pl.loop(0, blocks)
     def _(b):
@@ -372,16 +372,13 @@
                     made[c][at, start : start + LANES] = (1.0 - twice * sine).astype(BF16)
                     made[c][at, start + width : start + width + LANES] = (twice * cosine).astype(BF16)
 
-        if far:
-            for c in range(count):
-                copy(c, b).start()
-
-    if far:
-
-        @pl.loop(0, blocks)
-        def _(b):
-            for c in range(count):
-                copy(c, b).wait()
+        for c in range(near, count):
+            copy(c, b).start()
+
+    @pl.loop(0, blocks)
+    def _(b):
+        for c in range(near, count):
+            copy(c, b).wait()
 
 
 def final_kernel(place_ref, meta_ref, win_ref, arrived_ref, coef_ref, lc_ref, *rest, group):
@@ -532,24 +529,23 @@
 
     index = freq_index.reshape(-1, LANES)
 
-    def basis_of(index, pieces, far):
+    def basis_of(index):
+        size, away = (span, 2 * width), CHUNKS - NEAR
         scratch = [pltpu.VMEM((span, LANES), F32)]
-        if far:
-            scratch += [pltpu.VMEM((span, 2 * width), BF16) for _ in pieces]
-            scratch += [pltpu.SemaphoreType.DMA((len(pieces), ep_count))]
-        place_of = pltpu.HBM if far else shaped
+        scratch += [pltpu.VMEM(size, BF16) for _ in range(away)]
+        scratch += [pltpu.SemaphoreType.DMA((away, ep_count))]
         return call(
-            lambda *refs: basis_kernel(*refs, pieces=pieces, far=far),
-            [place_of((span, 2 * width), BF16) for _ in pieces],
+            lambda *refs: basis_kernel(*refs, pieces=range(CHUNKS), near=NEAR),
+            [shaped(size, BF16)] * NEAR + [pltpu.HBM(size, BF16)] * away,
             (jitter, index),
             scratch=scratch,
-            out_space=[pltpu.HBM if far else pltpu.VMEM] * len(pieces),
+            out_space=[pltpu.VMEM] * NEAR + [pltpu.HBM] * away,
             name="basis",
         )
 
     wide, index = lax.optimization_barrier((wide, index))
     win = lax.all_to_all(wide, "ep", split_axis=0, concat_axis=0, tiled=True)
-    win, *basis = lax.optimization_barrier((win, *basis_of(index, range(NEAR, CHUNKS), True)))
+    win, *basis = lax.optimization_barrier((win, *basis_of(index)))
 
     window_rows = 2 * rows
     products = order * order * 3 // 4
@@ -585,12 +581,7 @@
             (arrived,),
             name=f"modes_{iteration}",
         )
-        if iteration == 0:
-            lines, index = lax.optimization_barrier((lines, index))
         lines = lax.all_to_all(lines, ("ep", "obj"), split_axis=0, concat_axis=0, tiled=True)
-        if iteration == 0:
-            lines, *close = lax.optimization_barrier((lines, *basis_of(index, range(NEAR), False)))
-            basis = close + basis
         args = (places, meta, win, lines.reshape(everyone, LANES), coef_t)
     basis[NEAR:] = [pltpu.with_memory_space_constraint(b, pltpu.HBM) for b in basis[NEAR:]]
     residual, power = call(

time: 117 us -> 117 us (level)
  blocking collectives: 56.4 us -> 73.7 us
  waiting for transfers between devices: 16.8 us -> 5.68 us
  starting transfers between devices: 14.5 us -> 9.2 us
  Pallas kernels: 28.3 us -> 27 us
    all_to_all x1 -> x2, blocking collectives: 17.9 us -> 36.5 us  [per_device(): lax.all_to_all(lines, ('ep', 'obj'), split_axis=0, concat_axis=0, tiled=T...]
    all_to_all x1 -> x0, waiting for transfers between devices: 10.2 us -> none  [per_device(): lax.all_to_all(lines, ('ep', 'obj'), split_axis=0, concat_axis=0, tiled=T...]
    all_to_all x1 -> x0, starting transfers between devices: 5.3 us -> none  [per_device(): lax.all_to_all(lines, ('ep', 'obj'), split_axis=0, concat_axis=0, tiled=T...]
    all_to_all x2, blocking collectives: 38.5 us -> 37.2 us  [per_device(): lax.all_to_all(send.reshape(group, 8, LANES), 'obj', split_axis=0, concat...]
    pallas_call x9 -> x8, Pallas kernels: 28.3 us -> 27 us  [call(): pl.pallas_call(kernel, out_shape=out_shape, in_specs=specs, out_specs=out...]
  transfers between devices with their start and end apart: 4 -> 3, of which waited for: 4 -> 2; matrix products, arithmetic and copies ran while one was open for 0% -> 0% of each run, Pallas kernels for 9% -> 9%
where the time goes in v6:
time: 117 us
  blocking collectives  73.7 us (63%)
  Pallas kernels  27 us (23%)
  starting transfers between devices  9.2 us (8%)
  waiting for transfers between devices  5.68 us (5%)
    all_to_all x2, blocking collectives, per_device(): lax.all_to_all(send.reshape(group, 8, LANES), 'obj', split_axis=0, concat...  37.2 us
    all_to_all x2, blocking collectives, per_device(): lax.all_to_all(lines, ('ep', 'obj'), split_axis=0, concat_axis=0, tiled=T...  36.5 us
    pallas_call x8, Pallas kernels, call(): pl.pallas_call(kernel, out_shape=out_shape, in_specs=specs, out_specs=out...  27 us
    all_to_all x1, starting transfers between devices, per_device(): win = lax.all_to_all(wide, 'ep', split_axis=0, concat_axis=0, tiled=True)  4.66 us
    ppermute x1, waiting for transfers between devices, per_device(): left = lax.ppermute(tail, 'obj', ring)  4.12 us
    ppermute x1, starting transfers between devices, per_device(): right = lax.ppermute(head, 'obj', back)  3.32 us
  transfers between devices with their start and end apart: 3, of which 2 were waited for; matrix products, arithmetic and copies ran while one was open for 0% of the time, Pallas kernels for 9%

profile of v6, /device:TPU:1, one launch (start us, length us, event | category | flops | bytes accessed | tf_op | source)
XLA Modules:
  0.0 116.5 jit_solution(16304740893716825207)
XLA Ops:
  0.6 0.0 copy-start.1
  0.6 0.0 copy-start.2
  0.7 0.9 prep.1
  1.6 3.3 %collective-permute-start.1 = (f32[72,128]{1,0:T(8,128)S(1)}, f32[72,128]{1,0:T(8,128)S(1)}, u32[]{:S(2)}, u32[]{:S(2)}) collective-permute-start(f32[72,128]{1,0:T(8,128)S(1)} %get-tuple-element.24), channel_id=1, source_target_pairs={{0,248},{8,0},{16,8},{24,16},{32,24},{40,32},{48,40},{56,48},{64,5... | collective-permute-start | bytes 110600 | tf_op jit(solution)/shard_map/ppermute | solution.py:516
  4.9 1.2 %collective-permute-start = (f32[72,128]{1,0:T(8,128)S(1)}, f32[72,128]{1,0:T(8,128)S(1)}, u32[]{:S(2)}, u32[]{:S(2)}) collective-permute-start(f32[72,128]{1,0:T(8,128)S(1)} %get-tuple-element.23.tail_ref), channel_id=1, source_target_pairs={{0,8},{8,16},{16,24},{24,32},{32,40},{40,48},{48,56},{56,64},{64,7... | collective-permute-start | bytes 110600 | tf_op jit(solution)/shard_map/ppermute | solution.py:515
  6.2 1.6 %collective-permute-done.1.right_ref = f32[72,128]{1,0:T(8,128)S(1)} collective-permute-done((f32[72,128]{1,0:T(8,128)S(1)}, f32[72,128]{1,0:T(8,128)S(1)}, u32[]{:S(2)}, u32[]{:S(2)}) %collective-permute-start.1) | collective-permute-done | bytes 36896 | tf_op jit(solution)/shard_map/ppermute | solution.py:516
  7.7 4.1 %collective-permute-done.left_ref = f32[72,128]{1,0:T(8,128)S(1)} collective-permute-done((f32[72,128]{1,0:T(8,128)S(1)}, f32[72,128]{1,0:T(8,128)S(1)}, u32[]{:S(2)}, u32[]{:S(2)}) %collective-permute-start) | collective-permute-done | bytes 36896 | tf_op jit(solution)/shard_map/ppermute | solution.py:515
  11.8 1.0 widen.1
  12.9 4.7 %all-to-all-start = ((bf16[8,432,128]{2,1,0:T(8,128)(2,1)}), bf16[8,432,128]{2,1,0:T(8,128)(2,1)S(1)}, u32[]{:S(2)}, u32[]{:S(2)}) async-start(bf16[8,432,128]{2,1,0:T(8,128)(2,1)} %get-tuple-element.27), calls=%async_computation | async-start | bytes 1769472 | tf_op jit(solution)/shard_map/all_to_all | solution.py:547
  17.5 0.0 copy-start
  17.5 0.0 copy-done.1
  17.5 0.0 copy-done.2
  17.6 9.9 %basis.1 = (bf16[1024,1024]{1,0:T(8,128)(2,1)S(1)}, bf16[1024,1024]{1,0:T(8,128)(2,1)}, bf16[1024,1024]{1,0:T(8,128)(2,1)}, bf16[1024,1024]{1,0:T(8,128)(2,1)}) custom-call(f32[8,128]{1,0:T(8,128)S(1)} %bitcast.15, s32[16,128]{1,0:T(8,128)S(1)} %bitcast.14), custom_call_target="tpu_custom_call" | custom-call | tf_op jit(solution)/shard_map/basis/pallas_call | solution.py:481
  27.5 0.0 all-to-all-done.refs_2_
  27.5 4.0 %objects_0.1 = (f32[16,256]{1,0:T(8,128)S(1)}, f32[256,128]{1,0:T(8,128)S(1)}) custom-call(s32[1]{0:T(128)} %bitcast.refs_0_, f32[8,256]{1,0:T(8,128)S(1)} %get-tuple-element.25.refs_1_, bf16[8,432,128]{2,1,0:T(8,128)(2,1)S(1)} %all-to-all-done.refs_2_), custom_call_target="tpu_custom_call" | custom-call | tf_op jit(solution)/shard_map/objects_0/pallas_call | solution.py:481
  31.5 22.4 %all_to_all.25.a = f32[32,8,128]{2,1,0:T(8,128)S(1)} all-to-all(f32[32,8,128]{2,1,0:T(8,128)S(1)} %bitcast.13), channel_id=1, replica_groups=mesh['obj'=32,'ep'=8] {'obj'}, dimensions={0} | all-to-all | bytes 262144 | tf_op jit(solution)/shard_map/all_to_all | solution.py:575
  53.9 0.6 modes_0.1
  54.5 18.4 %all_to_all.26 = f32[256,1,128]{2,1,0:T(1,128)S(1)} all-to-all(f32[256,1,128]{2,1,0:T(1,128)S(1)} %modes_0.1), channel_id=1, replica_groups=mesh['obj'=32,'ep'=8] {'ep','obj'}, dimensions={0} | all-to-all | bytes 262144 | tf_op jit(solution)/shard_map/all_to_all | solution.py:584
  73.0 4.4 %objects_1.1 = (f32[16,256]{1,0:T(8,128)S(1)}, f32[256,128]{1,0:T(8,128)S(1)}) custom-call(s32[1]{0:T(128)} %bitcast.refs_0_, f32[8,256]{1,0:T(8,128)S(1)} %get-tuple-element.25.refs_1_, bf16[8,432,128]{2,1,0:T(8,128)(2,1)S(1)} %all-to-all-done.refs_2_, f32[256,128]{1,0:T(8,128)S(1)} %bitcast.11, f32[16,256]{1,0:T(8,128)S(1)} %get-tuple-element.35.refs_4_), custom_call_target="tpu_custom_call" | custom-call | tf_op jit(solution)/shard_map/objects_1/pallas_call | solution.py:481
  77.3 14.8 %all_to_all.27.a = f32[32,8,128]{2,1,0:T(8,128)S(1)} all-to-all(f32[32,8,128]{2,1,0:T(8,128)S(1)} %bitcast.12), channel_id=1, replica_groups=mesh['obj'=32,'ep'=8] {'obj'}, dimensions={0} | all-to-all | bytes 262144 | tf_op jit(solution)/shard_map/all_to_all | solution.py:575
  92.2 0.6 modes_1.1
  92.8 18.1 %all_to_all.28 = f32[256,1,128]{2,1,0:T(1,128)S(1)} all-to-all(f32[256,1,128]{2,1,0:T(1,128)S(1)} %modes_1.1), channel_id=1, replica_groups=mesh['obj'=32,'ep'=8] {'ep','obj'}, dimensions={0} | all-to-all | bytes 262144 | tf_op jit(solution)/shard_map/all_to_all | solution.py:584
  110.9 0.0 copy-done
  110.9 5.5 %spectrum.1 = (f32[128,128]{1,0:T(8,128)}, f32[16,2048]{1,0:T(8,128)}) custom-call(s32[1]{0:T(128)} %bitcast.refs_0_, f32[8,256]{1,0:T(8,128)S(1)} %get-tuple-element.25.refs_1_, bf16[8,432,128]{2,1,0:T(8,128)(2,1)S(1)} %all-to-all-done.refs_2_, f32[256,128]{1,0:T(8,128)S(1)} %bitcast.10, f32[16,256]{1,0:T(8,128)S(1)} %get-tuple-element.37.refs_4_, ...), custom_call_target="tpu_custom_call" | custom-call | tf_op jit(solution)/shard_map/spectrum/pallas_call | solution.py:481
Async XLA Ops:
  0.6 16.9 %copy-start.1 = (s32[2048]{0:T(1024)S(1)}, s32[2048]{0:T(1024)}, u32[]{:S(2)}) copy-start(s32[2048]{0:T(1024)} %param.13) | copy-start | bytes 24580
  0.6 16.9 %copy-start.2 = (f32[1024]{0:T(1024)S(1)}, f32[1024]{0:T(1024)}, u32[]{:S(2)}) copy-start(f32[1024]{0:T(1024)} %param.12) | copy-start | bytes 12292
  1.6 6.1 %collective-permute-start.1 = (f32[72,128]{1,0:T(8,128)S(1)}, f32[72,128]{1,0:T(8,128)S(1)}, u32[]{:S(2)}, u32[]{:S(2)}) collective-permute-start(f32[72,128]{1,0:T(8,128)S(1)} %get-tuple-element.24), channel_id=1, source_target_pairs={{0,248},{8,0},{16,8},{24,16},{32,24},{40,32},{48,40},{56,48},{64,5... | collective-permute-start | bytes 110600 | tf_op jit(solution)/shard_map/ppermute | solution.py:516
  4.9 6.9 %collective-permute-start = (f32[72,128]{1,0:T(8,128)S(1)}, f32[72,128]{1,0:T(8,128)S(1)}, u32[]{:S(2)}, u32[]{:S(2)}) collective-permute-start(f32[72,128]{1,0:T(8,128)S(1)} %get-tuple-element.23.tail_ref), channel_id=1, source_target_pairs={{0,8},{8,16},{16,24},{24,32},{32,40},{40,48},{48,56},{56,64},{64,7... | collective-permute-start | bytes 110600 | tf_op jit(solution)/shard_map/ppermute | solution.py:515
  12.9 14.6 %all-to-all-start = ((bf16[8,432,128]{2,1,0:T(8,128)(2,1)}), bf16[8,432,128]{2,1,0:T(8,128)(2,1)S(1)}, u32[]{:S(2)}, u32[]{:S(2)}) async-start(bf16[8,432,128]{2,1,0:T(8,128)(2,1)} %get-tuple-element.27), calls=%async_computation | async-start | bytes 1769472 | tf_op jit(solution)/shard_map/all_to_all | solution.py:547
  17.5 93.4 %copy-start = (f32[128,128]{1,0:T(8,128)S(1)}, f32[128,128]{1,0:T(8,128)}, u32[]{:S(2)}) copy-start(f32[128,128]{1,0:T(8,128)} %refs_5_.1) | copy-start | bytes 196612

commit v7 on v6

--- a/solution.py
+++ b/solution.py
@@ -322,7 +322,7 @@
     grid = (np.cos(np.pi * (np.arange(400) + 0.5) / 400) + 1) / 2
     u = np.sqrt(grid) / 2
     sine = np.polynomial.polynomial.polyfit(grid, np.sin(np.pi * u) / u, 4)
-    cosine = np.polynomial.polynomial.polyfit(grid, np.cos(np.pi * u), 5)
+    cosine = np.polynomial.polynomial.polyfit(grid, np.cos(np.pi * u), 4)
     return [float(c) * 4.0**k for k, c in enumerate(sine)], [float(c) * 4.0**k for k, c in enumerate(cosine)]
 
 
@@ -347,7 +347,7 @@
     index = lax.broadcasted_iota(jnp.int32, (LANES, LANES), 0)
     for b in range(blocks):
         time_ref[LANES * b : LANES * (b + 1)] = (index + LANES * b).astype(F32) + jitter[:, b : b + 1]
-    step = 32
+    step = 64
 
     def copy(c, b):
         at = pl.ds(pl.multiple_of(LANES * b, LANES), LANES)

time: 117 us -> 116 us (level)
  transfers between devices with their start and end apart: 3 -> 3, of which waited for: 2 -> 2; matrix products, arithmetic and copies ran while one was open for 0% -> 0% of each run, Pallas kernels for 9% -> 8%
where the time goes in v7:
time: 116 us
  blocking collectives  73.9 us (64%)
  Pallas kernels  26.2 us (23%)
  starting transfers between devices  9.2 us (8%)
  waiting for transfers between devices  5.68 us (5%)
    all_to_all x2, blocking collectives, per_device(): lax.all_to_all(send.reshape(group, 8, LANES), 'obj', split_axis=0, concat...  38 us
    all_to_all x2, blocking collectives, per_device(): lax.all_to_all(lines, ('ep', 'obj'), split_axis=0, concat_axis=0, tiled=T...  35.8 us
    pallas_call x8, Pallas kernels, call(): pl.pallas_call(kernel, out_shape=out_shape, in_specs=specs, out_specs=out...  26.2 us
    all_to_all x1, starting transfers between devices, per_device(): win = lax.all_to_all(wide, 'ep', split_axis=0, concat_axis=0, tiled=True)  4.66 us
    ppermute x1, waiting for transfers between devices, per_device(): left = lax.ppermute(tail, 'obj', ring)  4.12 us
    ppermute x1, starting transfers between devices, per_device(): right = lax.ppermute(head, 'obj', back)  3.32 us
  transfers between devices with their start and end apart: 3, of which 2 were waited for; matrix products, arithmetic and copies ran while one was open for 0% of the time, Pallas kernels for 8%

profile of v7, /device:TPU:1, one launch (start us, length us, event | category | flops | bytes accessed | tf_op | source)
XLA Modules:
  0.0 115.9 jit_solution(9583504263495191069)
XLA Ops:
  0.6 0.0 copy-start.1
  0.6 0.0 copy-start.2
  0.7 0.9 prep.1
  1.6 3.3 %collective-permute-start.1 = (f32[72,128]{1,0:T(8,128)S(1)}, f32[72,128]{1,0:T(8,128)S(1)}, u32[]{:S(2)}, u32[]{:S(2)}) collective-permute-start(f32[72,128]{1,0:T(8,128)S(1)} %get-tuple-element.24), channel_id=1, source_target_pairs={{0,248},{8,0},{16,8},{24,16},{32,24},{40,32},{48,40},{56,48},{64,5... | collective-permute-start | bytes 110600 | tf_op jit(solution)/shard_map/ppermute | solution.py:516
  4.9 1.2 %collective-permute-start = (f32[72,128]{1,0:T(8,128)S(1)}, f32[72,128]{1,0:T(8,128)S(1)}, u32[]{:S(2)}, u32[]{:S(2)}) collective-permute-start(f32[72,128]{1,0:T(8,128)S(1)} %get-tuple-element.23.tail_ref), channel_id=1, source_target_pairs={{0,8},{8,16},{16,24},{24,32},{32,40},{40,48},{48,56},{56,64},{64,7... | collective-permute-start | bytes 110600 | tf_op jit(solution)/shard_map/ppermute | solution.py:515
  6.2 1.6 %collective-permute-done.1.right_ref = f32[72,128]{1,0:T(8,128)S(1)} collective-permute-done((f32[72,128]{1,0:T(8,128)S(1)}, f32[72,128]{1,0:T(8,128)S(1)}, u32[]{:S(2)}, u32[]{:S(2)}) %collective-permute-start.1) | collective-permute-done | bytes 36896 | tf_op jit(solution)/shard_map/ppermute | solution.py:516
  7.7 4.1 %collective-permute-done.left_ref = f32[72,128]{1,0:T(8,128)S(1)} collective-permute-done((f32[72,128]{1,0:T(8,128)S(1)}, f32[72,128]{1,0:T(8,128)S(1)}, u32[]{:S(2)}, u32[]{:S(2)}) %collective-permute-start) | collective-permute-done | bytes 36896 | tf_op jit(solution)/shard_map/ppermute | solution.py:515
  11.8 1.0 widen.1
  12.9 4.7 %all-to-all-start = ((bf16[8,432,128]{2,1,0:T(8,128)(2,1)}), bf16[8,432,128]{2,1,0:T(8,128)(2,1)S(1)}, u32[]{:S(2)}, u32[]{:S(2)}) async-start(bf16[8,432,128]{2,1,0:T(8,128)(2,1)} %get-tuple-element.27), calls=%async_computation | async-start | bytes 1769472 | tf_op jit(solution)/shard_map/all_to_all | solution.py:547
  17.5 0.0 copy-start
  17.5 0.0 copy-done.1
  17.5 0.0 copy-done.2
  17.6 9.2 %basis.1 = (bf16[1024,1024]{1,0:T(8,128)(2,1)S(1)}, bf16[1024,1024]{1,0:T(8,128)(2,1)}, bf16[1024,1024]{1,0:T(8,128)(2,1)}, bf16[1024,1024]{1,0:T(8,128)(2,1)}) custom-call(f32[8,128]{1,0:T(8,128)S(1)} %bitcast.15, s32[16,128]{1,0:T(8,128)S(1)} %bitcast.14), custom_call_target="tpu_custom_call" | custom-call | tf_op jit(solution)/shard_map/basis/pallas_call | solution.py:481
  26.7 0.0 all-to-all-done.refs_2_
  26.7 4.0 %objects_0.1 = (f32[16,256]{1,0:T(8,128)S(1)}, f32[256,128]{1,0:T(8,128)S(1)}) custom-call(s32[1]{0:T(128)} %bitcast.refs_0_, f32[8,256]{1,0:T(8,128)S(1)} %get-tuple-element.25.refs_1_, bf16[8,432,128]{2,1,0:T(8,128)(2,1)S(1)} %all-to-all-done.refs_2_), custom_call_target="tpu_custom_call" | custom-call | tf_op jit(solution)/shard_map/objects_0/pallas_call | solution.py:481
  30.7 23.2 %all_to_all.25.a = f32[32,8,128]{2,1,0:T(8,128)S(1)} all-to-all(f32[32,8,128]{2,1,0:T(8,128)S(1)} %bitcast.13), channel_id=1, replica_groups=mesh['obj'=32,'ep'=8] {'obj'}, dimensions={0} | all-to-all | bytes 262144 | tf_op jit(solution)/shard_map/all_to_all | solution.py:575
  53.9 0.6 modes_0.1
  54.5 18.0 %all_to_all.26 = f32[256,1,128]{2,1,0:T(1,128)S(1)} all-to-all(f32[256,1,128]{2,1,0:T(1,128)S(1)} %modes_0.1), channel_id=1, replica_groups=mesh['obj'=32,'ep'=8] {'ep','obj'}, dimensions={0} | all-to-all | bytes 262144 | tf_op jit(solution)/shard_map/all_to_all | solution.py:584
  72.5 4.4 %objects_1.1 = (f32[16,256]{1,0:T(8,128)S(1)}, f32[256,128]{1,0:T(8,128)S(1)}) custom-call(s32[1]{0:T(128)} %bitcast.refs_0_, f32[8,256]{1,0:T(8,128)S(1)} %get-tuple-element.25.refs_1_, bf16[8,432,128]{2,1,0:T(8,128)(2,1)S(1)} %all-to-all-done.refs_2_, f32[256,128]{1,0:T(8,128)S(1)} %bitcast.11, f32[16,256]{1,0:T(8,128)S(1)} %get-tuple-element.35.refs_4_), custom_call_target="tpu_custom_call" | custom-call | tf_op jit(solution)/shard_map/objects_1/pallas_call | solution.py:481
  76.9 14.8 %all_to_all.27.a = f32[32,8,128]{2,1,0:T(8,128)S(1)} all-to-all(f32[32,8,128]{2,1,0:T(8,128)S(1)} %bitcast.12), channel_id=1, replica_groups=mesh['obj'=32,'ep'=8] {'obj'}, dimensions={0} | all-to-all | bytes 262144 | tf_op jit(solution)/shard_map/all_to_all | solution.py:575
  91.7 0.6 modes_1.1
  92.4 17.9 %all_to_all.28 = f32[256,1,128]{2,1,0:T(1,128)S(1)} all-to-all(f32[256,1,128]{2,1,0:T(1,128)S(1)} %modes_1.1), channel_id=1, replica_groups=mesh['obj'=32,'ep'=8] {'ep','obj'}, dimensions={0} | all-to-all | bytes 262144 | tf_op jit(solution)/shard_map/all_to_all | solution.py:584
  110.2 0.0 copy-done
  110.2 5.5 %spectrum.1 = (f32[128,128]{1,0:T(8,128)}, f32[16,2048]{1,0:T(8,128)}) custom-call(s32[1]{0:T(128)} %bitcast.refs_0_, f32[8,256]{1,0:T(8,128)S(1)} %get-tuple-element.25.refs_1_, bf16[8,432,128]{2,1,0:T(8,128)(2,1)S(1)} %all-to-all-done.refs_2_, f32[256,128]{1,0:T(8,128)S(1)} %bitcast.10, f32[16,256]{1,0:T(8,128)S(1)} %get-tuple-element.37.refs_4_, ...), custom_call_target="tpu_custom_call" | custom-call | tf_op jit(solution)/shard_map/spectrum/pallas_call | solution.py:481
Async XLA Ops:
  0.6 16.9 %copy-start.1 = (s32[2048]{0:T(1024)S(1)}, s32[2048]{0:T(1024)}, u32[]{:S(2)}) copy-start(s32[2048]{0:T(1024)} %param.13) | copy-start | bytes 24580
  0.6 16.9 %copy-start.2 = (f32[1024]{0:T(1024)S(1)}, f32[1024]{0:T(1024)}, u32[]{:S(2)}) copy-start(f32[1024]{0:T(1024)} %param.12) | copy-start | bytes 12292
  1.6 6.1 %collective-permute-start.1 = (f32[72,128]{1,0:T(8,128)S(1)}, f32[72,128]{1,0:T(8,128)S(1)}, u32[]{:S(2)}, u32[]{:S(2)}) collective-permute-start(f32[72,128]{1,0:T(8,128)S(1)} %get-tuple-element.24), channel_id=1, source_target_pairs={{0,248},{8,0},{16,8},{24,16},{32,24},{40,32},{48,40},{56,48},{64,5... | collective-permute-start | bytes 110600 | tf_op jit(solution)/shard_map/ppermute | solution.py:516
  4.9 6.9 %collective-permute-start = (f32[72,128]{1,0:T(8,128)S(1)}, f32[72,128]{1,0:T(8,128)S(1)}, u32[]{:S(2)}, u32[]{:S(2)}) collective-permute-start(f32[72,128]{1,0:T(8,128)S(1)} %get-tuple-element.23.tail_ref), channel_id=1, source_target_pairs={{0,8},{8,16},{16,24},{24,32},{32,40},{40,48},{48,56},{56,64},{64,7... | collective-permute-start | bytes 110600 | tf_op jit(solution)/shard_map/ppermute | solution.py:515
  12.9 13.9 %all-to-all-start = ((bf16[8,432,128]{2,1,0:T(8,128)(2,1)}), bf16[8,432,128]{2,1,0:T(8,128)(2,1)S(1)}, u32[]{:S(2)}, u32[]{:S(2)}) async-start(bf16[8,432,128]{2,1,0:T(8,128)(2,1)} %get-tuple-element.27), calls=%async_computation | async-start | bytes 1769472 | tf_op jit(solution)/shard_map/all_to_all | solution.py:547
  17.5 92.7 %copy-start = (f32[128,128]{1,0:T(8,128)S(1)}, f32[128,128]{1,0:T(8,128)}, u32[]{:S(2)}) copy-start(f32[128,128]{1,0:T(8,128)} %refs_5_.1) | copy-start | bytes 196612
